TPU v7x, 32 devices: a whole 2x2x4 slice. The times are simulated.
32 devices in a mesh: src: 4 (over z), snk: 4 (over x, core), sub: 2 (over y).
Axes of the slice: x: 2, y: 2, z: 4, core: 2. Of those that a mesh axis runs over, the one named last changes fastest.
Arguments:
- peram: bfloat16 [4, 4, 2, 512, 512], P('src', 'snk', None, 'sub'), may hold values from -6 to 6
- elemental: bfloat16 [2, 512, 512], replicated, may hold values from -0.0078125 to 0.0078125
- spin_signs: int32 [4], replicated, may hold values from 0 to 1
- insertions: int32 [4], replicated, may hold values from 0 to 3
Outputs:
- peram_full: bfloat16 [4, 4, 2, 512, 512], P('src', 'snk', None, 'sub')
- contraction: float32 [4, 4, 2, 512, 512], P('src', 'snk', None, 'sub')
Inputs may be any that keep to these rules, and one draw needn't show every extreme that they name: `spin_signs`: one entry for each of the four spin blocks. `insertions`: insertion times may repeat.
All inputs are finite; a program needn't handle non-finite values.
Results may differ from a plain program's by a relative error of at most 0.0029.
Values may be sent and summed in bfloat16 or wider, within the bound.
No kernel may reach another device: no remote copies, remote signals or barrier semaphores. Data moves between devices by JAX's collectives and lax.ppermute only.
A program may use at most 64 MiB of HBM per device.

v0:
```python
import jax
import jax.numpy as jnp
from jax import lax
from jax.experimental import pallas as pl
from jax.experimental.pallas import tpu as pltpu
from jax.sharding import PartitionSpec as P

AXES = ("src", "snk", "sub")


def complex_product(first, second):
    real_part = jnp.dot(first[0], second[0], preferred_element_type=jnp.float32) - jnp.dot(
        first[1], second[1], preferred_element_type=jnp.float32
    )
    imag_part = jnp.dot(first[0], second[1], preferred_element_type=jnp.float32) + jnp.dot(
        first[1], second[0], preferred_element_type=jnp.float32
    )
    return jnp.stack([real_part, imag_part], axis=0)


def broadcast(block, axis, owner):
    block = jnp.where(lax.axis_index(axis) == owner, block, jnp.zeros_like(block))
    return lax.psum(block, axis)


def swap(value, axis, mask):
    size = lax.axis_size(axis)
    return lax.ppermute(value, axis, [(i, i ^ mask) for i in range(size)])


def scalars(*values):
    return jnp.stack([jnp.asarray(value, jnp.int32) for value in values])


SMEM = pl.BlockSpec(memory_space=pltpu.SMEM)
VMEM = pl.BlockSpec(memory_space=pltpu.VMEM)


def local_call(kernel, out_shape, operands, tables=2, scratch=(), flops=0):
    outs = out_shape if isinstance(out_shape, (list, tuple)) else [out_shape]
    moved = sum(x.size * x.dtype.itemsize for x in (*operands, *outs))
    return pl.pallas_call(
        kernel,
        out_shape=out_shape,
        in_specs=[SMEM] * tables + [VMEM] * (len(operands) - tables),
        out_specs=jax.tree.map(lambda _: VMEM, out_shape),
        scratch_shapes=scratch,
        cost_estimate=pl.CostEstimate(flops=flops, bytes_accessed=moved, transcendentals=0),
    )(*operands)


def mirror_kernel(place_ref, sign_ref, own_ref, *out_refs):
    half = place_ref[0]
    rows, width = own_ref.shape[1:]
    group = width // sign_ref.shape[0]
    n_sub = len(out_refs)
    for shift in range(n_sub):
        target = lax.rem(half + shift, n_sub)
        start = target * rows
        for i in range(0, rows, group):
            for j in range(0, rows, group):
                row = sign_ref[(target * rows + i) // group]
                column = sign_ref[(half * rows + j) // group]
                flip = ((1 - 2 * row) * (1 - 2 * column)).astype(jnp.float32)
                for part, scale in ((0, flip), (1, -flip)):
                    block = own_ref[part, j : j + group, pl.ds(pl.multiple_of(start + i, 128), group)]
                    block = scale * block.astype(jnp.float32).T
                    out_refs[shift][part, i : i + group, j : j + group] = block.astype(jnp.bfloat16)


def mirror_pieces(own, spin_signs):
    n_sub = lax.axis_size("sub")
    rows = own.shape[1]
    piece = jax.ShapeDtypeStruct((2, rows, rows), own.dtype)
    return local_call(mirror_kernel, [piece] * n_sub, (scalars(lax.axis_index("sub")), spin_signs, own))


def place(a, b, h):
    return (a * lax.axis_size("snk") + b) * lax.axis_size("sub") + h


def send(value, pairs):
    return lax.ppermute(value, AXES, pairs)


def mirror_pairs(shift, chosen):
    n_src, n_snk, n_sub = (lax.axis_size(axis) for axis in AXES)
    return [
        (place(b, a, h), place(a, b, (h + shift) % n_sub))
        for b in range(min(n_src, n_snk))
        for a in range(b)
        if chosen(b, a)
        for h in range(n_sub)
    ]


def assemble(own, arrived):
    n_sub = lax.axis_size("sub")
    half = lax.axis_index("sub")
    columns = []
    for part in range(n_sub):
        column = arrived[0]
        for shift in range(1, n_sub):
            column = jnp.where(lax.rem(part + shift, n_sub) == half, arrived[shift], column)
        columns.append(column)
    upper = jnp.concatenate(columns, axis=2)
    return jnp.where(lax.axis_index("src") >= lax.axis_index("snk"), own, upper)


def fill_upper(own, spin_signs):
    pieces = mirror_pieces(own, spin_signs)
    shifts = range(lax.axis_size("sub"))
    return assemble(own, [send(pieces[k], mirror_pairs(k, lambda b, a: True)) for k in shifts])


def by_broadcast(full_half, payload, insertions):
    n_sub = lax.axis_size("sub")
    total = jnp.zeros(full_half.shape, jnp.float32)
    for index in range(insertions.shape[0]):
        moment = insertions[index]
        received = broadcast(payload, "snk", moment)
        halves = [broadcast(full_half, ("src", "sub"), moment * n_sub + part) for part in range(n_sub)]
        total = total + complex_product(received, jnp.concatenate(halves, axis=1))
    return total


def left_panel(keep, give):
    n_snk, n_sub = lax.axis_size("snk"), lax.axis_size("sub")
    across = [(b * n_sub + h, (b ^ 2) * n_sub + (h ^ 1)) for b in range(n_snk) for h in range(n_sub)]
    give_y = swap(give, "sub", 1)
    keep_x = swap(keep, "snk", 2)
    give_x = lax.ppermute(give, ("snk", "sub"), across)
    near = jnp.concatenate([keep, give_y], axis=1)
    far = jnp.concatenate([keep_x, give_x], axis=1)
    near_other = swap(near, "snk", 1)
    far_other = swap(far, "snk", 1)
    return near, near_other, far, far_other


def dot(first, second):
    return jnp.dot(first, second, preferred_element_type=jnp.float32)


def home_kernel(table, _, own, direct0, direct1, hand0, hand1, elem, home, home0, home1, keep, give):
    lower, relayed, half = table[0], table[1], table[2]
    rows = own.shape[1]

    @pl.when(lower == 1)
    def _():
        home[...] = own[...]

    def put(first, second):
        home[:, :, pl.ds(pl.multiple_of(half * rows, 128), rows)] = first[...]
        home[:, :, pl.ds(pl.multiple_of((1 - half) * rows, 128), rows)] = second[...]

    @pl.when((lower == 0) & (relayed == 0))
    def _():
        put(direct0, direct1)

    @pl.when((lower == 0) & (relayed == 1))
    def _():
        put(hand0, hand1)

    home0[...] = home[:, :, :rows]
    home1[...] = home[:, :, rows:]
    for start, out in ((half, keep), (1 - half, give)):
        columns = pl.ds(pl.multiple_of(start * rows, 128), rows)
        out[0] = (dot(home[0], elem[0, :, columns]) - dot(home[1], elem[1, :, columns])).astype(jnp.bfloat16)
        out[1] = (dot(home[0], elem[1, :, columns]) + dot(home[1], elem[0, :, columns])).astype(jnp.bfloat16)


def pick_kernel(table, _, early, late0, late1, out0, out1):
    rows = out0.shape[2]

    @pl.when(table[0] == 1)
    def _():
        out0[...] = early[:, :, :rows]
        out1[...] = early[:, :, rows:]

    @pl.when(table[0] == 0)
    def _():
        out0[...] = late0[...]
        out1[...] = late1[...]


def times(ins, moment):
    count = jnp.int32(0)
    for index in range(ins.shape[0]):
        count = count + (ins[index] == moment).astype(jnp.int32)
    return count.astype(jnp.float32)


def product(count, left, right):
    real = count * (dot(left[0], right[0]) - dot(left[1], right[1]))
    imag = count * (dot(left[0], right[1]) + dot(left[1], right[0]))
    return real, imag


def early_kernel(table, ins, left0, left1, left2, left3, home0, home1, near_early, near, far0, far1, acc, last, chosen, beside):
    a, b, near_ready = table[0], table[1], table[2]
    rows = home0.shape[2]

    def choose(k, out):
        for index, left in enumerate((left0, left1, left2, left3)):

            @pl.when(k == index)
            def _():
                out[...] = left[...]

    @pl.when(near_ready == 1)
    def _():
        beside[...] = near_early[...]

    @pl.when(near_ready == 0)
    def _():
        beside[...] = near[...]

    for step in (0, 1, 3):
        choose(a ^ step ^ b, chosen)
        count = times(ins, a ^ step)
        for part in range(2):
            columns = slice(part * rows, (part + 1) * rows)
            right = {0: (home0, home1)[part], 1: beside.at[:, :, columns], 3: (far0, far1)[part]}[step]
            real, imag = product(count, chosen, right)
            if step:
                real = acc[0, :, columns] + real
                imag = acc[1, :, columns] + imag
            acc[0, :, columns] = real
            acc[1, :, columns] = imag
    choose(a ^ 2 ^ b, last)


def late_kernel(part, table, ins, acc, last, block, mine, give):
    rows = mine.shape[1]
    columns = slice(part * rows, (part + 1) * rows)
    real, imag = product(times(ins, table[0] ^ 2), last, block)
    for index, value in ((0, real), (1, imag)):
        total = acc[index, :, columns] + value
        mine[index] = total[:rows]
        give[index] = total[rows:].astype(jnp.bfloat16)


def finish_kernel(table, _, mine0, given0, mine1, given1, out):
    rows = mine0.shape[1]
    out[:, :, :rows] = mine0[...] + given0[...].astype(jnp.float32)
    out[:, :, rows:] = mine1[...] + given1[...].astype(jnp.float32)


def along_z(mask, chosen):
    return [
        (place(a, b, h), place(a ^ mask, b, h))
        for a in range(lax.axis_size("src"))
        for b in range(lax.axis_size("snk"))
        if chosen(a, b)
        for h in range(lax.axis_size("sub"))
    ]


def by_doubling(own, elemental, spin_signs, insertions):
    a = lax.axis_index("src")
    b = lax.axis_index("snk")
    rows, width = own.shape[1:]
    parts = range(width // rows)
    shifts = range(lax.axis_size("sub"))

    def relayed(b, a):
        return (b, a) == (3, 1)

    def ready(a, b):
        return a >= b

    def ready_far(a, b):
        return a >= b and (b >= 2 or a < 2)

    pieces = mirror_pieces(own, spin_signs)
    relay = [send(pieces[k], [(place(3, 1, h), place(3, 3, (h + k) % 2)) for h in shifts]) for k in shifts]
    direct = [send(pieces[k], mirror_pairs(k, lambda b, a: not relayed(b, a))) for k in shifts]
    handed = [send(relay[k], [(place(3, 3, h), place(1, 3, h)) for h in shifts]) for k in shifts]
    near_early = send(own, along_z(1, ready))
    far_early = send(own, along_z(3, ready_far))

    piece = jax.ShapeDtypeStruct((2, rows, rows), own.dtype)
    tile = jax.ShapeDtypeStruct(own.shape, own.dtype)
    full_half, home0, home1, keep, give = local_call(
        home_kernel,
        [tile, piece, piece, piece, piece],
        (scalars(a >= b, (a == 1) & (b == 3), lax.axis_index("sub")), spin_signs, own, *direct, *handed, elemental),
        flops=8 * rows * width * width,
    )
    far_late = [send(value, along_z(3, lambda a, b: not ready_far(a, b))) for value in (home0, home1)]
    near = send(full_half, along_z(1, lambda a, b: not ready(a, b)))
    from_far = a ^ 3
    was_ready = (from_far >= b) & ((b >= 2) | (from_far < 2))
    far = local_call(pick_kernel, [piece, piece], (scalars(was_ready), spin_signs, far_early, *far_late))
    late = [swap(far[part], "src", 1) for part in parts]
    left = left_panel(keep, give)
    table = scalars(a, b, (a ^ 1) >= b)
    acc, last = local_call(
        early_kernel,
        [jax.ShapeDtypeStruct((2, 2 * rows, width), jnp.float32), jax.ShapeDtypeStruct((2, 2 * rows, rows), own.dtype)],
        (table, insertions, *left, home0, home1, near_early, near, *far),
        scratch=[pltpu.VMEM((2, 2 * rows, rows), own.dtype), pltpu.VMEM(own.shape, own.dtype)],
        flops=3 * 16 * rows * rows * width,
    )
    ends = []
    for part in parts:
        mine, given = local_call(
            lambda *refs, part=part: late_kernel(part, *refs),
            [jax.ShapeDtypeStruct((2, rows, rows), jnp.float32), piece],
            (table, insertions, acc, last, late[part]),
            flops=16 * rows * rows * rows,
        )
        ends += [mine, swap(given, "sub", 1)]
    total = local_call(finish_kernel, jax.ShapeDtypeStruct(own.shape, jnp.float32), (table, insertions, *ends))
    return full_half, total


def local(peram, elemental, spin_signs, insertions):
    own = peram[0, 0]
    if lax.axis_size("src") == lax.axis_size("snk") == 4 and lax.axis_size("sub") == 2:
        full_half, total = by_doubling(own, elemental, spin_signs, insertions)
    else:
        full_half = fill_upper(own, spin_signs)
        payload = complex_product(full_half, elemental).astype(jnp.bfloat16)
        total = by_broadcast(full_half, payload, insertions)
    return (full_half[None, None], total[None, None])


def solution(mesh):
    return jax.shard_map(
        local,
        mesh=mesh,
        in_specs=(P("src", "snk", None, "sub", None), P(), P(), P()),
        out_specs=(P("src", "snk", None, "sub", None), P("src", "snk", None, "sub", None)),
        check_vma=False,
    )
```

profile of v0, /device:TPU:0, one launch (start us, length us, event | category | flops | bytes accessed | tf_op | source)
XLA Modules:
  0.0 100.3 jit_solution(4199125290612414452)
XLA Ops:
  0.6 0.0 copy-start
  0.6 2.0 %shard_map.59 = (bf16[2,256,256]{2,1,0:T(8,128)(2,1)}, bf16[2,256,256]{2,1,0:T(8,128)(2,1)}) custom-call(s32[1]{0:T(128)} %bitcast.2.place_ref, s32[4]{0:T(128)} %_.4, bf16[2,256,512]{2,1,0:T(8,128)(2,1)} %bitcast.10), custom_call_target="tpu_custom_call" | custom-call | bytes 1048596 | tf_op jit(solution)/shard_map/pallas_call | solution.py:42
  2.7 0.7 collective-permute-start.2
  3.4 0.7 collective-permute-start.4
  4.0 0.7 collective-permute-start
  4.7 0.7 collective-permute-start.1
  5.4 0.7 collective-permute-start.3
  6.1 0.7 collective-permute-start.5
  6.8 0.6 pad_add_fusion.table
  7.5 0.0 copy-start.4
  7.5 0.6 copy-done.2
  8.2 0.1 copy-done.4
  8.3 0.1 copy-done.5
  8.4 0.7 copy-done.6
  9.1 3.4 %shard_map.60 = (bf16[2,256,512]{2,1,0:T(8,128)(2,1)}, bf16[2,256,256]{2,1,0:T(8,128)(2,1)}, bf16[2,256,256]{2,1,0:T(8,128)(2,1)}, bf16[2,256,256]{2,1,0:T(8,128)(2,1)}, bf16[2,256,256]{2,1,0:T(8,128)(2,1)}) custom-call(s32[3]{0:T(128)} %pad_add_fusion.table, s32[4]{0:T(128)} %_.4, bf16[2,256,512]{2,1,0:T(8,128)(2,1)} %bitcast.11, ...), custom_call_target="tpu_custom_call" | custom-call | flops 536870912 | bytes 4194332 | tf_op jit(solution)/shard_map/pallas_call | solution.py:42
  12.4 24.3 %collective-permute-start.8 = (bf16[2,256,256]{2,1,0:T(8,128)(2,1)}, bf16[2,256,256]{2,1,0:T(8,128)(2,1)S(1)}, u32[]{:S(2)}, u32[]{:S(2)}) collective-permute-start(bf16[2,256,256]{2,1,0:T(8,128)(2,1)} %get-tuple-element.20), channel_id=1, source_target_pairs={{0,4},{2,6},{4,0},{6,2},{1,5},{3,7},{5,1},{7,3},{8,12},{10,14},{12... | collective-permute-start | bytes 786440 | tf_op jit(solution)/shard_map/ppermute | solution.py:28
  36.7 1.3 %collective-permute-start.13 = (bf16[2,256,512]{2,1,0:T(8,128)(2,1)S(1)}, bf16[2,256,512]{2,1,0:T(8,128)(2,1)S(1)}, u32[]{:S(2)}, u32[]{:S(2)}) collective-permute-start(bf16[2,256,512]{2,1,0:T(8,128)(2,1)S(1)} %bitcast.12), channel_id=1, source_target_pairs={{0,24},{1,25},{8,16},{9,17},{10,18},{11,19},{20,12},{21,13},{28,4}... | collective-permute-start | bytes 1572872 | tf_op jit(solution)/shard_map/ppermute | solution.py:83
  38.0 0.1 collective-permute-start.9
  38.1 2.0 %collective-permute-start.11 = (bf16[2,256,512]{2,1,0:T(8,128)(2,1)S(1)}, bf16[2,256,512]{2,1,0:T(8,128)(2,1)S(1)}, u32[]{:S(2)}, u32[]{:S(2)}) collective-permute-start(bf16[2,256,512]{2,1,0:T(8,128)(2,1)S(1)} %bitcast.13), channel_id=1, source_target_pairs={{0,8},{1,9},{8,0},{9,1},{10,2},{11,3},{16,24},{17,25},{18,26},{19,... | collective-permute-start | bytes 1572872 | tf_op jit(solution)/shard_map/ppermute | solution.py:83
  40.1 1.6 %collective-permute-start.6 = (bf16[2,256,256]{2,1,0:T(8,128)(2,1)}, bf16[2,256,256]{2,1,0:T(8,128)(2,1)S(1)}, u32[]{:S(2)}, u32[]{:S(2)}) collective-permute-start(bf16[2,256,256]{2,1,0:T(8,128)(2,1)} %get-tuple-element.21), channel_id=1, source_target_pairs={{0,1},{1,0},{2,3},{3,2},{4,5},{5,4},{6,7},{7,6},{8,9},{9,8},{10,11... | collective-permute-start | bytes 786440 | tf_op jit(solution)/shard_map/ppermute | solution.py:28
  41.7 1.0 constant_dynamic-update-slice_fusion.1
  42.7 1.3 %collective-permute-start.14 = (bf16[2,256,256]{2,1,0:T(8,128)(2,1)}, bf16[2,256,256]{2,1,0:T(8,128)(2,1)S(1)}, u32[]{:S(2)}, u32[]{:S(2)}) collective-permute-start(bf16[2,256,256]{2,1,0:T(8,128)(2,1)} %get-tuple-element.22.home0), channel_id=1, source_target_pairs={{2,26},{3,27},{4,28},{5,29},{6,30},{7,31},{12,20},{13,21},{14,22},... | collective-permute-start | bytes 786440 | tf_op jit(solution)/shard_map/ppermute | solution.py:83
  44.0 1.6 %collective-permute-done.9 = bf16[2,256,256]{2,1,0:T(8,128)(2,1)S(1)} collective-permute-done((bf16[2,256,256]{2,1,0:T(8,128)(2,1)}, bf16[2,256,256]{2,1,0:T(8,128)(2,1)S(1)}, u32[]{:S(2)}, u32[]{:S(2)}) %collective-permute-start.9) | collective-permute-done | bytes 262176 | tf_op jit(solution)/shard_map/ppermute | solution.py:132
  45.6 1.5 %collective-permute-start.12 = (bf16[2,256,512]{2,1,0:T(8,128)(2,1)}, bf16[2,256,512]{2,1,0:T(8,128)(2,1)}, u32[]{:S(2)}, u32[]{:S(2)}) collective-permute-start(bf16[2,256,512]{2,1,0:T(8,128)(2,1)} %get-tuple-element.19), channel_id=1, source_target_pairs={{2,10},{3,11},{4,12},{5,13},{6,14},{7,15},{12,4},{13,5},{14,6},{15... | collective-permute-start | bytes 1572872 | tf_op jit(solution)/shard_map/ppermute | solution.py:83
  47.1 1.2 %collective-permute-done.6 = bf16[2,256,256]{2,1,0:T(8,128)(2,1)S(1)} collective-permute-done((bf16[2,256,256]{2,1,0:T(8,128)(2,1)}, bf16[2,256,256]{2,1,0:T(8,128)(2,1)S(1)}, u32[]{:S(2)}, u32[]{:S(2)}) %collective-permute-start.6) | collective-permute-done | bytes 262176 | tf_op jit(solution)/shard_map/ppermute | solution.py:28
  48.4 0.6 collective-permute-start.7
  49.0 8.5 %collective-permute-done.14.late0 = bf16[2,256,256]{2,1,0:T(8,128)(2,1)S(1)} collective-permute-done((bf16[2,256,256]{2,1,0:T(8,128)(2,1)}, bf16[2,256,256]{2,1,0:T(8,128)(2,1)S(1)}, u32[]{:S(2)}, u32[]{:S(2)}) %collective-permute-start.14) | collective-permute-done | bytes 262176 | tf_op jit(solution)/shard_map/ppermute | solution.py:83
  57.5 1.3 %collective-permute-start.15 = (bf16[2,256,256]{2,1,0:T(8,128)(2,1)S(1)}, bf16[2,256,256]{2,1,0:T(8,128)(2,1)S(1)}, u32[]{:S(2)}, u32[]{:S(2)}) collective-permute-start(bf16[2,256,256]{2,1,0:T(8,128)(2,1)S(1)} %copy-done.15), channel_id=1, source_target_pairs={{2,26},{3,27},{4,28},{5,29},{6,30},{7,31},{12,20},{13,21},{14,22},... | collective-permute-start | bytes 786440 | tf_op jit(solution)/shard_map/ppermute | solution.py:83
  58.8 8.8 %collective-permute-done.15.late1 = bf16[2,256,256]{2,1,0:T(8,128)(2,1)S(1)} collective-permute-done((bf16[2,256,256]{2,1,0:T(8,128)(2,1)S(1)}, bf16[2,256,256]{2,1,0:T(8,128)(2,1)S(1)}, u32[]{:S(2)}, u32[]{:S(2)}) %collective-permute-start.15) | collective-permute-done | bytes 262176 | tf_op jit(solution)/shard_map/ppermute | solution.py:83
  67.7 0.7 copy-done.7
  68.4 2.1 %shard_map.61 = (bf16[2,256,256]{2,1,0:T(8,128)(2,1)}, bf16[2,256,256]{2,1,0:T(8,128)(2,1)}) custom-call(s32[1]{0:T(128)} %bitcast.8.table, s32[4]{0:T(128)} %_.4, bf16[2,256,512]{2,1,0:T(8,128)(2,1)} %copy-done.1, bf16[2,256,256]{2,1,0:T(8,128)(2,1)} %copy-done.3, bf16[2,256,256]{2,1,0:T(8,128)(2,1)} %copy-done.7), custom_call_target="tpu_custom_call" | custom-call | bytes 1572884 | tf_op jit(solution)/shard_map/pallas_call | solution.py:42
  70.4 2.4 %collective-permute-start.18 = (bf16[2,256,256]{2,1,0:T(8,128)(2,1)}, bf16[2,256,256]{2,1,0:T(8,128)(2,1)S(1)}, u32[]{:S(2)}, u32[]{:S(2)}) collective-permute-start(bf16[2,256,256]{2,1,0:T(8,128)(2,1)} %get-tuple-element.25.far1), channel_id=1, source_target_pairs={{0,8},{8,0},{16,24},{24,16},{1,9},{9,1},{17,25},{25,17},{2,10},{10... | collective-permute-start | bytes 786440 | tf_op jit(solution)/shard_map/ppermute | solution.py:28
  72.8 0.1 collective-permute-start.16
  72.9 0.6 pad_add_fusion.1.table.refs_0_
  73.5 0.1 copy-done.14
  73.6 6.0 %shard_map.62 = (f32[2,512,512]{2,1,0:T(8,128)}, bf16[2,512,256]{2,1,0:T(8,128)(2,1)}) custom-call(s32[3]{0:T(128)} %pad_add_fusion.1.table.refs_0_, s32[4]{0:T(128)} %_.5, bf16[2,512,256]{2,1,0:T(8,128)(2,1)} %copy-done.12, bf16[2,512,256]{2,1,0:T(8,128)(2,1)} %collective-permute-done.7.left1, bf16[2,512,256]{2,1,0:T(8,128)(2,1)} %copy-done.13, ...), custom_call_target="tpu_custom_call" | custom-call | flops 1610612736 | bytes 6815772 | tf_op jit(solution)/shard_map/pallas_call | solution.py:42
  79.6 0.5 collective-permute-done.18.refs_4_
  80.1 0.7 copy-done.11
  80.8 3.0 %shard_map.64 = (f32[2,256,256]{2,1,0:T(8,128)}, bf16[2,256,256]{2,1,0:T(8,128)(2,1)}) custom-call(s32[3]{0:T(128)} %pad_add_fusion.1.table.refs_0_, s32[4]{0:T(128)} %_.5, f32[2,512,512]{2,1,0:T(8,128)} %get-tuple-element.26.refs_2_, bf16[2,512,256]{2,1,0:T(8,128)(2,1)} %get-tuple-element.27.refs_3_, bf16[2,256,256]{2,1,0:T(8,128)(2,1)} %copy-done.11), custom_call_target="tpu_custom_call" | custom-call | flops 268435456 | bytes 3670044 | tf_op jit(solution)/shard_map/pallas_call | solution.py:42
  83.9 1.0 %collective-permute-start.19 = (bf16[2,256,256]{2,1,0:T(8,128)(2,1)}, bf16[2,256,256]{2,1,0:T(8,128)(2,1)S(1)}, u32[]{:S(2)}, u32[]{:S(2)}) collective-permute-start(bf16[2,256,256]{2,1,0:T(8,128)(2,1)} %get-tuple-element.31), channel_id=1, source_target_pairs={{0,1},{1,0},{2,3},{3,2},{4,5},{5,4},{6,7},{7,6},{8,9},{9,8},{10,11... | collective-permute-start | bytes 786440 | tf_op jit(solution)/shard_map/ppermute | solution.py:28
  84.9 0.2 collective-permute-done.16.refs_4_
  85.1 0.7 copy-done.10
  85.8 3.1 %shard_map.63 = (f32[2,256,256]{2,1,0:T(8,128)}, bf16[2,256,256]{2,1,0:T(8,128)(2,1)}) custom-call(s32[3]{0:T(128)} %pad_add_fusion.1.table.refs_0_, s32[4]{0:T(128)} %_.5, f32[2,512,512]{2,1,0:T(8,128)} %get-tuple-element.26.refs_2_, bf16[2,512,256]{2,1,0:T(8,128)(2,1)} %get-tuple-element.27.refs_3_, bf16[2,256,256]{2,1,0:T(8,128)(2,1)} %copy-done.10), custom_call_target="tpu_custom_call" | custom-call | flops 268435456 | bytes 3670044 | tf_op jit(solution)/shard_map/pallas_call | solution.py:42
  88.9 0.8 collective-permute-start.17
  89.7 2.2 %collective-permute-done.19.given1 = bf16[2,256,256]{2,1,0:T(8,128)(2,1)S(1)} collective-permute-done((bf16[2,256,256]{2,1,0:T(8,128)(2,1)}, bf16[2,256,256]{2,1,0:T(8,128)(2,1)S(1)}, u32[]{:S(2)}, u32[]{:S(2)}) %collective-permute-start.19) | collective-permute-done | bytes 262176 | tf_op jit(solution)/shard_map/ppermute | solution.py:28
  91.9 5.3 %collective-permute-done.17.given0 = bf16[2,256,256]{2,1,0:T(8,128)(2,1)S(1)} collective-permute-done((bf16[2,256,256]{2,1,0:T(8,128)(2,1)}, bf16[2,256,256]{2,1,0:T(8,128)(2,1)S(1)}, u32[]{:S(2)}, u32[]{:S(2)}) %collective-permute-start.17) | collective-permute-done | bytes 262176 | tf_op jit(solution)/shard_map/ppermute | solution.py:28
  97.2 0.7 copy-done.9
  97.9 2.4 %shard_map.65 = f32[2,256,512]{2,1,0:T(8,128)} custom-call(s32[3]{0:T(128)} %pad_add_fusion.1.table.refs_0_, s32[4]{0:T(128)} %_.5, f32[2,256,256]{2,1,0:T(8,128)} %get-tuple-element.28.mine0, bf16[2,256,256]{2,1,0:T(8,128)(2,1)} %copy-done.9, f32[2,256,256]{2,1,0:T(8,128)} %get-tuple-element.30.mine1, bf16[2,256,256]{2,1,0:T(8,128)(2,1)} %copy-done.8), custom_call_target="tpu_custom_call" | custom-call | bytes 2621468 | tf_op jit(solution)/shard_map/pallas_call | solution.py:42
  (37 shorter events, 0.1 us)
Async XLA Ops:
  0.6 36.1 %copy-start = (bf16[1,1,2,256,512]{4,3,2,1,0:T(8,128)(2,1)S(1)}, bf16[1,1,2,256,512]{4,3,2,1,0:T(8,128)(2,1)}, u32[]{:S(2)}) copy-start(bf16[1,1,2,256,512]{4,3,2,1,0:T(8,128)(2,1)} %param.4) | copy-start | bytes 1572868
  2.7 2.7 %collective-permute-start.2 = (bf16[2,256,256]{2,1,0:T(8,128)(2,1)}, bf16[2,256,256]{2,1,0:T(8,128)(2,1)S(1)}, u32[]{:S(2)}, u32[]{:S(2)}) collective-permute-start(bf16[2,256,256]{2,1,0:T(8,128)(2,1)} %get-tuple-element.17), channel_id=1, source_target_pairs={{26,30},{27,31}} | collective-permute-start | bytes 786440 | tf_op jit(solution)/shard_map/ppermute | solution.py:83
  3.4 2.8 %collective-permute-start.4 = (bf16[2,256,256]{2,1,0:T(8,128)(2,1)}, bf16[2,256,256]{2,1,0:T(8,128)(2,1)S(1)}, u32[]{:S(2)}, u32[]{:S(2)}) collective-permute-start(bf16[2,256,256]{2,1,0:T(8,128)(2,1)} %get-tuple-element.18), channel_id=1, source_target_pairs={{26,31},{27,30}} | collective-permute-start | bytes 786440 | tf_op jit(solution)/shard_map/ppermute | solution.py:83
  4.0 3.4 %collective-permute-start = (bf16[2,256,256]{2,1,0:T(8,128)(2,1)}, bf16[2,256,256]{2,1,0:T(8,128)(2,1)S(1)}, u32[]{:S(2)}, u32[]{:S(2)}) collective-permute-start(bf16[2,256,256]{2,1,0:T(8,128)(2,1)} %get-tuple-element.17), channel_id=1, source_target_pairs={{8,2},{9,3},{16,4},{17,5},{18,12},{19,13},{24,6},{25,7},{28,22},{2... | collective-permute-start | bytes 786440 | tf_op jit(solution)/shard_map/ppermute | solution.py:83
  4.7 2.8 %collective-permute-start.1 = (bf16[2,256,256]{2,1,0:T(8,128)(2,1)}, bf16[2,256,256]{2,1,0:T(8,128)(2,1)S(1)}, u32[]{:S(2)}, u32[]{:S(2)}) collective-permute-start(bf16[2,256,256]{2,1,0:T(8,128)(2,1)} %get-tuple-element.18), channel_id=1, source_target_pairs={{8,3},{9,2},{16,5},{17,4},{18,13},{19,12},{24,7},{25,6},{28,23},{2... | collective-permute-start | bytes 786440 | tf_op jit(solution)/shard_map/ppermute | solution.py:83
  5.4 2.1 %collective-permute-start.3 = (bf16[2,256,256]{2,1,0:T(8,128)(2,1)S(1)}, bf16[2,256,256]{2,1,0:T(8,128)(2,1)S(1)}, u32[]{:S(2)}, u32[]{:S(2)}) collective-permute-start(bf16[2,256,256]{2,1,0:T(8,128)(2,1)S(1)} %collective-permute-done.2), channel_id=1, source_target_pairs={{30,14},{31,15}} | collective-permute-start | bytes 786440 | tf_op jit(solution)/shard_map/ppermute | solution.py:83
  6.1 1.4 %collective-permute-start.5 = (bf16[2,256,256]{2,1,0:T(8,128)(2,1)S(1)}, bf16[2,256,256]{2,1,0:T(8,128)(2,1)S(1)}, u32[]{:S(2)}, u32[]{:S(2)}) collective-permute-start(bf16[2,256,256]{2,1,0:T(8,128)(2,1)S(1)} %collective-permute-done.4), channel_id=1, source_target_pairs={{30,14},{31,15}} | collective-permute-start | bytes 786440 | tf_op jit(solution)/shard_map/ppermute | solution.py:83
  7.5 0.7 copy-start.2
  7.5 0.8 copy-start.4
  7.5 0.9 copy-start.5
  8.4 0.7 copy-start.6
  12.4 45.1 %copy-start.15 = (bf16[2,256,256]{2,1,0:T(8,128)(2,1)S(1)}, bf16[2,256,256]{2,1,0:T(8,128)(2,1)}, u32[]{:S(2)}) copy-start(bf16[2,256,256]{2,1,0:T(8,128)(2,1)} %get-tuple-element.23.home1) | copy-start | bytes 786436
  12.4 30.3 %collective-permute-start.8 = (bf16[2,256,256]{2,1,0:T(8,128)(2,1)}, bf16[2,256,256]{2,1,0:T(8,128)(2,1)S(1)}, u32[]{:S(2)}, u32[]{:S(2)}) collective-permute-start(bf16[2,256,256]{2,1,0:T(8,128)(2,1)} %get-tuple-element.20), channel_id=1, source_target_pairs={{0,4},{2,6},{4,0},{6,2},{1,5},{3,7},{5,1},{7,3},{8,12},{10,14},{12... | collective-permute-start | bytes 786440 | tf_op jit(solution)/shard_map/ppermute | solution.py:28
  36.7 11.7 %collective-permute-start.13 = (bf16[2,256,512]{2,1,0:T(8,128)(2,1)S(1)}, bf16[2,256,512]{2,1,0:T(8,128)(2,1)S(1)}, u32[]{:S(2)}, u32[]{:S(2)}) collective-permute-start(bf16[2,256,512]{2,1,0:T(8,128)(2,1)S(1)} %bitcast.12), channel_id=1, source_target_pairs={{0,24},{1,25},{8,16},{9,17},{10,18},{11,19},{20,12},{21,13},{28,4}... | collective-permute-start | bytes 1572872 | tf_op jit(solution)/shard_map/ppermute | solution.py:83
  38.0 7.6 %collective-permute-start.9 = (bf16[2,256,256]{2,1,0:T(8,128)(2,1)}, bf16[2,256,256]{2,1,0:T(8,128)(2,1)S(1)}, u32[]{:S(2)}, u32[]{:S(2)}) collective-permute-start(bf16[2,256,256]{2,1,0:T(8,128)(2,1)} %get-tuple-element.21), channel_id=1, source_target_pairs={{0,5},{1,4},{2,7},{3,6},{4,1},{5,0},{6,3},{7,2},{8,13},{9,12},{10,... | collective-permute-start | bytes 786440 | tf_op jit(solution)/shard_map/ppermute | solution.py:132
  38.1 34.6 %collective-permute-start.11 = (bf16[2,256,512]{2,1,0:T(8,128)(2,1)S(1)}, bf16[2,256,512]{2,1,0:T(8,128)(2,1)S(1)}, u32[]{:S(2)}, u32[]{:S(2)}) collective-permute-start(bf16[2,256,512]{2,1,0:T(8,128)(2,1)S(1)} %bitcast.13), channel_id=1, source_target_pairs={{0,8},{1,9},{8,0},{9,1},{10,2},{11,3},{16,24},{17,25},{18,26},{19,... | collective-permute-start | bytes 1572872 | tf_op jit(solution)/shard_map/ppermute | solution.py:83
  40.1 8.2 %collective-permute-start.6 = (bf16[2,256,256]{2,1,0:T(8,128)(2,1)}, bf16[2,256,256]{2,1,0:T(8,128)(2,1)S(1)}, u32[]{:S(2)}, u32[]{:S(2)}) collective-permute-start(bf16[2,256,256]{2,1,0:T(8,128)(2,1)} %get-tuple-element.21), channel_id=1, source_target_pairs={{0,1},{1,0},{2,3},{3,2},{4,5},{5,4},{6,7},{7,6},{8,9},{9,8},{10,11... | collective-permute-start | bytes 786440 | tf_op jit(solution)/shard_map/ppermute | solution.py:28
  42.7 14.8 %collective-permute-start.14 = (bf16[2,256,256]{2,1,0:T(8,128)(2,1)}, bf16[2,256,256]{2,1,0:T(8,128)(2,1)S(1)}, u32[]{:S(2)}, u32[]{:S(2)}) collective-permute-start(bf16[2,256,256]{2,1,0:T(8,128)(2,1)} %get-tuple-element.22.home0), channel_id=1, source_target_pairs={{2,26},{3,27},{4,28},{5,29},{6,30},{7,31},{12,20},{13,21},{14,22},... | collective-permute-start | bytes 786440 | tf_op jit(solution)/shard_map/ppermute | solution.py:83
  45.6 27.8 %collective-permute-start.12 = (bf16[2,256,512]{2,1,0:T(8,128)(2,1)}, bf16[2,256,512]{2,1,0:T(8,128)(2,1)}, u32[]{:S(2)}, u32[]{:S(2)}) collective-permute-start(bf16[2,256,512]{2,1,0:T(8,128)(2,1)} %get-tuple-element.19), channel_id=1, source_target_pairs={{2,10},{3,11},{4,12},{5,13},{6,14},{7,15},{12,4},{13,5},{14,6},{15... | collective-permute-start | bytes 1572872 | tf_op jit(solution)/shard_map/ppermute | solution.py:83
  47.1 26.4 %copy-start.13 = (bf16[2,512,256]{2,1,0:T(8,128)(2,1)}, bf16[2,512,256]{2,1,0:T(8,128)(2,1)S(1)}, u32[]{:S(2)}) copy-start(bf16[2,512,256]{2,1,0:T(8,128)(2,1)S(1)} %constant_dynamic-update-slice_fusion.2.left2) | copy-start | bytes 1572868
  48.4 25.1 %collective-permute-start.10 = (bf16[2,512,256]{2,1,0:T(8,128)(2,1)S(1)}, bf16[2,512,256]{2,1,0:T(8,128)(2,1)}, u32[]{:S(2)}, u32[]{:S(2)}) collective-permute-start(bf16[2,512,256]{2,1,0:T(8,128)(2,1)S(1)} %constant_dynamic-update-slice_fusion.2.left2), channel_id=1, source_target_pairs={{0,2},{2,0},{4,6},{6,4},{1,3},{3,1},{5,7},{7,5},{8,10},{10,8},{12,... | collective-permute-start | bytes 1572872 | tf_op jit(solution)/shard_map/ppermute | solution.py:28
  48.4 25.1 %copy-start.12 = (bf16[2,512,256]{2,1,0:T(8,128)(2,1)}, bf16[2,512,256]{2,1,0:T(8,128)(2,1)S(1)}, u32[]{:S(2)}) copy-start(bf16[2,512,256]{2,1,0:T(8,128)(2,1)S(1)} %constant_dynamic-update-slice_fusion.left0) | copy-start | bytes 1572868
  48.4 19.3 %copy-start.1 = (bf16[2,256,512]{2,1,0:T(8,128)(2,1)}, bf16[2,256,512]{2,1,0:T(8,128)(2,1)S(1)}, u32[]{:S(2)}) copy-start(bf16[2,256,512]{2,1,0:T(8,128)(2,1)S(1)} %collective-permute-done.13.early) | copy-start | bytes 1572868
  48.4 25.1 %collective-permute-start.7 = (bf16[2,512,256]{2,1,0:T(8,128)(2,1)S(1)}, bf16[2,512,256]{2,1,0:T(8,128)(2,1)}, u32[]{:S(2)}, u32[]{:S(2)}) collective-permute-start(bf16[2,512,256]{2,1,0:T(8,128)(2,1)S(1)} %constant_dynamic-update-slice_fusion.left0), channel_id=1, source_target_pairs={{0,2},{2,0},{4,6},{6,4},{1,3},{3,1},{5,7},{7,5},{8,10},{10,8},{12,... | collective-permute-start | bytes 1572872 | tf_op jit(solution)/shard_map/ppermute | solution.py:28
  57.5 10.2 %copy-start.3 = (bf16[2,256,256]{2,1,0:T(8,128)(2,1)}, bf16[2,256,256]{2,1,0:T(8,128)(2,1)S(1)}, u32[]{:S(2)}) copy-start(bf16[2,256,256]{2,1,0:T(8,128)(2,1)S(1)} %collective-permute-done.14.late0) | copy-start | bytes 786436
  57.5 10.2 %collective-permute-start.15 = (bf16[2,256,256]{2,1,0:T(8,128)(2,1)S(1)}, bf16[2,256,256]{2,1,0:T(8,128)(2,1)S(1)}, u32[]{:S(2)}, u32[]{:S(2)}) collective-permute-start(bf16[2,256,256]{2,1,0:T(8,128)(2,1)S(1)} %copy-done.15), channel_id=1, source_target_pairs={{2,26},{3,27},{4,28},{5,29},{6,30},{7,31},{12,20},{13,21},{14,22},... | collective-permute-start | bytes 786440 | tf_op jit(solution)/shard_map/ppermute | solution.py:83
  67.7 0.7 copy-start.7
  70.4 9.7 %collective-permute-start.18 = (bf16[2,256,256]{2,1,0:T(8,128)(2,1)}, bf16[2,256,256]{2,1,0:T(8,128)(2,1)S(1)}, u32[]{:S(2)}, u32[]{:S(2)}) collective-permute-start(bf16[2,256,256]{2,1,0:T(8,128)(2,1)} %get-tuple-element.25.far1), channel_id=1, source_target_pairs={{0,8},{8,0},{16,24},{24,16},{1,9},{9,1},{17,25},{25,17},{2,10},{10... | collective-permute-start | bytes 786440 | tf_op jit(solution)/shard_map/ppermute | solution.py:28
  72.8 0.8 copy-start.14
  72.8 12.4 %collective-permute-start.16 = (bf16[2,256,256]{2,1,0:T(8,128)(2,1)}, bf16[2,256,256]{2,1,0:T(8,128)(2,1)S(1)}, u32[]{:S(2)}, u32[]{:S(2)}) collective-permute-start(bf16[2,256,256]{2,1,0:T(8,128)(2,1)} %get-tuple-element.24.far0), channel_id=1, source_target_pairs={{0,8},{8,0},{16,24},{24,16},{1,9},{9,1},{17,25},{25,17},{2,10},{10... | collective-permute-start | bytes 786440 | tf_op jit(solution)/shard_map/ppermute | solution.py:28
  80.1 0.7 copy-start.11
  83.9 8.0 %collective-permute-start.19 = (bf16[2,256,256]{2,1,0:T(8,128)(2,1)}, bf16[2,256,256]{2,1,0:T(8,128)(2,1)S(1)}, u32[]{:S(2)}, u32[]{:S(2)}) collective-permute-start(bf16[2,256,256]{2,1,0:T(8,128)(2,1)} %get-tuple-element.31), channel_id=1, source_target_pairs={{0,1},{1,0},{2,3},{3,2},{4,5},{5,4},{6,7},{7,6},{8,9},{9,8},{10,11... | collective-permute-start | bytes 786440 | tf_op jit(solution)/shard_map/ppermute | solution.py:28
  85.1 0.7 copy-start.10
  88.9 8.3 %collective-permute-start.17 = (bf16[2,256,256]{2,1,0:T(8,128)(2,1)}, bf16[2,256,256]{2,1,0:T(8,128)(2,1)S(1)}, u32[]{:S(2)}, u32[]{:S(2)}) collective-permute-start(bf16[2,256,256]{2,1,0:T(8,128)(2,1)} %get-tuple-element.29), channel_id=1, source_target_pairs={{0,1},{1,0},{2,3},{3,2},{4,5},{5,4},{6,7},{7,6},{8,9},{9,8},{10,11... | collective-permute-start | bytes 786440 | tf_op jit(solution)/shard_map/ppermute | solution.py:28
  91.9 5.3 %copy-start.8 = (bf16[2,256,256]{2,1,0:T(8,128)(2,1)}, bf16[2,256,256]{2,1,0:T(8,128)(2,1)S(1)}, u32[]{:S(2)}) copy-start(bf16[2,256,256]{2,1,0:T(8,128)(2,1)S(1)} %collective-permute-done.19.given1) | copy-start | bytes 786436
  97.2 0.7 copy-start.9
where the time goes:
time: 101 us; the launch traced here: 100 us
  starting transfers between devices  42.2 us (42%)
  waiting for transfers between devices  28.5 us (28%)
  Pallas kernels  22 us (22%)
  local copies, waits for them, and re-layouts  5.47 us (5%)
  other arithmetic  1.26 us (1%)
    ppermute x8, starting transfers between devices, swap(): return lax.ppermute(value, axis, [(i, i ^ mask) for i in range(size)])  30.7 us
    pallas_call x7, Pallas kernels, local_call(): pl.pallas_call(kernel, out_shape=out_shape, in_specs=[SMEM] * tables + [V...  22 us
    ppermute x11, waiting for transfers between devices, send(): return lax.ppermute(value, AXES, pairs)  17.4 us
    ppermute x11, starting transfers between devices, send(): return lax.ppermute(value, AXES, pairs)  11.4 us
    ppermute x8, waiting for transfers between devices, swap(): return lax.ppermute(value, axis, [(i, i ^ mask) for i in range(size)])  9.5 us
    unnamed x34, local copies, waits for them, and re-layouts  5.44 us
  transfers between devices with their start and end apart: 20, of which 8 were waited for; matrix products, arithmetic and copies ran while one was open for 2% of the time, Pallas kernels for 14%

commit v1 on v0

--- a/solution.py
+++ b/solution.py
@@ -28,15 +28,11 @@
     return lax.ppermute(value, axis, [(i, i ^ mask) for i in range(size)])
 
 
-def scalars(*values):
-    return jnp.stack([jnp.asarray(value, jnp.int32) for value in values])
-
-
 SMEM = pl.BlockSpec(memory_space=pltpu.SMEM)
 VMEM = pl.BlockSpec(memory_space=pltpu.VMEM)
 
 
-def local_call(kernel, out_shape, operands, tables=2, scratch=(), flops=0):
+def local_call(kernel, out_shape, operands, tables=0, scratch=(), flops=0, limit=16 * 2**20):
     outs = out_shape if isinstance(out_shape, (list, tuple)) else [out_shape]
     moved = sum(x.size * x.dtype.itemsize for x in (*operands, *outs))
     return pl.pallas_call(
@@ -46,13 +42,16 @@
         out_specs=jax.tree.map(lambda _: VMEM, out_shape),
         scratch_shapes=scratch,
         cost_estimate=pl.CostEstimate(flops=flops, bytes_accessed=moved, transcendentals=0),
+        compiler_params=pltpu.CompilerParams(vmem_limit_bytes=limit),
     )(*operands)
 
 
-def mirror_kernel(place_ref, sign_ref, own_ref, *out_refs):
-    half = place_ref[0]
+def mirror_kernel(sign_ref, own_ref, *out_refs):
+    half = lax.axis_index("sub")
     rows, width = own_ref.shape[1:]
     group = width // sign_ref.shape[0]
+    *out_refs, copy_ref = out_refs
+    copy_ref[...] = own_ref[...]
     n_sub = len(out_refs)
     for shift in range(n_sub):
         target = lax.rem(half + shift, n_sub)
@@ -72,7 +71,9 @@
     n_sub = lax.axis_size("sub")
     rows = own.shape[1]
     piece = jax.ShapeDtypeStruct((2, rows, rows), own.dtype)
-    return local_call(mirror_kernel, [piece] * n_sub, (scalars(lax.axis_index("sub")), spin_signs, own))
+    whole = jax.ShapeDtypeStruct(own.shape, own.dtype)
+    *pieces, own = local_call(mirror_kernel, [piece] * n_sub + [whole], (spin_signs, own), tables=1)
+    return pieces, own
 
 
 def place(a, b, h):
@@ -108,7 +109,7 @@
 
 
 def fill_upper(own, spin_signs):
-    pieces = mirror_pieces(own, spin_signs)
+    pieces, own = mirror_pieces(own, spin_signs)
     shifts = range(lax.axis_size("sub"))
     return assemble(own, [send(pieces[k], mirror_pairs(k, lambda b, a: True)) for k in shifts])
 
@@ -141,11 +142,17 @@
     return jnp.dot(first, second, preferred_element_type=jnp.float32)
 
 
-def home_kernel(table, _, own, direct0, direct1, hand0, hand1, elem, home, home0, home1, keep, give):
-    lower, relayed, half = table[0], table[1], table[2]
+def stage_kernel(value, out):
+    out[...] = value[...]
+
+
+def home_kernel(own, direct0, direct1, hand0, hand1, elem, home, home0, home1, keep, give):
+    a, b, half = (lax.axis_index(axis) for axis in AXES)
+    lower = a >= b
+    relayed = (a == 1) & (b == 3)
     rows = own.shape[1]
 
-    @pl.when(lower == 1)
+    @pl.when(lower)
     def _():
         home[...] = own[...]
 
@@ -153,11 +160,11 @@
         home[:, :, pl.ds(pl.multiple_of(half * rows, 128), rows)] = first[...]
         home[:, :, pl.ds(pl.multiple_of((1 - half) * rows, 128), rows)] = second[...]
 
-    @pl.when((lower == 0) & (relayed == 0))
+    @pl.when(jnp.logical_not(lower | relayed))
     def _():
         put(direct0, direct1)
 
-    @pl.when((lower == 0) & (relayed == 1))
+    @pl.when(relayed)
     def _():
         put(hand0, hand1)
 
@@ -169,18 +176,25 @@
         out[1] = (dot(home[0], elem[1, :, columns]) + dot(home[1], elem[0, :, columns])).astype(jnp.bfloat16)
 
 
-def pick_kernel(table, _, early, late0, late1, out0, out1):
-    rows = out0.shape[2]
-
-    @pl.when(table[0] == 1)
-    def _():
-        out0[...] = early[:, :, :rows]
-        out1[...] = early[:, :, rows:]
-
-    @pl.when(table[0] == 0)
-    def _():
-        out0[...] = late0[...]
-        out1[...] = late1[...]
+def ready(a, b):
+    return a >= b
+
+
+def ready_far(a, b):
+    return (a >= b) & ((b >= 2) | (a < 2))
+
+
+def pick_kernel(part, early, late, out):
+    rows = out.shape[2]
+    was_ready = ready_far(lax.axis_index("src") ^ 3, lax.axis_index("snk"))
+
+    @pl.when(was_ready)
+    def _():
+        out[...] = early[:, :, part * rows : (part + 1) * rows]
+
+    @pl.when(jnp.logical_not(was_ready))
+    def _():
+        out[...] = late[...]
 
 
 def times(ins, moment):
@@ -196,8 +210,9 @@
     return real, imag
 
 
-def early_kernel(table, ins, left0, left1, left2, left3, home0, home1, near_early, near, far0, far1, acc, last, chosen, beside):
-    a, b, near_ready = table[0], table[1], table[2]
+def early_kernel(ins, left0, left1, left2, left3, home0, home1, near_early, near, far0, far1, acc, last, chosen, beside):
+    a, b = lax.axis_index("src"), lax.axis_index("snk")
+    near_ready = ready(a ^ 1, b)
     rows = home0.shape[2]
 
     def choose(k, out):
@@ -207,11 +222,11 @@
             def _():
                 out[...] = left[...]
 
-    @pl.when(near_ready == 1)
+    @pl.when(near_ready)
     def _():
         beside[...] = near_early[...]
 
-    @pl.when(near_ready == 0)
+    @pl.when(jnp.logical_not(near_ready))
     def _():
         beside[...] = near[...]
 
@@ -230,17 +245,17 @@
     choose(a ^ 2 ^ b, last)
 
 
-def late_kernel(part, table, ins, acc, last, block, mine, give):
+def late_kernel(part, ins, acc, last, block, mine, give):
     rows = mine.shape[1]
     columns = slice(part * rows, (part + 1) * rows)
-    real, imag = product(times(ins, table[0] ^ 2), last, block)
+    real, imag = product(times(ins, lax.axis_index("src") ^ 2), last, block)
     for index, value in ((0, real), (1, imag)):
         total = acc[index, :, columns] + value
         mine[index] = total[:rows]
         give[index] = total[rows:].astype(jnp.bfloat16)
 
 
-def finish_kernel(table, _, mine0, given0, mine1, given1, out):
+def finish_kernel(mine0, given0, mine1, given1, out):
     rows = mine0.shape[1]
     out[:, :, :rows] = mine0[...] + given0[...].astype(jnp.float32)
     out[:, :, rows:] = mine1[...] + given1[...].astype(jnp.float32)
@@ -257,8 +272,6 @@
 
 
 def by_doubling(own, elemental, spin_signs, insertions):
-    a = lax.axis_index("src")
-    b = lax.axis_index("snk")
     rows, width = own.shape[1:]
     parts = range(width // rows)
     shifts = range(lax.axis_size("sub"))
@@ -266,16 +279,12 @@
     def relayed(b, a):
         return (b, a) == (3, 1)
 
-    def ready(a, b):
-        return a >= b
-
-    def ready_far(a, b):
-        return a >= b and (b >= 2 or a < 2)
-
-    pieces = mirror_pieces(own, spin_signs)
+    pieces, own = mirror_pieces(own, spin_signs)
     relay = [send(pieces[k], [(place(3, 1, h), place(3, 3, (h + k) % 2)) for h in shifts]) for k in shifts]
     direct = [send(pieces[k], mirror_pairs(k, lambda b, a: not relayed(b, a))) for k in shifts]
     handed = [send(relay[k], [(place(3, 3, h), place(1, 3, h)) for h in shifts]) for k in shifts]
+    elemental = local_call(stage_kernel, jax.ShapeDtypeStruct(elemental.shape, elemental.dtype), (elemental,))
+    own, elemental = lax.optimization_barrier((own, elemental))
     near_early = send(own, along_z(1, ready))
     far_early = send(own, along_z(3, ready_far))
 
@@ -284,21 +293,22 @@
     full_half, home0, home1, keep, give = local_call(
         home_kernel,
         [tile, piece, piece, piece, piece],
-        (scalars(a >= b, (a == 1) & (b == 3), lax.axis_index("sub")), spin_signs, own, *direct, *handed, elemental),
+        (own, *direct, *handed, elemental),
         flops=8 * rows * width * width,
     )
     far_late = [send(value, along_z(3, lambda a, b: not ready_far(a, b))) for value in (home0, home1)]
     near = send(full_half, along_z(1, lambda a, b: not ready(a, b)))
-    from_far = a ^ 3
-    was_ready = (from_far >= b) & ((b >= 2) | (from_far < 2))
-    far = local_call(pick_kernel, [piece, piece], (scalars(was_ready), spin_signs, far_early, *far_late))
+    far = [
+        local_call(lambda *refs, part=part: pick_kernel(part, *refs), piece, (far_early, far_late[part]))
+        for part in parts
+    ]
     late = [swap(far[part], "src", 1) for part in parts]
     left = left_panel(keep, give)
-    table = scalars(a, b, (a ^ 1) >= b)
     acc, last = local_call(
         early_kernel,
         [jax.ShapeDtypeStruct((2, 2 * rows, width), jnp.float32), jax.ShapeDtypeStruct((2, 2 * rows, rows), own.dtype)],
-        (table, insertions, *left, home0, home1, near_early, near, *far),
+        (insertions, *left, home0, home1, near_early, near, *far),
+        tables=1,
         scratch=[pltpu.VMEM((2, 2 * rows, rows), own.dtype), pltpu.VMEM(own.shape, own.dtype)],
         flops=3 * 16 * rows * rows * width,
     )
@@ -307,11 +317,12 @@
         mine, given = local_call(
             lambda *refs, part=part: late_kernel(part, *refs),
             [jax.ShapeDtypeStruct((2, rows, rows), jnp.float32), piece],
-            (table, insertions, acc, last, late[part]),
+            (insertions, acc, last, late[part]),
+            tables=1,
             flops=16 * rows * rows * rows,
         )
         ends += [mine, swap(given, "sub", 1)]
-    total = local_call(finish_kernel, jax.ShapeDtypeStruct(own.shape, jnp.float32), (table, insertions, *ends))
+    total = local_call(finish_kernel, jax.ShapeDtypeStruct(own.shape, jnp.float32), tuple(ends))
     return full_half, total
 
 

time: 101 us -> 88.9 us (0.88)
  Pallas kernels: 22 us -> 8.34 us
  waiting for transfers between devices: 28.5 us -> 35 us
  local copies, waits for them, and re-layouts: 5.47 us -> 2.99 us
  other arithmetic: 1.26 us -> 0 us
    pallas_call x7 -> x9, Pallas kernels: 22 us -> 8.34 us  [local_call(): pl.pallas_call(kernel, out_shape=out_shape, in_specs=[SMEM] * tables + [V...]
    ppermute x8, waiting for transfers between devices: 9.5 us -> 15.1 us  [swap(): return lax.ppermute(value, axis, [(i, i ^ mask) for i in range(size)])]
    unnamed x34 -> x10, local copies, waits for them, and re-layouts: 5.44 us -> 2.95 us
    another operation x2 -> x0, other arithmetic: 1.26 us -> none  [scalars(): return jnp.stack([jnp.asarray(value, jnp.int32) for value in values])]
  transfers between devices with their start and end apart: 20 -> 20, of which waited for: 8 -> 9; matrix products, arithmetic and copies ran while one was open for 2% -> 0% of each run, Pallas kernels for 14% -> 6%
where the time goes in v1:
time: 88.9 us; the launch traced here: 88.6 us
  starting transfers between devices  41.3 us (46%)
  waiting for transfers between devices  35 us (39%)
  Pallas kernels  8.34 us (9%)
  local copies, waits for them, and re-layouts  2.99 us (3%)
  between operations  0.93 us (1%)
    ppermute x8, starting transfers between devices, swap(): return lax.ppermute(value, axis, [(i, i ^ mask) for i in range(size)])  30.7 us
    ppermute x11, waiting for transfers between devices, send(): return lax.ppermute(value, AXES, pairs)  17.4 us
    ppermute x8, waiting for transfers between devices, swap(): return lax.ppermute(value, axis, [(i, i ^ mask) for i in range(size)])  15.1 us
    ppermute x11, starting transfers between devices, send(): return lax.ppermute(value, AXES, pairs)  10.5 us
    pallas_call x9, Pallas kernels, local_call(): pl.pallas_call(kernel, out_shape=out_shape, in_specs=[SMEM] * tables + [V...  8.34 us
    unnamed x10, local copies, waits for them, and re-layouts  2.95 us
    ppermute x1, waiting for transfers between devices, left_panel(): give_x = lax.ppermute(give, ('snk', 'sub'), across)  2.49 us
  transfers between devices with their start and end apart: 20, of which 9 were waited for; matrix products, arithmetic and copies ran while one was open for 0% of the time, Pallas kernels for 6%

profile of v1, /device:TPU:0, one launch (start us, length us, event | category | flops | bytes accessed | tf_op | source)
XLA Modules:
  0.0 88.6 jit_solution(10207422555430753456)
XLA Ops:
  0.6 1.0 %copy-done.1 = bf16[1,1,2,256,512]{4,3,2,1,0:T(8,128)(2,1)S(1)} copy-done((bf16[1,1,2,256,512]{4,3,2,1,0:T(8,128)(2,1)S(1)}, bf16[1,1,2,256,512]{4,3,2,1,0:T(8,128)(2,1)}, u32[]{:S(2)}) %copy-start.1) | copy-done | bytes 524312
  1.7 0.7 copy-done.3
  2.3 0.8 shard_map.59
  3.1 0.7 collective-permute-start.2
  3.8 0.7 collective-permute-start.4
  4.5 0.7 collective-permute-start
  5.2 0.7 collective-permute-start.1
  5.8 0.0 collective-permute-done.2
  5.9 0.7 collective-permute-start.3
  6.5 0.0 collective-permute-done.4
  6.6 0.7 collective-permute-start.5
  7.2 0.0 copy-start
  7.2 1.2 %copy-done = bf16[2,512,512]{2,1,0:T(8,128)(2,1)S(1)} copy-done((bf16[2,512,512]{2,1,0:T(8,128)(2,1)S(1)}, bf16[2,512,512]{2,1,0:T(8,128)(2,1)}, u32[]{:S(2)}) %copy-start) | copy-done | bytes 1048600
  8.5 0.1 shard_map.60.elem
  8.5 0.0 collective-permute-done.direct0
  8.6 0.0 collective-permute-done.3.hand0
  8.6 1.4 %shard_map.61 = (bf16[2,256,512]{2,1,0:T(8,128)(2,1)}, bf16[2,256,256]{2,1,0:T(8,128)(2,1)S(1)}, bf16[2,256,256]{2,1,0:T(8,128)(2,1)S(1)}, bf16[2,256,256]{2,1,0:T(8,128)(2,1)S(1)}, bf16[2,256,256]{2,1,0:T(8,128)(2,1)S(1)}) custom-call(bf16[2,256,512]{2,1,0:T(8,128)(2,1)S(1)} %get-tuple-element.19.own, ...), custom_call_target="tpu_custom_call" | custom-call | flops 536870912 | bytes 4194304 | tf_op jit(solution)/shard_map/pallas_call | solution.py:38
  9.9 23.6 %collective-permute-start.8 = (bf16[2,256,256]{2,1,0:T(8,128)(2,1)S(1)}, bf16[2,256,256]{2,1,0:T(8,128)(2,1)S(1)}, u32[]{:S(2)}, u32[]{:S(2)}) collective-permute-start(bf16[2,256,256]{2,1,0:T(8,128)(2,1)S(1)} %get-tuple-element.24), channel_id=1, source_target_pairs={{0,4},{2,6},{4,0},{6,2},{1,5},{3,7},{5,1},{7,3},{8,12},{10,14},{12... | collective-permute-start | bytes 786440 | tf_op jit(solution)/shard_map/ppermute | solution.py:28
  33.5 1.3 %collective-permute-start.13 = (bf16[2,256,512]{2,1,0:T(8,128)(2,1)S(1)}, bf16[2,256,512]{2,1,0:T(8,128)(2,1)S(1)}, u32[]{:S(2)}, u32[]{:S(2)}) collective-permute-start(bf16[2,256,512]{2,1,0:T(8,128)(2,1)S(1)} %get-tuple-element.19.own), channel_id=1, source_target_pairs={{0,24},{1,25},{8,16},{9,17},{10,18},{11,19},{20,12},{21,13},{28,4}... | collective-permute-start | bytes 1572872 | tf_op jit(solution)/shard_map/ppermute | solution.py:84
  34.8 0.0 copy-start.2
  34.8 0.1 collective-permute-start.9
  34.9 1.9 %collective-permute-start.11 = (bf16[2,256,512]{2,1,0:T(8,128)(2,1)S(1)}, bf16[2,256,512]{2,1,0:T(8,128)(2,1)S(1)}, u32[]{:S(2)}, u32[]{:S(2)}) collective-permute-start(bf16[2,256,512]{2,1,0:T(8,128)(2,1)S(1)} %get-tuple-element.19.own), channel_id=1, source_target_pairs={{0,8},{1,9},{8,0},{9,1},{10,2},{11,3},{16,24},{17,25},{18,26},{19,... | collective-permute-start | bytes 1572872 | tf_op jit(solution)/shard_map/ppermute | solution.py:84
  36.9 1.5 %collective-permute-start.6 = (bf16[2,256,256]{2,1,0:T(8,128)(2,1)S(1)}, bf16[2,256,256]{2,1,0:T(8,128)(2,1)S(1)}, u32[]{:S(2)}, u32[]{:S(2)}) collective-permute-start(bf16[2,256,256]{2,1,0:T(8,128)(2,1)S(1)} %get-tuple-element.25), channel_id=1, source_target_pairs={{0,1},{1,0},{2,3},{3,2},{4,5},{5,4},{6,7},{7,6},{8,9},{9,8},{10,11... | collective-permute-start | bytes 786440 | tf_op jit(solution)/shard_map/ppermute | solution.py:28
  38.3 0.1 collective-permute-done.8
  38.5 1.3 %collective-permute-start.15 = (bf16[2,256,256]{2,1,0:T(8,128)(2,1)S(1)}, bf16[2,256,256]{2,1,0:T(8,128)(2,1)S(1)}, u32[]{:S(2)}, u32[]{:S(2)}) collective-permute-start(bf16[2,256,256]{2,1,0:T(8,128)(2,1)S(1)} %get-tuple-element.27.home1), channel_id=1, source_target_pairs={{2,26},{3,27},{4,28},{5,29},{6,30},{7,31},{12,20},{13,21},{14,22},... | collective-permute-start | bytes 786440 | tf_op jit(solution)/shard_map/ppermute | solution.py:84
  39.8 2.5 %collective-permute-done.9 = bf16[2,256,256]{2,1,0:T(8,128)(2,1)S(1)} collective-permute-done((bf16[2,256,256]{2,1,0:T(8,128)(2,1)S(1)}, bf16[2,256,256]{2,1,0:T(8,128)(2,1)S(1)}, u32[]{:S(2)}, u32[]{:S(2)}) %collective-permute-start.9) | collective-permute-done | bytes 262176 | tf_op jit(solution)/shard_map/ppermute | solution.py:133
  42.3 0.7 collective-permute-start.12
  43.0 2.0 %collective-permute-done.6 = bf16[2,256,256]{2,1,0:T(8,128)(2,1)S(1)} collective-permute-done((bf16[2,256,256]{2,1,0:T(8,128)(2,1)S(1)}, bf16[2,256,256]{2,1,0:T(8,128)(2,1)S(1)}, u32[]{:S(2)}, u32[]{:S(2)}) %collective-permute-start.6) | collective-permute-done | bytes 262176 | tf_op jit(solution)/shard_map/ppermute | solution.py:28
  45.0 0.0 collective-permute-done.13.refs_0_
  45.0 0.6 collective-permute-start.7
  45.6 8.5 %collective-permute-done.15.refs_1_ = bf16[2,256,256]{2,1,0:T(8,128)(2,1)S(1)} collective-permute-done((bf16[2,256,256]{2,1,0:T(8,128)(2,1)S(1)}, bf16[2,256,256]{2,1,0:T(8,128)(2,1)S(1)}, u32[]{:S(2)}, u32[]{:S(2)}) %collective-permute-start.15) | collective-permute-done | bytes 262176 | tf_op jit(solution)/shard_map/ppermute | solution.py:84
  54.1 1.3 %collective-permute-start.14 = (bf16[2,256,256]{2,1,0:T(8,128)(2,1)S(1)}, bf16[2,256,256]{2,1,0:T(8,128)(2,1)S(1)}, u32[]{:S(2)}, u32[]{:S(2)}) collective-permute-start(bf16[2,256,256]{2,1,0:T(8,128)(2,1)S(1)} %get-tuple-element.26.home0), channel_id=1, source_target_pairs={{2,26},{3,27},{4,28},{5,29},{6,30},{7,31},{12,20},{13,21},{14,22},... | collective-permute-start | bytes 786440 | tf_op jit(solution)/shard_map/ppermute | solution.py:84
  55.4 8.8 %collective-permute-done.14.refs_1_ = bf16[2,256,256]{2,1,0:T(8,128)(2,1)S(1)} collective-permute-done((bf16[2,256,256]{2,1,0:T(8,128)(2,1)S(1)}, bf16[2,256,256]{2,1,0:T(8,128)(2,1)S(1)}, u32[]{:S(2)}, u32[]{:S(2)}) %collective-permute-start.14) | collective-permute-done | bytes 262176 | tf_op jit(solution)/shard_map/ppermute | solution.py:84
  64.3 2.3 %collective-permute-start.18 = (bf16[2,256,256]{2,1,0:T(8,128)(2,1)S(1)}, bf16[2,256,256]{2,1,0:T(8,128)(2,1)S(1)}, u32[]{:S(2)}, u32[]{:S(2)}) collective-permute-start(bf16[2,256,256]{2,1,0:T(8,128)(2,1)S(1)} %shard_map.63.far1), channel_id=1, source_target_pairs={{0,8},{8,0},{16,24},{24,16},{1,9},{9,1},{17,25},{25,17},{2,10},{10... | collective-permute-start | bytes 786440 | tf_op jit(solution)/shard_map/ppermute | solution.py:28
  66.6 0.0 collective-permute-done.11.near_early
  66.6 0.1 collective-permute-start.16
  66.7 0.0 collective-permute-done.12.near
  66.7 0.0 collective-permute-done.10.left3
  66.7 3.0 %shard_map.64 = (f32[2,512,512]{2,1,0:T(8,128)S(1)}, bf16[2,512,256]{2,1,0:T(8,128)(2,1)S(1)}) custom-call(s32[4]{0:T(128)S(1)} %copy-done.2, bf16[2,512,256]{2,1,0:T(8,128)(2,1)S(1)} %constant_dynamic-update-slice_fusion.left0, bf16[2,512,256]{2,1,0:T(8,128)(2,1)S(1)} %collective-permute-done.7.left1, ...), custom_call_target="tpu_custom_call" | custom-call | flops 1610612736 | bytes 6815760 | tf_op jit(solution)/shard_map/pallas_call | solution.py:38
  69.7 4.0 %collective-permute-done.18.refs_3_ = bf16[2,256,256]{2,1,0:T(8,128)(2,1)S(1)} collective-permute-done((bf16[2,256,256]{2,1,0:T(8,128)(2,1)S(1)}, bf16[2,256,256]{2,1,0:T(8,128)(2,1)S(1)}, u32[]{:S(2)}, u32[]{:S(2)}) %collective-permute-start.18) | collective-permute-done | bytes 262176 | tf_op jit(solution)/shard_map/ppermute | solution.py:28
  73.7 1.0 %shard_map.66 = (f32[2,256,256]{2,1,0:T(8,128)S(1)}, bf16[2,256,256]{2,1,0:T(8,128)(2,1)S(1)}) custom-call(s32[4]{0:T(128)S(1)} %copy-done.2, f32[2,512,512]{2,1,0:T(8,128)S(1)} %get-tuple-element.28.refs_1_, bf16[2,512,256]{2,1,0:T(8,128)(2,1)S(1)} %get-tuple-element.29.refs_2_, bf16[2,256,256]{2,1,0:T(8,128)(2,1)S(1)} %collective-permute-done.18.refs_3_), custom_call_target="tpu_custom_call" | custom-call | flops 268435456 | bytes 3670032 | tf_op jit(solution)/shard_map/pallas_call | solution.py:38
  74.7 1.4 %collective-permute-start.19 = (bf16[2,256,256]{2,1,0:T(8,128)(2,1)S(1)}, bf16[2,256,256]{2,1,0:T(8,128)(2,1)S(1)}, u32[]{:S(2)}, u32[]{:S(2)}) collective-permute-start(bf16[2,256,256]{2,1,0:T(8,128)(2,1)S(1)} %get-tuple-element.33), channel_id=1, source_target_pairs={{0,1},{1,0},{2,3},{3,2},{4,5},{5,4},{6,7},{7,6},{8,9},{9,8},{10,11... | collective-permute-start | bytes 786440 | tf_op jit(solution)/shard_map/ppermute | solution.py:28
  76.1 2.6 %collective-permute-done.16.refs_3_ = bf16[2,256,256]{2,1,0:T(8,128)(2,1)S(1)} collective-permute-done((bf16[2,256,256]{2,1,0:T(8,128)(2,1)S(1)}, bf16[2,256,256]{2,1,0:T(8,128)(2,1)S(1)}, u32[]{:S(2)}, u32[]{:S(2)}) %collective-permute-start.16) | collective-permute-done | bytes 262176 | tf_op jit(solution)/shard_map/ppermute | solution.py:28
  78.7 1.0 %shard_map.65 = (f32[2,256,256]{2,1,0:T(8,128)S(1)}, bf16[2,256,256]{2,1,0:T(8,128)(2,1)S(1)}) custom-call(s32[4]{0:T(128)S(1)} %copy-done.2, f32[2,512,512]{2,1,0:T(8,128)S(1)} %get-tuple-element.28.refs_1_, bf16[2,512,256]{2,1,0:T(8,128)(2,1)S(1)} %get-tuple-element.29.refs_2_, bf16[2,256,256]{2,1,0:T(8,128)(2,1)S(1)} %collective-permute-done.16.refs_3_), custom_call_target="tpu_custom_call" | custom-call | flops 268435456 | bytes 3670032 | tf_op jit(solution)/shard_map/pallas_call | solution.py:38
  79.7 1.4 %collective-permute-start.17 = (bf16[2,256,256]{2,1,0:T(8,128)(2,1)S(1)}, bf16[2,256,256]{2,1,0:T(8,128)(2,1)S(1)}, u32[]{:S(2)}, u32[]{:S(2)}) collective-permute-start(bf16[2,256,256]{2,1,0:T(8,128)(2,1)S(1)} %get-tuple-element.31), channel_id=1, source_target_pairs={{0,1},{1,0},{2,3},{3,2},{4,5},{5,4},{6,7},{7,6},{8,9},{9,8},{10,11... | collective-permute-start | bytes 786440 | tf_op jit(solution)/shard_map/ppermute | solution.py:28
  81.1 0.8 collective-permute-done.19.given1
  81.9 5.6 %collective-permute-done.17.given0 = bf16[2,256,256]{2,1,0:T(8,128)(2,1)S(1)} collective-permute-done((bf16[2,256,256]{2,1,0:T(8,128)(2,1)S(1)}, bf16[2,256,256]{2,1,0:T(8,128)(2,1)S(1)}, u32[]{:S(2)}, u32[]{:S(2)}) %collective-permute-start.17) | collective-permute-done | bytes 262176 | tf_op jit(solution)/shard_map/ppermute | solution.py:28
  87.5 1.1 %shard_map.67 = f32[2,256,512]{2,1,0:T(8,128)} custom-call(f32[2,256,256]{2,1,0:T(8,128)S(1)} %get-tuple-element.30.mine0, bf16[2,256,256]{2,1,0:T(8,128)(2,1)S(1)} %collective-permute-done.17.given0, f32[2,256,256]{2,1,0:T(8,128)S(1)} %get-tuple-element.32.mine1, bf16[2,256,256]{2,1,0:T(8,128)(2,1)S(1)} %collective-permute-done.19.given1), custom_call_target="tpu_custom_call" | custom-call | bytes 2621440 | tf_op jit(solution)/shard_map/pallas_call | solution.py:38
  (13 shorter events, 0.1 us)
Async XLA Ops:
  0.6 1.0 %copy-start.1 = (bf16[1,1,2,256,512]{4,3,2,1,0:T(8,128)(2,1)S(1)}, bf16[1,1,2,256,512]{4,3,2,1,0:T(8,128)(2,1)}, u32[]{:S(2)}) copy-start(bf16[1,1,2,256,512]{4,3,2,1,0:T(8,128)(2,1)} %param.4) | copy-start | bytes 1572868
  1.7 0.7 copy-start.3
  3.1 2.7 %collective-permute-start.2 = (bf16[2,256,256]{2,1,0:T(8,128)(2,1)S(1)}, bf16[2,256,256]{2,1,0:T(8,128)(2,1)S(1)}, u32[]{:S(2)}, u32[]{:S(2)}) collective-permute-start(bf16[2,256,256]{2,1,0:T(8,128)(2,1)S(1)} %get-tuple-element.20), channel_id=1, source_target_pairs={{26,30},{27,31}} | collective-permute-start | bytes 786440 | tf_op jit(solution)/shard_map/ppermute | solution.py:84
  3.8 2.8 %collective-permute-start.4 = (bf16[2,256,256]{2,1,0:T(8,128)(2,1)S(1)}, bf16[2,256,256]{2,1,0:T(8,128)(2,1)S(1)}, u32[]{:S(2)}, u32[]{:S(2)}) collective-permute-start(bf16[2,256,256]{2,1,0:T(8,128)(2,1)S(1)} %get-tuple-element.21), channel_id=1, source_target_pairs={{26,31},{27,30}} | collective-permute-start | bytes 786440 | tf_op jit(solution)/shard_map/ppermute | solution.py:84
  4.5 4.1 %collective-permute-start = (bf16[2,256,256]{2,1,0:T(8,128)(2,1)S(1)}, bf16[2,256,256]{2,1,0:T(8,128)(2,1)S(1)}, u32[]{:S(2)}, u32[]{:S(2)}) collective-permute-start(bf16[2,256,256]{2,1,0:T(8,128)(2,1)S(1)} %get-tuple-element.20), channel_id=1, source_target_pairs={{8,2},{9,3},{16,4},{17,5},{18,12},{19,13},{24,6},{25,7},{28,22},{2... | collective-permute-start | bytes 786440 | tf_op jit(solution)/shard_map/ppermute | solution.py:84
  5.2 3.4 %collective-permute-start.1 = (bf16[2,256,256]{2,1,0:T(8,128)(2,1)S(1)}, bf16[2,256,256]{2,1,0:T(8,128)(2,1)S(1)}, u32[]{:S(2)}, u32[]{:S(2)}) collective-permute-start(bf16[2,256,256]{2,1,0:T(8,128)(2,1)S(1)} %get-tuple-element.21), channel_id=1, source_target_pairs={{8,3},{9,2},{16,5},{17,4},{18,13},{19,12},{24,7},{25,6},{28,23},{2... | collective-permute-start | bytes 786440 | tf_op jit(solution)/shard_map/ppermute | solution.py:84
  5.9 2.7 %collective-permute-start.3 = (bf16[2,256,256]{2,1,0:T(8,128)(2,1)S(1)}, bf16[2,256,256]{2,1,0:T(8,128)(2,1)S(1)}, u32[]{:S(2)}, u32[]{:S(2)}) collective-permute-start(bf16[2,256,256]{2,1,0:T(8,128)(2,1)S(1)} %collective-permute-done.2), channel_id=1, source_target_pairs={{30,14},{31,15}} | collective-permute-start | bytes 786440 | tf_op jit(solution)/shard_map/ppermute | solution.py:84
  6.6 2.0 %collective-permute-start.5 = (bf16[2,256,256]{2,1,0:T(8,128)(2,1)S(1)}, bf16[2,256,256]{2,1,0:T(8,128)(2,1)S(1)}, u32[]{:S(2)}, u32[]{:S(2)}) collective-permute-start(bf16[2,256,256]{2,1,0:T(8,128)(2,1)S(1)} %collective-permute-done.4), channel_id=1, source_target_pairs={{30,14},{31,15}} | collective-permute-start | bytes 786440 | tf_op jit(solution)/shard_map/ppermute | solution.py:84
  7.2 1.2 %copy-start = (bf16[2,512,512]{2,1,0:T(8,128)(2,1)S(1)}, bf16[2,512,512]{2,1,0:T(8,128)(2,1)}, u32[]{:S(2)}) copy-start(bf16[2,512,512]{2,1,0:T(8,128)(2,1)} %value.1) | copy-start | bytes 3145732
  9.9 28.5 %collective-permute-start.8 = (bf16[2,256,256]{2,1,0:T(8,128)(2,1)S(1)}, bf16[2,256,256]{2,1,0:T(8,128)(2,1)S(1)}, u32[]{:S(2)}, u32[]{:S(2)}) collective-permute-start(bf16[2,256,256]{2,1,0:T(8,128)(2,1)S(1)} %get-tuple-element.24), channel_id=1, source_target_pairs={{0,4},{2,6},{4,0},{6,2},{1,5},{3,7},{5,1},{7,3},{8,12},{10,14},{12... | collective-permute-start | bytes 786440 | tf_op jit(solution)/shard_map/ppermute | solution.py:28
  33.5 11.5 %collective-permute-start.13 = (bf16[2,256,512]{2,1,0:T(8,128)(2,1)S(1)}, bf16[2,256,512]{2,1,0:T(8,128)(2,1)S(1)}, u32[]{:S(2)}, u32[]{:S(2)}) collective-permute-start(bf16[2,256,512]{2,1,0:T(8,128)(2,1)S(1)} %get-tuple-element.19.own), channel_id=1, source_target_pairs={{0,24},{1,25},{8,16},{9,17},{10,18},{11,19},{20,12},{21,13},{28,4}... | collective-permute-start | bytes 1572872 | tf_op jit(solution)/shard_map/ppermute | solution.py:84
  34.8 31.9 %copy-start.2 = (s32[4]{0:T(128)S(1)}, s32[4]{0:T(128)}, u32[]{:S(2)}) copy-start(s32[4]{0:T(128)} %refs_0_.3) | copy-start | bytes 52
  34.8 7.4 %collective-permute-start.9 = (bf16[2,256,256]{2,1,0:T(8,128)(2,1)S(1)}, bf16[2,256,256]{2,1,0:T(8,128)(2,1)S(1)}, u32[]{:S(2)}, u32[]{:S(2)}) collective-permute-start(bf16[2,256,256]{2,1,0:T(8,128)(2,1)S(1)} %get-tuple-element.25), channel_id=1, source_target_pairs={{0,5},{1,4},{2,7},{3,6},{4,1},{5,0},{6,3},{7,2},{8,13},{9,12},{10,... | collective-permute-start | bytes 786440 | tf_op jit(solution)/shard_map/ppermute | solution.py:133
  34.9 31.6 %collective-permute-start.11 = (bf16[2,256,512]{2,1,0:T(8,128)(2,1)S(1)}, bf16[2,256,512]{2,1,0:T(8,128)(2,1)S(1)}, u32[]{:S(2)}, u32[]{:S(2)}) collective-permute-start(bf16[2,256,512]{2,1,0:T(8,128)(2,1)S(1)} %get-tuple-element.19.own), channel_id=1, source_target_pairs={{0,8},{1,9},{8,0},{9,1},{10,2},{11,3},{16,24},{17,25},{18,26},{19,... | collective-permute-start | bytes 1572872 | tf_op jit(solution)/shard_map/ppermute | solution.py:84
  36.9 8.1 %collective-permute-start.6 = (bf16[2,256,256]{2,1,0:T(8,128)(2,1)S(1)}, bf16[2,256,256]{2,1,0:T(8,128)(2,1)S(1)}, u32[]{:S(2)}, u32[]{:S(2)}) collective-permute-start(bf16[2,256,256]{2,1,0:T(8,128)(2,1)S(1)} %get-tuple-element.25), channel_id=1, source_target_pairs={{0,1},{1,0},{2,3},{3,2},{4,5},{5,4},{6,7},{7,6},{8,9},{9,8},{10,11... | collective-permute-start | bytes 786440 | tf_op jit(solution)/shard_map/ppermute | solution.py:28
  38.5 15.6 %collective-permute-start.15 = (bf16[2,256,256]{2,1,0:T(8,128)(2,1)S(1)}, bf16[2,256,256]{2,1,0:T(8,128)(2,1)S(1)}, u32[]{:S(2)}, u32[]{:S(2)}) collective-permute-start(bf16[2,256,256]{2,1,0:T(8,128)(2,1)S(1)} %get-tuple-element.27.home1), channel_id=1, source_target_pairs={{2,26},{3,27},{4,28},{5,29},{6,30},{7,31},{12,20},{13,21},{14,22},... | collective-permute-start | bytes 786440 | tf_op jit(solution)/shard_map/ppermute | solution.py:84
  42.3 24.4 %collective-permute-start.12 = (bf16[2,256,512]{2,1,0:T(8,128)(2,1)}, bf16[2,256,512]{2,1,0:T(8,128)(2,1)S(1)}, u32[]{:S(2)}, u32[]{:S(2)}) collective-permute-start(bf16[2,256,512]{2,1,0:T(8,128)(2,1)} %get-tuple-element.23), channel_id=1, source_target_pairs={{2,10},{3,11},{4,12},{5,13},{6,14},{7,15},{12,4},{13,5},{14,6},{15... | collective-permute-start | bytes 1572872 | tf_op jit(solution)/shard_map/ppermute | solution.py:84
  45.0 21.7 %collective-permute-start.10 = (bf16[2,512,256]{2,1,0:T(8,128)(2,1)S(1)}, bf16[2,512,256]{2,1,0:T(8,128)(2,1)S(1)}, u32[]{:S(2)}, u32[]{:S(2)}) collective-permute-start(bf16[2,512,256]{2,1,0:T(8,128)(2,1)S(1)} %constant_dynamic-update-slice_fusion.2.left2), channel_id=1, source_target_pairs={{0,2},{2,0},{4,6},{6,4},{1,3},{3,1},{5,7},{7,5},{8,10},{10,8},{12,... | collective-permute-start | bytes 1572872 | tf_op jit(solution)/shard_map/ppermute | solution.py:28
  45.0 21.7 %collective-permute-start.7 = (bf16[2,512,256]{2,1,0:T(8,128)(2,1)S(1)}, bf16[2,512,256]{2,1,0:T(8,128)(2,1)S(1)}, u32[]{:S(2)}, u32[]{:S(2)}) collective-permute-start(bf16[2,512,256]{2,1,0:T(8,128)(2,1)S(1)} %constant_dynamic-update-slice_fusion.left0), channel_id=1, source_target_pairs={{0,2},{2,0},{4,6},{6,4},{1,3},{3,1},{5,7},{7,5},{8,10},{10,8},{12,... | collective-permute-start | bytes 1572872 | tf_op jit(solution)/shard_map/ppermute | solution.py:28
  54.1 10.2 %collective-permute-start.14 = (bf16[2,256,256]{2,1,0:T(8,128)(2,1)S(1)}, bf16[2,256,256]{2,1,0:T(8,128)(2,1)S(1)}, u32[]{:S(2)}, u32[]{:S(2)}) collective-permute-start(bf16[2,256,256]{2,1,0:T(8,128)(2,1)S(1)} %get-tuple-element.26.home0), channel_id=1, source_target_pairs={{2,26},{3,27},{4,28},{5,29},{6,30},{7,31},{12,20},{13,21},{14,22},... | collective-permute-start | bytes 786440 | tf_op jit(solution)/shard_map/ppermute | solution.py:84
  64.3 9.4 %collective-permute-start.18 = (bf16[2,256,256]{2,1,0:T(8,128)(2,1)S(1)}, bf16[2,256,256]{2,1,0:T(8,128)(2,1)S(1)}, u32[]{:S(2)}, u32[]{:S(2)}) collective-permute-start(bf16[2,256,256]{2,1,0:T(8,128)(2,1)S(1)} %shard_map.63.far1), channel_id=1, source_target_pairs={{0,8},{8,0},{16,24},{24,16},{1,9},{9,1},{17,25},{25,17},{2,10},{10... | collective-permute-start | bytes 786440 | tf_op jit(solution)/shard_map/ppermute | solution.py:28
  66.6 12.1 %collective-permute-start.16 = (bf16[2,256,256]{2,1,0:T(8,128)(2,1)S(1)}, bf16[2,256,256]{2,1,0:T(8,128)(2,1)S(1)}, u32[]{:S(2)}, u32[]{:S(2)}) collective-permute-start(bf16[2,256,256]{2,1,0:T(8,128)(2,1)S(1)} %shard_map.62.far0), channel_id=1, source_target_pairs={{0,8},{8,0},{16,24},{24,16},{1,9},{9,1},{17,25},{25,17},{2,10},{10... | collective-permute-start | bytes 786440 | tf_op jit(solution)/shard_map/ppermute | solution.py:28
  74.7 7.2 %collective-permute-start.19 = (bf16[2,256,256]{2,1,0:T(8,128)(2,1)S(1)}, bf16[2,256,256]{2,1,0:T(8,128)(2,1)S(1)}, u32[]{:S(2)}, u32[]{:S(2)}) collective-permute-start(bf16[2,256,256]{2,1,0:T(8,128)(2,1)S(1)} %get-tuple-element.33), channel_id=1, source_target_pairs={{0,1},{1,0},{2,3},{3,2},{4,5},{5,4},{6,7},{7,6},{8,9},{9,8},{10,11... | collective-permute-start | bytes 786440 | tf_op jit(solution)/shard_map/ppermute | solution.py:28
  79.7 7.8 %collective-permute-start.17 = (bf16[2,256,256]{2,1,0:T(8,128)(2,1)S(1)}, bf16[2,256,256]{2,1,0:T(8,128)(2,1)S(1)}, u32[]{:S(2)}, u32[]{:S(2)}) collective-permute-start(bf16[2,256,256]{2,1,0:T(8,128)(2,1)S(1)} %get-tuple-element.31), channel_id=1, source_target_pairs={{0,1},{1,0},{2,3},{3,2},{4,5},{5,4},{6,7},{7,6},{8,9},{9,8},{10,11... | collective-permute-start | bytes 786440 | tf_op jit(solution)/shard_map/ppermute | solution.py:28

commit v2 on v1

--- a/solution.py
+++ b/solution.py
@@ -149,7 +149,7 @@
 def home_kernel(own, direct0, direct1, hand0, hand1, elem, home, home0, home1, keep, give):
     a, b, half = (lax.axis_index(axis) for axis in AXES)
     lower = a >= b
-    relayed = (a == 1) & (b == 3)
+    relayed = (a == 0) & (b == 3)
     rows = own.shape[1]
 
     @pl.when(lower)
@@ -184,13 +184,10 @@
     return (a >= b) & ((b >= 2) | (a < 2))
 
 
-def pick_kernel(part, early, late, out):
-    rows = out.shape[2]
-    was_ready = ready_far(lax.axis_index("src") ^ 3, lax.axis_index("snk"))
-
+def pick(was_ready, early, late, out):
     @pl.when(was_ready)
     def _():
-        out[...] = early[:, :, part * rows : (part + 1) * rows]
+        out[...] = early[...]
 
     @pl.when(jnp.logical_not(was_ready))
     def _():
@@ -210,47 +207,47 @@
     return real, imag
 
 
-def early_kernel(ins, left0, left1, left2, left3, home0, home1, near_early, near, far0, far1, acc, last, chosen, beside):
+def choose(lefts, step, out):
+    k = lax.axis_index("src") ^ lax.axis_index("snk") ^ step
+    for index, left in enumerate(lefts):
+
+        @pl.when(k == index)
+        def _():
+            out[...] = left[...]
+
+
+def early_kernel(
+    ins, left0, left1, left2, left3, home0, home1, far_early, far0, far1, acc, left_near, left_last, chosen, block
+):
     a, b = lax.axis_index("src"), lax.axis_index("snk")
-    near_ready = ready(a ^ 1, b)
+    lefts = (left0, left1, left2, left3)
     rows = home0.shape[2]
-
-    def choose(k, out):
-        for index, left in enumerate((left0, left1, left2, left3)):
-
-            @pl.when(k == index)
-            def _():
-                out[...] = left[...]
-
-    @pl.when(near_ready)
-    def _():
-        beside[...] = near_early[...]
-
-    @pl.when(jnp.logical_not(near_ready))
-    def _():
-        beside[...] = near[...]
-
-    for step in (0, 1, 3):
-        choose(a ^ step ^ b, chosen)
+    for step in (0, 3):
+        choose(lefts, step, chosen)
         count = times(ins, a ^ step)
         for part in range(2):
             columns = slice(part * rows, (part + 1) * rows)
-            right = {0: (home0, home1)[part], 1: beside.at[:, :, columns], 3: (far0, far1)[part]}[step]
-            real, imag = product(count, chosen, right)
-            if step:
-                real = acc[0, :, columns] + real
-                imag = acc[1, :, columns] + imag
-            acc[0, :, columns] = real
-            acc[1, :, columns] = imag
-    choose(a ^ 2 ^ b, last)
-
-
-def late_kernel(part, ins, acc, last, block, mine, give):
+            if step == 0:
+                acc[0, :, columns], acc[1, :, columns] = product(count, chosen, (home0, home1)[part])
+            else:
+                pick(ready_far(a ^ 3, b), far_early.at[:, :, columns], (far0, far1)[part], block)
+                real, imag = product(count, chosen, block)
+                acc[0, :, columns] += real
+                acc[1, :, columns] += imag
+    choose(lefts, 1, left_near)
+    choose(lefts, 2, left_last)
+
+
+def late_kernel(part, ins, acc, left_near, left_last, near_early, near, skip, late, mine, give, block):
     rows = mine.shape[1]
     columns = slice(part * rows, (part + 1) * rows)
-    real, imag = product(times(ins, lax.axis_index("src") ^ 2), last, block)
-    for index, value in ((0, real), (1, imag)):
-        total = acc[index, :, columns] + value
+    a, b = lax.axis_index("src"), lax.axis_index("snk")
+    pick(ready(a ^ 1, b), near_early.at[:, :, columns], near.at[:, :, columns], block)
+    first = product(times(ins, a ^ 1), left_near, block)
+    pick(ready_far(a ^ 2, b), skip.at[:, :, columns], late, block)
+    second = product(times(ins, a ^ 2), left_last, block)
+    for index in range(2):
+        total = acc[index, :, columns] + first[index] + second[index]
         mine[index] = total[:rows]
         give[index] = total[rows:].astype(jnp.bfloat16)
 
@@ -277,16 +274,17 @@
     shifts = range(lax.axis_size("sub"))
 
     def relayed(b, a):
-        return (b, a) == (3, 1)
+        return (b, a) == (3, 0)
 
     pieces, own = mirror_pieces(own, spin_signs)
-    relay = [send(pieces[k], [(place(3, 1, h), place(3, 3, (h + k) % 2)) for h in shifts]) for k in shifts]
+    relay = [send(pieces[k], [(place(3, 0, h), place(3, 2, (h + k) % 2)) for h in shifts]) for k in shifts]
     direct = [send(pieces[k], mirror_pairs(k, lambda b, a: not relayed(b, a))) for k in shifts]
-    handed = [send(relay[k], [(place(3, 3, h), place(1, 3, h)) for h in shifts]) for k in shifts]
+    handed = [send(relay[k], [(place(3, 2, h), place(0, 3, h)) for h in shifts]) for k in shifts]
     elemental = local_call(stage_kernel, jax.ShapeDtypeStruct(elemental.shape, elemental.dtype), (elemental,))
     own, elemental = lax.optimization_barrier((own, elemental))
+    skip_early = send(own, along_z(2, ready_far))
+    far_early = send(own, along_z(3, ready_far))
     near_early = send(own, along_z(1, ready))
-    far_early = send(own, along_z(3, ready_far))
 
     piece = jax.ShapeDtypeStruct((2, rows, rows), own.dtype)
     tile = jax.ShapeDtypeStruct(own.shape, own.dtype)
@@ -298,27 +296,25 @@
     )
     far_late = [send(value, along_z(3, lambda a, b: not ready_far(a, b))) for value in (home0, home1)]
     near = send(full_half, along_z(1, lambda a, b: not ready(a, b)))
-    far = [
-        local_call(lambda *refs, part=part: pick_kernel(part, *refs), piece, (far_early, far_late[part]))
-        for part in parts
-    ]
-    late = [swap(far[part], "src", 1) for part in parts]
+    late = [send(far_late[part], along_z(1, lambda a, b: not ready_far(a ^ 3, b))) for part in parts]
     left = left_panel(keep, give)
-    acc, last = local_call(
+    panel = jax.ShapeDtypeStruct((2, 2 * rows, rows), own.dtype)
+    acc, *lefts = local_call(
         early_kernel,
-        [jax.ShapeDtypeStruct((2, 2 * rows, width), jnp.float32), jax.ShapeDtypeStruct((2, 2 * rows, rows), own.dtype)],
-        (insertions, *left, home0, home1, near_early, near, *far),
+        [jax.ShapeDtypeStruct((2, 2 * rows, width), jnp.float32), panel, panel],
+        (insertions, *left, home0, home1, far_early, *far_late),
         tables=1,
-        scratch=[pltpu.VMEM((2, 2 * rows, rows), own.dtype), pltpu.VMEM(own.shape, own.dtype)],
-        flops=3 * 16 * rows * rows * width,
+        scratch=[pltpu.VMEM(panel.shape, panel.dtype), pltpu.VMEM(piece.shape, piece.dtype)],
+        flops=2 * 16 * rows * rows * width,
     )
     ends = []
     for part in parts:
         mine, given = local_call(
             lambda *refs, part=part: late_kernel(part, *refs),
             [jax.ShapeDtypeStruct((2, rows, rows), jnp.float32), piece],
-            (insertions, acc, last, late[part]),
+            (insertions, acc, *lefts, near_early, near, skip_early, late[part]),
             tables=1,
+            scratch=[pltpu.VMEM((2, rows, rows), own.dtype)],
             flops=16 * rows * rows * rows,
         )
         ends += [mine, swap(given, "sub", 1)]

time: 88.9 us -> 98.6 us (1.11)
  starting transfers between devices: 41.3 us -> 57.4 us
  waiting for transfers between devices: 35 us -> 28.1 us
    ppermute x11 -> x14, starting transfers between devices: 10.5 us -> 30 us  [send(): return lax.ppermute(value, AXES, pairs)]
    ppermute x8 -> x6, waiting for transfers between devices: 15.1 us -> 7.47 us  [swap(): return lax.ppermute(value, axis, [(i, i ^ mask) for i in range(size)])]
    ppermute x8 -> x6, starting transfers between devices: 30.7 us -> 26.4 us  [swap(): return lax.ppermute(value, axis, [(i, i ^ mask) for i in range(size)])]
    ppermute x1, waiting for transfers between devices: 2.49 us -> 3.57 us  [left_panel(): give_x = lax.ppermute(give, ('snk', 'sub'), across)]
    pallas_call x9 -> x7, Pallas kernels: 8.34 us -> 8.68 us  [local_call(): pl.pallas_call(kernel, out_shape=out_shape, in_specs=[SMEM] * tables + [V...]
    ppermute x11 -> x14, waiting for transfers between devices: 17.4 us -> 17.1 us  [send(): return lax.ppermute(value, AXES, pairs)]
    unnamed x10 -> x12, local copies, waits for them, and re-layouts: 2.95 us -> 2.96 us
  transfers between devices with their start and end apart: 20 -> 21, of which waited for: 9 -> 7; matrix products, arithmetic and copies ran while one was open for 0% -> 0% of each run, Pallas kernels for 6% -> 6%
where the time goes in v2:
time: 98.6 us; the launch traced here: 98.1 us
  starting transfers between devices  57.4 us (58%)
  waiting for transfers between devices  28.1 us (28%)
  Pallas kernels  8.68 us (9%)
  local copies, waits for them, and re-layouts  2.99 us (3%)
    ppermute x14, starting transfers between devices, send(): return lax.ppermute(value, AXES, pairs)  30 us
    ppermute x6, starting transfers between devices, swap(): return lax.ppermute(value, axis, [(i, i ^ mask) for i in range(size)])  26.4 us
    ppermute x14, waiting for transfers between devices, send(): return lax.ppermute(value, AXES, pairs)  17.1 us
    pallas_call x7, Pallas kernels, local_call(): pl.pallas_call(kernel, out_shape=out_shape, in_specs=[SMEM] * tables + [V...  8.68 us
    ppermute x6, waiting for transfers between devices, swap(): return lax.ppermute(value, axis, [(i, i ^ mask) for i in range(size)])  7.47 us
    ppermute x1, waiting for transfers between devices, left_panel(): give_x = lax.ppermute(give, ('snk', 'sub'), across)  3.57 us
    unnamed x12, local copies, waits for them, and re-layouts  2.96 us
  transfers between devices with their start and end apart: 21, of which 7 were waited for; matrix products, arithmetic and copies ran while one was open for 0% of the time, Pallas kernels for 6%

profile of v2, /device:TPU:0, one launch (start us, length us, event | category | flops | bytes accessed | tf_op | source)
XLA Modules:
  0.0 98.1 jit_solution(1343802233177760591)
XLA Ops:
  0.6 1.0 %copy-done.1 = bf16[1,1,2,256,512]{4,3,2,1,0:T(8,128)(2,1)S(1)} copy-done((bf16[1,1,2,256,512]{4,3,2,1,0:T(8,128)(2,1)S(1)}, bf16[1,1,2,256,512]{4,3,2,1,0:T(8,128)(2,1)}, u32[]{:S(2)}) %copy-start.1) | copy-done | bytes 524312
  1.7 0.7 copy-done.3
  2.3 0.8 shard_map.59
  3.1 0.7 collective-permute-start.2
  3.8 0.7 collective-permute-start.4
  4.5 0.7 collective-permute-start
  5.2 0.7 collective-permute-start.1
  5.9 0.7 collective-permute-start.3
  6.5 0.0 collective-permute-done.4
  6.6 0.7 collective-permute-start.5
  7.2 0.0 copy-start
  7.2 1.2 %copy-done = bf16[2,512,512]{2,1,0:T(8,128)(2,1)S(1)} copy-done((bf16[2,512,512]{2,1,0:T(8,128)(2,1)S(1)}, bf16[2,512,512]{2,1,0:T(8,128)(2,1)}, u32[]{:S(2)}) %copy-start) | copy-done | bytes 1048600
  8.5 0.1 shard_map.60.elem
  8.5 0.0 copy-start.2
  8.6 0.0 collective-permute-done.1.direct1
  8.6 0.0 collective-permute-done.3.hand0
  8.6 1.4 %shard_map.61 = (bf16[2,256,512]{2,1,0:T(8,128)(2,1)}, bf16[2,256,256]{2,1,0:T(8,128)(2,1)S(1)}, bf16[2,256,256]{2,1,0:T(8,128)(2,1)S(1)}, bf16[2,256,256]{2,1,0:T(8,128)(2,1)S(1)}, bf16[2,256,256]{2,1,0:T(8,128)(2,1)S(1)}) custom-call(bf16[2,256,512]{2,1,0:T(8,128)(2,1)S(1)} %get-tuple-element.20.own, ...), custom_call_target="tpu_custom_call" | custom-call | flops 536870912 | bytes 4194304 | tf_op jit(solution)/shard_map/pallas_call | solution.py:38
  9.9 3.0 %collective-permute-start.6 = (bf16[2,256,256]{2,1,0:T(8,128)(2,1)S(1)}, bf16[2,256,256]{2,1,0:T(8,128)(2,1)S(1)}, u32[]{:S(2)}, u32[]{:S(2)}) collective-permute-start(bf16[2,256,256]{2,1,0:T(8,128)(2,1)S(1)} %get-tuple-element.26), channel_id=1, source_target_pairs={{0,1},{1,0},{2,3},{3,2},{4,5},{5,4},{6,7},{7,6},{8,9},{9,8},{10,11... | collective-permute-start | bytes 786440 | tf_op jit(solution)/shard_map/ppermute | solution.py:28
  12.9 21.1 %collective-permute-start.8 = (bf16[2,256,256]{2,1,0:T(8,128)(2,1)S(1)}, bf16[2,256,256]{2,1,0:T(8,128)(2,1)S(1)}, u32[]{:S(2)}, u32[]{:S(2)}) collective-permute-start(bf16[2,256,256]{2,1,0:T(8,128)(2,1)S(1)} %get-tuple-element.25), channel_id=1, source_target_pairs={{0,4},{2,6},{4,0},{6,2},{1,5},{3,7},{5,1},{7,3},{8,12},{10,14},{12... | collective-permute-start | bytes 786440 | tf_op jit(solution)/shard_map/ppermute | solution.py:28
  34.0 1.3 %collective-permute-start.11 = (bf16[2,256,512]{2,1,0:T(8,128)(2,1)S(1)}, bf16[2,256,512]{2,1,0:T(8,128)(2,1)S(1)}, u32[]{:S(2)}, u32[]{:S(2)}) collective-permute-start(bf16[2,256,512]{2,1,0:T(8,128)(2,1)S(1)} %get-tuple-element.20.own), channel_id=1, source_target_pairs={{0,24},{1,25},{8,16},{9,17},{10,18},{11,19},{20,12},{21,13},{28,4}... | collective-permute-start | bytes 1572872 | tf_op jit(solution)/shard_map/ppermute | solution.py:84
  35.3 1.0 %collective-permute-start.9 = (bf16[2,256,256]{2,1,0:T(8,128)(2,1)S(1)}, bf16[2,256,256]{2,1,0:T(8,128)(2,1)S(1)}, u32[]{:S(2)}, u32[]{:S(2)}) collective-permute-start(bf16[2,256,256]{2,1,0:T(8,128)(2,1)S(1)} %get-tuple-element.26), channel_id=1, source_target_pairs={{0,5},{1,4},{2,7},{3,6},{4,1},{5,0},{6,3},{7,2},{8,13},{9,12},{10,... | collective-permute-start | bytes 786440 | tf_op jit(solution)/shard_map/ppermute | solution.py:133
  36.4 1.3 %collective-permute-start.12 = (bf16[2,256,256]{2,1,0:T(8,128)(2,1)S(1)}, bf16[2,256,256]{2,1,0:T(8,128)(2,1)S(1)}, u32[]{:S(2)}, u32[]{:S(2)}) collective-permute-start(bf16[2,256,256]{2,1,0:T(8,128)(2,1)S(1)} %get-tuple-element.27.home0), channel_id=1, source_target_pairs={{2,26},{3,27},{4,28},{5,29},{6,30},{7,31},{12,20},{13,21},{14,22},... | collective-permute-start | bytes 786440 | tf_op jit(solution)/shard_map/ppermute | solution.py:84
  37.7 1.3 %collective-permute-start.13 = (bf16[2,256,256]{2,1,0:T(8,128)(2,1)S(1)}, bf16[2,256,256]{2,1,0:T(8,128)(2,1)S(1)}, u32[]{:S(2)}, u32[]{:S(2)}) collective-permute-start(bf16[2,256,256]{2,1,0:T(8,128)(2,1)S(1)} %get-tuple-element.28.home1), channel_id=1, source_target_pairs={{2,26},{3,27},{4,28},{5,29},{6,30},{7,31},{12,20},{13,21},{14,22},... | collective-permute-start | bytes 786440 | tf_op jit(solution)/shard_map/ppermute | solution.py:84
  39.0 0.0 collective-permute-done.8
  39.0 0.1 collective-permute-start.7
  39.1 3.6 %collective-permute-done.9 = bf16[2,256,256]{2,1,0:T(8,128)(2,1)S(1)} collective-permute-done((bf16[2,256,256]{2,1,0:T(8,128)(2,1)S(1)}, bf16[2,256,256]{2,1,0:T(8,128)(2,1)S(1)}, u32[]{:S(2)}, u32[]{:S(2)}) %collective-permute-start.9) | collective-permute-done | bytes 262176 | tf_op jit(solution)/shard_map/ppermute | solution.py:133
  42.7 0.1 collective-permute-start.10
  42.8 3.9 %collective-permute-done.11.far_early = bf16[2,256,512]{2,1,0:T(8,128)(2,1)S(1)} collective-permute-done((bf16[2,256,512]{2,1,0:T(8,128)(2,1)S(1)}, bf16[2,256,512]{2,1,0:T(8,128)(2,1)S(1)}, u32[]{:S(2)}, u32[]{:S(2)}) %collective-permute-start.11) | collective-permute-done | bytes 524320 | tf_op jit(solution)/shard_map/ppermute | solution.py:84
  46.7 11.7 %collective-permute-start.14 = (bf16[2,256,512]{2,1,0:T(8,128)(2,1)S(1)}, bf16[2,256,512]{2,1,0:T(8,128)(2,1)S(1)}, u32[]{:S(2)}, u32[]{:S(2)}) collective-permute-start(bf16[2,256,512]{2,1,0:T(8,128)(2,1)S(1)} %get-tuple-element.20.own), channel_id=1, source_target_pairs={{0,8},{1,9},{8,0},{9,1},{10,2},{11,3},{16,24},{17,25},{18,26},{19,... | collective-permute-start | bytes 1572872 | tf_op jit(solution)/shard_map/ppermute | solution.py:84
  58.4 0.0 collective-permute-done.12.far0
  58.4 3.9 %collective-permute-start.16 = (bf16[2,256,512]{2,1,0:T(8,128)(2,1)S(1)}, bf16[2,256,512]{2,1,0:T(8,128)(2,1)S(1)}, u32[]{:S(2)}, u32[]{:S(2)}) collective-permute-start(bf16[2,256,512]{2,1,0:T(8,128)(2,1)S(1)} %get-tuple-element.20.own), channel_id=1, source_target_pairs={{0,16},{1,17},{8,24},{9,25},{10,26},{11,27},{20,4},{21,5},{28,12},... | collective-permute-start | bytes 1572872 | tf_op jit(solution)/shard_map/ppermute | solution.py:84
  62.3 0.0 collective-permute-done.13.far1
  62.3 0.7 collective-permute-start.15
  63.0 0.0 collective-permute-done.7.left1
  63.0 3.9 %collective-permute-start.17 = (bf16[2,256,256]{2,1,0:T(8,128)(2,1)S(1)}, bf16[2,256,256]{2,1,0:T(8,128)(2,1)S(1)}, u32[]{:S(2)}, u32[]{:S(2)}) collective-permute-start(bf16[2,256,256]{2,1,0:T(8,128)(2,1)S(1)} %collective-permute-done.12.far0), channel_id=1, source_target_pairs={{0,8},{1,9},{2,10},{3,11},{8,0},{9,1},{10,2},{11,3},{14,6},{15,7},... | collective-permute-start | bytes 786440 | tf_op jit(solution)/shard_map/ppermute | solution.py:84
  66.9 0.0 collective-permute-done.10.left3
  66.9 1.9 %collective-permute-start.19 = (bf16[2,256,256]{2,1,0:T(8,128)(2,1)S(1)}, bf16[2,256,256]{2,1,0:T(8,128)(2,1)S(1)}, u32[]{:S(2)}, u32[]{:S(2)}) collective-permute-start(bf16[2,256,256]{2,1,0:T(8,128)(2,1)S(1)} %collective-permute-done.13.far1), channel_id=1, source_target_pairs={{0,8},{1,9},{2,10},{3,11},{8,0},{9,1},{10,2},{11,3},{14,6},{15,7},... | collective-permute-start | bytes 786440 | tf_op jit(solution)/shard_map/ppermute | solution.py:84
  68.9 2.4 %shard_map.62 = (f32[2,512,512]{2,1,0:T(8,128)S(1)}, bf16[2,512,256]{2,1,0:T(8,128)(2,1)S(1)}, bf16[2,512,256]{2,1,0:T(8,128)(2,1)S(1)}) custom-call(s32[4]{0:T(128)S(1)} %copy-done.2, bf16[2,512,256]{2,1,0:T(8,128)(2,1)S(1)} %constant_dynamic-update-slice_fusion.left0, bf16[2,512,256]{2,1,0:T(8,128)(2,1)S(1)} %collective-permute-done.7.left1, ...), custom_call_target="tpu_custom_call" | custom-call | flops 1073741824 | bytes 6815760 | tf_op jit(solution)/shard_map/pallas_call | solution.py:38
  71.3 6.6 %collective-permute-done.16.refs_6_ = bf16[2,256,512]{2,1,0:T(8,128)(2,1)S(1)} collective-permute-done((bf16[2,256,512]{2,1,0:T(8,128)(2,1)S(1)}, bf16[2,256,512]{2,1,0:T(8,128)(2,1)S(1)}, u32[]{:S(2)}, u32[]{:S(2)}) %collective-permute-start.16) | collective-permute-done | bytes 524320 | tf_op jit(solution)/shard_map/ppermute | solution.py:84
  77.9 5.6 %collective-permute-done.17.refs_7_ = bf16[2,256,256]{2,1,0:T(8,128)(2,1)S(1)} collective-permute-done((bf16[2,256,256]{2,1,0:T(8,128)(2,1)S(1)}, bf16[2,256,256]{2,1,0:T(8,128)(2,1)S(1)}, u32[]{:S(2)}, u32[]{:S(2)}) %collective-permute-start.17) | collective-permute-done | bytes 262176 | tf_op jit(solution)/shard_map/ppermute | solution.py:84
  83.5 1.5 %shard_map.63 = (f32[2,256,256]{2,1,0:T(8,128)S(1)}, bf16[2,256,256]{2,1,0:T(8,128)(2,1)S(1)}) custom-call(s32[4]{0:T(128)S(1)} %copy-done.2, f32[2,512,512]{2,1,0:T(8,128)S(1)} %get-tuple-element.29.refs_1_, bf16[2,512,256]{2,1,0:T(8,128)(2,1)S(1)} %get-tuple-element.30.refs_2_, bf16[2,512,256]{2,1,0:T(8,128)(2,1)S(1)} %get-tuple-element.31.refs_3_, ...), custom_call_target="tpu_custom_call" | custom-call | flops 268435456 | bytes 5767184 | tf_op jit(solution)/shard_map/pallas_call | solution.py:38
  85.0 1.6 %collective-permute-start.18 = (bf16[2,256,256]{2,1,0:T(8,128)(2,1)S(1)}, bf16[2,256,256]{2,1,0:T(8,128)(2,1)S(1)}, u32[]{:S(2)}, u32[]{:S(2)}) collective-permute-start(bf16[2,256,256]{2,1,0:T(8,128)(2,1)S(1)} %get-tuple-element.33), channel_id=1, source_target_pairs={{0,1},{1,0},{2,3},{3,2},{4,5},{5,4},{6,7},{7,6},{8,9},{9,8},{10,11... | collective-permute-start | bytes 786440 | tf_op jit(solution)/shard_map/ppermute | solution.py:28
  86.6 0.9 collective-permute-done.19.refs_7_
  87.5 1.5 %shard_map.64 = (f32[2,256,256]{2,1,0:T(8,128)S(1)}, bf16[2,256,256]{2,1,0:T(8,128)(2,1)S(1)}) custom-call(s32[4]{0:T(128)S(1)} %copy-done.2, f32[2,512,512]{2,1,0:T(8,128)S(1)} %get-tuple-element.29.refs_1_, bf16[2,512,256]{2,1,0:T(8,128)(2,1)S(1)} %get-tuple-element.30.refs_2_, bf16[2,512,256]{2,1,0:T(8,128)(2,1)S(1)} %get-tuple-element.31.refs_3_, ...), custom_call_target="tpu_custom_call" | custom-call | flops 268435456 | bytes 5767184 | tf_op jit(solution)/shard_map/pallas_call | solution.py:38
  89.0 0.6 collective-permute-start.20
  89.6 3.4 %collective-permute-done.18.given0 = bf16[2,256,256]{2,1,0:T(8,128)(2,1)S(1)} collective-permute-done((bf16[2,256,256]{2,1,0:T(8,128)(2,1)S(1)}, bf16[2,256,256]{2,1,0:T(8,128)(2,1)S(1)}, u32[]{:S(2)}, u32[]{:S(2)}) %collective-permute-start.18) | collective-permute-done | bytes 262176 | tf_op jit(solution)/shard_map/ppermute | solution.py:28
  93.0 4.1 %collective-permute-done.20.given1 = bf16[2,256,256]{2,1,0:T(8,128)(2,1)S(1)} collective-permute-done((bf16[2,256,256]{2,1,0:T(8,128)(2,1)S(1)}, bf16[2,256,256]{2,1,0:T(8,128)(2,1)S(1)}, u32[]{:S(2)}, u32[]{:S(2)}) %collective-permute-start.20) | collective-permute-done | bytes 262176 | tf_op jit(solution)/shard_map/ppermute | solution.py:28
  97.1 1.1 %shard_map.65 = f32[2,256,512]{2,1,0:T(8,128)} custom-call(f32[2,256,256]{2,1,0:T(8,128)S(1)} %get-tuple-element.32.mine0, bf16[2,256,256]{2,1,0:T(8,128)(2,1)S(1)} %collective-permute-done.18.given0, f32[2,256,256]{2,1,0:T(8,128)S(1)} %get-tuple-element.34.mine1, bf16[2,256,256]{2,1,0:T(8,128)(2,1)S(1)} %collective-permute-done.20.given1), custom_call_target="tpu_custom_call" | custom-call | bytes 2621440 | tf_op jit(solution)/shard_map/pallas_call | solution.py:38
  (15 shorter events, 0.1 us)
Async XLA Ops:
  0.6 1.0 %copy-start.1 = (bf16[1,1,2,256,512]{4,3,2,1,0:T(8,128)(2,1)S(1)}, bf16[1,1,2,256,512]{4,3,2,1,0:T(8,128)(2,1)}, u32[]{:S(2)}) copy-start(bf16[1,1,2,256,512]{4,3,2,1,0:T(8,128)(2,1)} %param.4) | copy-start | bytes 1572868
  1.7 0.7 copy-start.3
  3.1 2.7 %collective-permute-start.2 = (bf16[2,256,256]{2,1,0:T(8,128)(2,1)S(1)}, bf16[2,256,256]{2,1,0:T(8,128)(2,1)S(1)}, u32[]{:S(2)}, u32[]{:S(2)}) collective-permute-start(bf16[2,256,256]{2,1,0:T(8,128)(2,1)S(1)} %get-tuple-element.21), channel_id=1, source_target_pairs={{24,28},{25,29}} | collective-permute-start | bytes 786440 | tf_op jit(solution)/shard_map/ppermute | solution.py:84
  3.8 2.8 %collective-permute-start.4 = (bf16[2,256,256]{2,1,0:T(8,128)(2,1)S(1)}, bf16[2,256,256]{2,1,0:T(8,128)(2,1)S(1)}, u32[]{:S(2)}, u32[]{:S(2)}) collective-permute-start(bf16[2,256,256]{2,1,0:T(8,128)(2,1)S(1)} %get-tuple-element.22), channel_id=1, source_target_pairs={{24,29},{25,28}} | collective-permute-start | bytes 786440 | tf_op jit(solution)/shard_map/ppermute | solution.py:84
  4.5 4.1 %collective-permute-start = (bf16[2,256,256]{2,1,0:T(8,128)(2,1)S(1)}, bf16[2,256,256]{2,1,0:T(8,128)(2,1)S(1)}, u32[]{:S(2)}, u32[]{:S(2)}) collective-permute-start(bf16[2,256,256]{2,1,0:T(8,128)(2,1)S(1)} %get-tuple-element.21), channel_id=1, source_target_pairs={{8,2},{9,3},{16,4},{17,5},{18,12},{19,13},{26,14},{27,15},{28,22},... | collective-permute-start | bytes 786440 | tf_op jit(solution)/shard_map/ppermute | solution.py:84
  5.2 3.4 %collective-permute-start.1 = (bf16[2,256,256]{2,1,0:T(8,128)(2,1)S(1)}, bf16[2,256,256]{2,1,0:T(8,128)(2,1)S(1)}, u32[]{:S(2)}, u32[]{:S(2)}) collective-permute-start(bf16[2,256,256]{2,1,0:T(8,128)(2,1)S(1)} %get-tuple-element.22), channel_id=1, source_target_pairs={{8,3},{9,2},{16,5},{17,4},{18,13},{19,12},{26,15},{27,14},{28,23},... | collective-permute-start | bytes 786440 | tf_op jit(solution)/shard_map/ppermute | solution.py:84
  5.9 2.7 %collective-permute-start.3 = (bf16[2,256,256]{2,1,0:T(8,128)(2,1)S(1)}, bf16[2,256,256]{2,1,0:T(8,128)(2,1)S(1)}, u32[]{:S(2)}, u32[]{:S(2)}) collective-permute-start(bf16[2,256,256]{2,1,0:T(8,128)(2,1)S(1)} %collective-permute-done.2), channel_id=1, source_target_pairs={{28,6},{29,7}} | collective-permute-start | bytes 786440 | tf_op jit(solution)/shard_map/ppermute | solution.py:84
  6.6 2.0 %collective-permute-start.5 = (bf16[2,256,256]{2,1,0:T(8,128)(2,1)S(1)}, bf16[2,256,256]{2,1,0:T(8,128)(2,1)S(1)}, u32[]{:S(2)}, u32[]{:S(2)}) collective-permute-start(bf16[2,256,256]{2,1,0:T(8,128)(2,1)S(1)} %collective-permute-done.4), channel_id=1, source_target_pairs={{28,6},{29,7}} | collective-permute-start | bytes 786440 | tf_op jit(solution)/shard_map/ppermute | solution.py:84
  7.2 1.2 %copy-start = (bf16[2,512,512]{2,1,0:T(8,128)(2,1)S(1)}, bf16[2,512,512]{2,1,0:T(8,128)(2,1)}, u32[]{:S(2)}) copy-start(bf16[2,512,512]{2,1,0:T(8,128)(2,1)} %value.1) | copy-start | bytes 3145732
  8.5 60.3 %copy-start.2 = (s32[4]{0:T(128)S(1)}, s32[4]{0:T(128)}, u32[]{:S(2)}) copy-start(s32[4]{0:T(128)} %refs_0_.3) | copy-start | bytes 52
  9.9 52.3 %copy-start.4 = (bf16[2,256,512]{2,1,0:T(8,128)(2,1)S(1)}, bf16[2,256,512]{2,1,0:T(8,128)(2,1)}, u32[]{:S(2)}) copy-start(bf16[2,256,512]{2,1,0:T(8,128)(2,1)} %get-tuple-element.24) | copy-start | bytes 1572868
  9.9 27.7 %collective-permute-start.6 = (bf16[2,256,256]{2,1,0:T(8,128)(2,1)S(1)}, bf16[2,256,256]{2,1,0:T(8,128)(2,1)S(1)}, u32[]{:S(2)}, u32[]{:S(2)}) collective-permute-start(bf16[2,256,256]{2,1,0:T(8,128)(2,1)S(1)} %get-tuple-element.26), channel_id=1, source_target_pairs={{0,1},{1,0},{2,3},{3,2},{4,5},{5,4},{6,7},{7,6},{8,9},{9,8},{10,11... | collective-permute-start | bytes 786440 | tf_op jit(solution)/shard_map/ppermute | solution.py:28
  12.9 26.1 %collective-permute-start.8 = (bf16[2,256,256]{2,1,0:T(8,128)(2,1)S(1)}, bf16[2,256,256]{2,1,0:T(8,128)(2,1)S(1)}, u32[]{:S(2)}, u32[]{:S(2)}) collective-permute-start(bf16[2,256,256]{2,1,0:T(8,128)(2,1)S(1)} %get-tuple-element.25), channel_id=1, source_target_pairs={{0,4},{2,6},{4,0},{6,2},{1,5},{3,7},{5,1},{7,3},{8,12},{10,14},{12... | collective-permute-start | bytes 786440 | tf_op jit(solution)/shard_map/ppermute | solution.py:28
  34.0 12.7 %collective-permute-start.11 = (bf16[2,256,512]{2,1,0:T(8,128)(2,1)S(1)}, bf16[2,256,512]{2,1,0:T(8,128)(2,1)S(1)}, u32[]{:S(2)}, u32[]{:S(2)}) collective-permute-start(bf16[2,256,512]{2,1,0:T(8,128)(2,1)S(1)} %get-tuple-element.20.own), channel_id=1, source_target_pairs={{0,24},{1,25},{8,16},{9,17},{10,18},{11,19},{20,12},{21,13},{28,4}... | collective-permute-start | bytes 1572872 | tf_op jit(solution)/shard_map/ppermute | solution.py:84
  35.3 7.3 %collective-permute-start.9 = (bf16[2,256,256]{2,1,0:T(8,128)(2,1)S(1)}, bf16[2,256,256]{2,1,0:T(8,128)(2,1)S(1)}, u32[]{:S(2)}, u32[]{:S(2)}) collective-permute-start(bf16[2,256,256]{2,1,0:T(8,128)(2,1)S(1)} %get-tuple-element.26), channel_id=1, source_target_pairs={{0,5},{1,4},{2,7},{3,6},{4,1},{5,0},{6,3},{7,2},{8,13},{9,12},{10,... | collective-permute-start | bytes 786440 | tf_op jit(solution)/shard_map/ppermute | solution.py:133
  36.4 22.0 %collective-permute-start.12 = (bf16[2,256,256]{2,1,0:T(8,128)(2,1)S(1)}, bf16[2,256,256]{2,1,0:T(8,128)(2,1)S(1)}, u32[]{:S(2)}, u32[]{:S(2)}) collective-permute-start(bf16[2,256,256]{2,1,0:T(8,128)(2,1)S(1)} %get-tuple-element.27.home0), channel_id=1, source_target_pairs={{2,26},{3,27},{4,28},{5,29},{6,30},{7,31},{12,20},{13,21},{14,22},... | collective-permute-start | bytes 786440 | tf_op jit(solution)/shard_map/ppermute | solution.py:84
  37.7 24.6 %collective-permute-start.13 = (bf16[2,256,256]{2,1,0:T(8,128)(2,1)S(1)}, bf16[2,256,256]{2,1,0:T(8,128)(2,1)S(1)}, u32[]{:S(2)}, u32[]{:S(2)}) collective-permute-start(bf16[2,256,256]{2,1,0:T(8,128)(2,1)S(1)} %get-tuple-element.28.home1), channel_id=1, source_target_pairs={{2,26},{3,27},{4,28},{5,29},{6,30},{7,31},{12,20},{13,21},{14,22},... | collective-permute-start | bytes 786440 | tf_op jit(solution)/shard_map/ppermute | solution.py:84
  39.0 24.0 %collective-permute-start.7 = (bf16[2,512,256]{2,1,0:T(8,128)(2,1)S(1)}, bf16[2,512,256]{2,1,0:T(8,128)(2,1)S(1)}, u32[]{:S(2)}, u32[]{:S(2)}) collective-permute-start(bf16[2,512,256]{2,1,0:T(8,128)(2,1)S(1)} %constant_dynamic-update-slice_fusion.left0), channel_id=1, source_target_pairs={{0,2},{2,0},{4,6},{6,4},{1,3},{3,1},{5,7},{7,5},{8,10},{10,8},{12,... | collective-permute-start | bytes 1572872 | tf_op jit(solution)/shard_map/ppermute | solution.py:28
  42.7 24.2 %collective-permute-start.10 = (bf16[2,512,256]{2,1,0:T(8,128)(2,1)S(1)}, bf16[2,512,256]{2,1,0:T(8,128)(2,1)S(1)}, u32[]{:S(2)}, u32[]{:S(2)}) collective-permute-start(bf16[2,512,256]{2,1,0:T(8,128)(2,1)S(1)} %constant_dynamic-update-slice_fusion.2.left2), channel_id=1, source_target_pairs={{0,2},{2,0},{4,6},{6,4},{1,3},{3,1},{5,7},{7,5},{8,10},{10,8},{12,... | collective-permute-start | bytes 1572872 | tf_op jit(solution)/shard_map/ppermute | solution.py:28
  46.7 24.6 %collective-permute-start.14 = (bf16[2,256,512]{2,1,0:T(8,128)(2,1)S(1)}, bf16[2,256,512]{2,1,0:T(8,128)(2,1)S(1)}, u32[]{:S(2)}, u32[]{:S(2)}) collective-permute-start(bf16[2,256,512]{2,1,0:T(8,128)(2,1)S(1)} %get-tuple-element.20.own), channel_id=1, source_target_pairs={{0,8},{1,9},{8,0},{9,1},{10,2},{11,3},{16,24},{17,25},{18,26},{19,... | collective-permute-start | bytes 1572872 | tf_op jit(solution)/shard_map/ppermute | solution.py:84
  58.4 19.5 %collective-permute-start.16 = (bf16[2,256,512]{2,1,0:T(8,128)(2,1)S(1)}, bf16[2,256,512]{2,1,0:T(8,128)(2,1)S(1)}, u32[]{:S(2)}, u32[]{:S(2)}) collective-permute-start(bf16[2,256,512]{2,1,0:T(8,128)(2,1)S(1)} %get-tuple-element.20.own), channel_id=1, source_target_pairs={{0,16},{1,17},{8,24},{9,25},{10,26},{11,27},{20,4},{21,5},{28,12},... | collective-permute-start | bytes 1572872 | tf_op jit(solution)/shard_map/ppermute | solution.py:84
  62.3 15.6 %collective-permute-start.15 = (bf16[2,256,512]{2,1,0:T(8,128)(2,1)S(1)}, bf16[2,256,512]{2,1,0:T(8,128)(2,1)S(1)}, u32[]{:S(2)}, u32[]{:S(2)}) collective-permute-start(bf16[2,256,512]{2,1,0:T(8,128)(2,1)S(1)} %copy-done.4), channel_id=1, source_target_pairs={{2,10},{3,11},{4,12},{5,13},{6,14},{7,15},{12,4},{13,5},{14,6},{15... | collective-permute-start | bytes 1572872 | tf_op jit(solution)/shard_map/ppermute | solution.py:84
  63.0 20.5 %collective-permute-start.17 = (bf16[2,256,256]{2,1,0:T(8,128)(2,1)S(1)}, bf16[2,256,256]{2,1,0:T(8,128)(2,1)S(1)}, u32[]{:S(2)}, u32[]{:S(2)}) collective-permute-start(bf16[2,256,256]{2,1,0:T(8,128)(2,1)S(1)} %collective-permute-done.12.far0), channel_id=1, source_target_pairs={{0,8},{1,9},{2,10},{3,11},{8,0},{9,1},{10,2},{11,3},{14,6},{15,7},... | collective-permute-start | bytes 786440 | tf_op jit(solution)/shard_map/ppermute | solution.py:84
  66.9 20.6 %collective-permute-start.19 = (bf16[2,256,256]{2,1,0:T(8,128)(2,1)S(1)}, bf16[2,256,256]{2,1,0:T(8,128)(2,1)S(1)}, u32[]{:S(2)}, u32[]{:S(2)}) collective-permute-start(bf16[2,256,256]{2,1,0:T(8,128)(2,1)S(1)} %collective-permute-done.13.far1), channel_id=1, source_target_pairs={{0,8},{1,9},{2,10},{3,11},{8,0},{9,1},{10,2},{11,3},{14,6},{15,7},... | collective-permute-start | bytes 786440 | tf_op jit(solution)/shard_map/ppermute | solution.py:84
  85.0 8.0 %collective-permute-start.18 = (bf16[2,256,256]{2,1,0:T(8,128)(2,1)S(1)}, bf16[2,256,256]{2,1,0:T(8,128)(2,1)S(1)}, u32[]{:S(2)}, u32[]{:S(2)}) collective-permute-start(bf16[2,256,256]{2,1,0:T(8,128)(2,1)S(1)} %get-tuple-element.33), channel_id=1, source_target_pairs={{0,1},{1,0},{2,3},{3,2},{4,5},{5,4},{6,7},{7,6},{8,9},{9,8},{10,11... | collective-permute-start | bytes 786440 | tf_op jit(solution)/shard_map/ppermute | solution.py:28
  89.0 8.0 %collective-permute-start.20 = (bf16[2,256,256]{2,1,0:T(8,128)(2,1)S(1)}, bf16[2,256,256]{2,1,0:T(8,128)(2,1)S(1)}, u32[]{:S(2)}, u32[]{:S(2)}) collective-permute-start(bf16[2,256,256]{2,1,0:T(8,128)(2,1)S(1)} %get-tuple-element.35), channel_id=1, source_target_pairs={{0,1},{1,0},{2,3},{3,2},{4,5},{5,4},{6,7},{7,6},{8,9},{9,8},{10,11... | collective-permute-start | bytes 786440 | tf_op jit(solution)/shard_map/ppermute | solution.py:28

commit v3 on v2

--- a/solution.py
+++ b/solution.py
@@ -181,7 +181,7 @@
 
 
 def ready_far(a, b):
-    return (a >= b) & ((b >= 2) | (a < 2))
+    return (a >= b) & ((b >= 2) | (a == 1))
 
 
 def pick(was_ready, early, late, out):
@@ -238,13 +238,19 @@
     choose(lefts, 2, left_last)
 
 
-def late_kernel(part, ins, acc, left_near, left_last, near_early, near, skip, late, mine, give, block):
+def late_kernel(part, ins, acc, left_near, left_last, near_early, near, skip, hop, late, mine, give, block):
     rows = mine.shape[1]
     columns = slice(part * rows, (part + 1) * rows)
     a, b = lax.axis_index("src"), lax.axis_index("snk")
     pick(ready(a ^ 1, b), near_early.at[:, :, columns], near.at[:, :, columns], block)
     first = product(times(ins, a ^ 1), left_near, block)
-    pick(ready_far(a ^ 2, b), skip.at[:, :, columns], late, block)
+    hopped = (a == 1) & (b >= 2)
+    pick(ready_far(a ^ 2, b) & jnp.logical_not(hopped), skip.at[:, :, columns], late, block)
+
+    @pl.when(hopped)
+    def _():
+        block[...] = hop[:, :, columns]
+
     second = product(times(ins, a ^ 2), left_last, block)
     for index in range(2):
         total = acc[index, :, columns] + first[index] + second[index]
@@ -282,7 +288,7 @@
     handed = [send(relay[k], [(place(3, 2, h), place(0, 3, h)) for h in shifts]) for k in shifts]
     elemental = local_call(stage_kernel, jax.ShapeDtypeStruct(elemental.shape, elemental.dtype), (elemental,))
     own, elemental = lax.optimization_barrier((own, elemental))
-    skip_early = send(own, along_z(2, ready_far))
+    skip_early = send(own, along_z(2, lambda a, b: ready_far(a, b) and a < 3))
     far_early = send(own, along_z(3, ready_far))
     near_early = send(own, along_z(1, ready))
 
@@ -294,6 +300,7 @@
         (own, *direct, *handed, elemental),
         flops=8 * rows * width * width,
     )
+    hop = send(near_early, [(place(2, b, h), place(1, b, h)) for b in range(2, 4) for h in shifts])
     far_late = [send(value, along_z(3, lambda a, b: not ready_far(a, b))) for value in (home0, home1)]
     near = send(full_half, along_z(1, lambda a, b: not ready(a, b)))
     late = [send(far_late[part], along_z(1, lambda a, b: not ready_far(a ^ 3, b))) for part in parts]
@@ -312,7 +319,7 @@
         mine, given = local_call(
             lambda *refs, part=part: late_kernel(part, *refs),
             [jax.ShapeDtypeStruct((2, rows, rows), jnp.float32), piece],
-            (insertions, acc, *lefts, near_early, near, skip_early, late[part]),
+            (insertions, acc, *lefts, near_early, near, skip_early, hop, late[part]),
             tables=1,
             scratch=[pltpu.VMEM((2, rows, rows), own.dtype)],
             flops=16 * rows * rows * rows,

time: 98.6 us -> 93.7 us (0.950)
  the two profiles are of different devices: /device:TPU:0 before, /device:TPU:3 now
where the time goes in v3:
time: 93.7 us; the launch traced here: 93.3 us
  starting transfers between devices  40.4 us (43%)
  waiting for transfers between devices  40.3 us (43%)
  Pallas kernels  8.7 us (9%)
  local copies, waits for them, and re-layouts  2.99 us (3%)
  between operations  0.96 us (1%)
    ppermute x15, waiting for transfers between devices, send(): return lax.ppermute(value, AXES, pairs)  30.9 us
    ppermute x15, starting transfers between devices, send(): return lax.ppermute(value, AXES, pairs)  26.3 us
    ppermute x6, starting transfers between devices, swap(): return lax.ppermute(value, axis, [(i, i ^ mask) for i in range(size)])  11.8 us
    ppermute x6, waiting for transfers between devices, swap(): return lax.ppermute(value, axis, [(i, i ^ mask) for i in range(size)])  9.34 us
    pallas_call x7, Pallas kernels, local_call(): pl.pallas_call(kernel, out_shape=out_shape, in_specs=[SMEM] * tables + [V...  8.7 us
    unnamed x12, local copies, waits for them, and re-layouts  2.96 us
    ppermute x1, starting transfers between devices, left_panel(): give_x = lax.ppermute(give, ('snk', 'sub'), across)  2.3 us
  transfers between devices with their start and end apart: 22, of which 8 were waited for; matrix products, arithmetic and copies ran while one was open for 0% of the time, Pallas kernels for 6%

profile of v3, /device:TPU:3, one launch (start us, length us, event | category | flops | bytes accessed | tf_op | source)
XLA Modules:
  0.0 93.3 jit_solution(15031179163353586292)
XLA Ops:
  0.6 1.0 %copy-done.1 = bf16[1,1,2,256,512]{4,3,2,1,0:T(8,128)(2,1)S(1)} copy-done((bf16[1,1,2,256,512]{4,3,2,1,0:T(8,128)(2,1)S(1)}, bf16[1,1,2,256,512]{4,3,2,1,0:T(8,128)(2,1)}, u32[]{:S(2)}) %copy-start.1) | copy-done | bytes 524312
  1.7 0.7 copy-done.3
  2.3 0.8 shard_map.59
  3.1 0.7 collective-permute-start.2
  3.8 0.7 collective-permute-start.4
  4.5 0.7 collective-permute-start
  5.2 0.7 collective-permute-start.1
  5.9 1.3 %collective-permute-start.3 = (bf16[2,256,256]{2,1,0:T(8,128)(2,1)S(1)}, bf16[2,256,256]{2,1,0:T(8,128)(2,1)S(1)}, u32[]{:S(2)}, u32[]{:S(2)}) collective-permute-start(bf16[2,256,256]{2,1,0:T(8,128)(2,1)S(1)} %collective-permute-done.2), channel_id=1, source_target_pairs={{28,6},{29,7}} | collective-permute-start | bytes 786440 | tf_op jit(solution)/shard_map/ppermute | solution.py:84
  7.2 1.3 %collective-permute-start.5 = (bf16[2,256,256]{2,1,0:T(8,128)(2,1)S(1)}, bf16[2,256,256]{2,1,0:T(8,128)(2,1)S(1)}, u32[]{:S(2)}, u32[]{:S(2)}) collective-permute-start(bf16[2,256,256]{2,1,0:T(8,128)(2,1)S(1)} %collective-permute-done.4), channel_id=1, source_target_pairs={{28,6},{29,7}} | collective-permute-start | bytes 786440 | tf_op jit(solution)/shard_map/ppermute | solution.py:84
  8.5 0.0 copy-start
  8.5 1.2 %copy-done = bf16[2,512,512]{2,1,0:T(8,128)(2,1)S(1)} copy-done((bf16[2,512,512]{2,1,0:T(8,128)(2,1)S(1)}, bf16[2,512,512]{2,1,0:T(8,128)(2,1)}, u32[]{:S(2)}) %copy-start) | copy-done | bytes 1048600
  9.7 0.1 shard_map.60.elem
  9.8 0.0 copy-start.2
  9.8 0.0 collective-permute-done.direct0
  9.8 11.1 %collective-permute-done.3.hand0 = bf16[2,256,256]{2,1,0:T(8,128)(2,1)S(1)} collective-permute-done((bf16[2,256,256]{2,1,0:T(8,128)(2,1)S(1)}, bf16[2,256,256]{2,1,0:T(8,128)(2,1)S(1)}, u32[]{:S(2)}, u32[]{:S(2)}) %collective-permute-start.3) | collective-permute-done | bytes 262176 | tf_op jit(solution)/shard_map/ppermute | solution.py:84
  20.9 3.8 %collective-permute-done.5.hand1 = bf16[2,256,256]{2,1,0:T(8,128)(2,1)S(1)} collective-permute-done((bf16[2,256,256]{2,1,0:T(8,128)(2,1)S(1)}, bf16[2,256,256]{2,1,0:T(8,128)(2,1)S(1)}, u32[]{:S(2)}, u32[]{:S(2)}) %collective-permute-start.5) | collective-permute-done | bytes 262176 | tf_op jit(solution)/shard_map/ppermute | solution.py:84
  24.6 1.4 %shard_map.61 = (bf16[2,256,512]{2,1,0:T(8,128)(2,1)}, bf16[2,256,256]{2,1,0:T(8,128)(2,1)S(1)}, bf16[2,256,256]{2,1,0:T(8,128)(2,1)S(1)}, bf16[2,256,256]{2,1,0:T(8,128)(2,1)S(1)}, bf16[2,256,256]{2,1,0:T(8,128)(2,1)S(1)}) custom-call(bf16[2,256,512]{2,1,0:T(8,128)(2,1)S(1)} %get-tuple-element.20.own, ...), custom_call_target="tpu_custom_call" | custom-call | flops 536870912 | bytes 4194304 | tf_op jit(solution)/shard_map/pallas_call | solution.py:38
  26.0 0.0 collective-permute-start.8
  26.0 1.4 %collective-permute-start.11 = (bf16[2,256,512]{2,1,0:T(8,128)(2,1)S(1)}, bf16[2,256,512]{2,1,0:T(8,128)(2,1)S(1)}, u32[]{:S(2)}, u32[]{:S(2)}) collective-permute-start(bf16[2,256,512]{2,1,0:T(8,128)(2,1)S(1)} %get-tuple-element.20.own), channel_id=1, source_target_pairs={{8,16},{9,17},{10,18},{11,19},{20,12},{21,13},{28,4},{29,5},{30,6}... | collective-permute-start | bytes 1572872 | tf_op jit(solution)/shard_map/ppermute | solution.py:84
  27.4 0.3 collective-permute-start.6
  27.8 0.7 collective-permute-start.14
  28.5 2.3 %collective-permute-start.9 = (bf16[2,256,256]{2,1,0:T(8,128)(2,1)S(1)}, bf16[2,256,256]{2,1,0:T(8,128)(2,1)S(1)}, u32[]{:S(2)}, u32[]{:S(2)}) collective-permute-start(bf16[2,256,256]{2,1,0:T(8,128)(2,1)S(1)} %get-tuple-element.26), channel_id=1, source_target_pairs={{0,5},{1,4},{2,7},{3,6},{4,1},{5,0},{6,3},{7,2},{8,13},{9,12},{10,... | collective-permute-start | bytes 786440 | tf_op jit(solution)/shard_map/ppermute | solution.py:133
  30.8 0.4 collective-permute-done.8
  31.2 5.4 %collective-permute-start.12 = (bf16[2,256,256]{2,1,0:T(8,128)(2,1)S(1)}, bf16[2,256,256]{2,1,0:T(8,128)(2,1)S(1)}, u32[]{:S(2)}, u32[]{:S(2)}) collective-permute-start(bf16[2,256,256]{2,1,0:T(8,128)(2,1)S(1)} %get-tuple-element.27.home0), channel_id=1, source_target_pairs={{0,24},{1,25},{2,26},{3,27},{4,28},{5,29},{6,30},{7,31},{12,20},{1... | collective-permute-start | bytes 786440 | tf_op jit(solution)/shard_map/ppermute | solution.py:84
  36.7 1.8 %collective-permute-start.13 = (bf16[2,256,256]{2,1,0:T(8,128)(2,1)S(1)}, bf16[2,256,256]{2,1,0:T(8,128)(2,1)S(1)}, u32[]{:S(2)}, u32[]{:S(2)}) collective-permute-start(bf16[2,256,256]{2,1,0:T(8,128)(2,1)S(1)} %get-tuple-element.28.home1), channel_id=1, source_target_pairs={{0,24},{1,25},{2,26},{3,27},{4,28},{5,29},{6,30},{7,31},{12,20},{1... | collective-permute-start | bytes 786440 | tf_op jit(solution)/shard_map/ppermute | solution.py:84
  38.6 0.0 collective-permute-done.9
  38.6 7.4 %collective-permute-start.7 = (bf16[2,512,256]{2,1,0:T(8,128)(2,1)S(1)}, bf16[2,512,256]{2,1,0:T(8,128)(2,1)S(1)}, u32[]{:S(2)}, u32[]{:S(2)}) collective-permute-start(bf16[2,512,256]{2,1,0:T(8,128)(2,1)S(1)} %constant_dynamic-update-slice_fusion.left0), channel_id=1, source_target_pairs={{0,2},{2,0},{4,6},{6,4},{1,3},{3,1},{5,7},{7,5},{8,10},{10,8},{12,... | collective-permute-start | bytes 1572872 | tf_op jit(solution)/shard_map/ppermute | solution.py:28
  46.0 0.0 collective-permute-done.11.far_early
  46.0 3.8 %collective-permute-start.10 = (bf16[2,512,256]{2,1,0:T(8,128)(2,1)S(1)}, bf16[2,512,256]{2,1,0:T(8,128)(2,1)S(1)}, u32[]{:S(2)}, u32[]{:S(2)}) collective-permute-start(bf16[2,512,256]{2,1,0:T(8,128)(2,1)S(1)} %constant_dynamic-update-slice_fusion.2.left2), channel_id=1, source_target_pairs={{0,2},{2,0},{4,6},{6,4},{1,3},{3,1},{5,7},{7,5},{8,10},{10,8},{12,... | collective-permute-start | bytes 1572872 | tf_op jit(solution)/shard_map/ppermute | solution.py:28
  49.8 0.0 collective-permute-done.14.refs_4_
  49.8 0.7 collective-permute-start.16
  50.5 7.7 %collective-permute-start.15 = (bf16[2,256,512]{2,1,0:T(8,128)(2,1)S(1)}, bf16[2,256,512]{2,1,0:T(8,128)(2,1)S(1)}, u32[]{:S(2)}, u32[]{:S(2)}) collective-permute-start(bf16[2,256,512]{2,1,0:T(8,128)(2,1)S(1)} %copy-done.4), channel_id=1, source_target_pairs={{2,10},{3,11},{4,12},{5,13},{6,14},{7,15},{12,4},{13,5},{14,6},{15... | collective-permute-start | bytes 1572872 | tf_op jit(solution)/shard_map/ppermute | solution.py:84
  58.2 0.7 collective-permute-start.17
  58.9 0.0 collective-permute-done.7.left1
  58.9 1.3 %collective-permute-start.18 = (bf16[2,256,256]{2,1,0:T(8,128)(2,1)S(1)}, bf16[2,256,256]{2,1,0:T(8,128)(2,1)S(1)}, u32[]{:S(2)}, u32[]{:S(2)}) collective-permute-start(bf16[2,256,256]{2,1,0:T(8,128)(2,1)S(1)} %collective-permute-done.12.far0), channel_id=1, source_target_pairs={{0,8},{1,9},{2,10},{3,11},{8,0},{9,1},{10,2},{11,3},{14,6},{15,7},... | collective-permute-start | bytes 786440 | tf_op jit(solution)/shard_map/ppermute | solution.py:84
  60.2 1.3 %collective-permute-start.20 = (bf16[2,256,256]{2,1,0:T(8,128)(2,1)S(1)}, bf16[2,256,256]{2,1,0:T(8,128)(2,1)S(1)}, u32[]{:S(2)}, u32[]{:S(2)}) collective-permute-start(bf16[2,256,256]{2,1,0:T(8,128)(2,1)S(1)} %collective-permute-done.13.far1), channel_id=1, source_target_pairs={{0,8},{1,9},{2,10},{3,11},{8,0},{9,1},{10,2},{11,3},{14,6},{15,7},... | collective-permute-start | bytes 786440 | tf_op jit(solution)/shard_map/ppermute | solution.py:84
  61.5 2.4 %shard_map.62 = (f32[2,512,512]{2,1,0:T(8,128)S(1)}, bf16[2,512,256]{2,1,0:T(8,128)(2,1)S(1)}, bf16[2,512,256]{2,1,0:T(8,128)(2,1)S(1)}) custom-call(s32[4]{0:T(128)S(1)} %copy-done.2, bf16[2,512,256]{2,1,0:T(8,128)(2,1)S(1)} %constant_dynamic-update-slice_fusion.left0, bf16[2,512,256]{2,1,0:T(8,128)(2,1)S(1)} %collective-permute-done.7.left1, ...), custom_call_target="tpu_custom_call" | custom-call | flops 1073741824 | bytes 6815760 | tf_op jit(solution)/shard_map/pallas_call | solution.py:38
  64.0 12.1 %collective-permute-done.15.refs_5_ = bf16[2,256,512]{2,1,0:T(8,128)(2,1)S(1)} collective-permute-done((bf16[2,256,512]{2,1,0:T(8,128)(2,1)S(1)}, bf16[2,256,512]{2,1,0:T(8,128)(2,1)S(1)}, u32[]{:S(2)}, u32[]{:S(2)}) %collective-permute-start.15) | collective-permute-done | bytes 524320 | tf_op jit(solution)/shard_map/ppermute | solution.py:84
  76.1 0.0 collective-permute-done.17.refs_7_
  76.1 2.5 %collective-permute-done.18.refs_8_ = bf16[2,256,256]{2,1,0:T(8,128)(2,1)S(1)} collective-permute-done((bf16[2,256,256]{2,1,0:T(8,128)(2,1)S(1)}, bf16[2,256,256]{2,1,0:T(8,128)(2,1)S(1)}, u32[]{:S(2)}, u32[]{:S(2)}) %collective-permute-start.18) | collective-permute-done | bytes 262176 | tf_op jit(solution)/shard_map/ppermute | solution.py:84
  78.6 1.5 %shard_map.63 = (f32[2,256,256]{2,1,0:T(8,128)S(1)}, bf16[2,256,256]{2,1,0:T(8,128)(2,1)S(1)}) custom-call(s32[4]{0:T(128)S(1)} %copy-done.2, f32[2,512,512]{2,1,0:T(8,128)S(1)} %get-tuple-element.29.refs_1_, bf16[2,512,256]{2,1,0:T(8,128)(2,1)S(1)} %get-tuple-element.30.refs_2_, bf16[2,512,256]{2,1,0:T(8,128)(2,1)S(1)} %get-tuple-element.31.refs_3_, ...), custom_call_target="tpu_custom_call" | custom-call | flops 268435456 | bytes 6291472 | tf_op jit(solution)/shard_map/pallas_call | solution.py:38
  80.1 0.2 collective-permute-start.19
  80.3 1.4 %collective-permute-done.20.refs_8_ = bf16[2,256,256]{2,1,0:T(8,128)(2,1)S(1)} collective-permute-done((bf16[2,256,256]{2,1,0:T(8,128)(2,1)S(1)}, bf16[2,256,256]{2,1,0:T(8,128)(2,1)S(1)}, u32[]{:S(2)}, u32[]{:S(2)}) %collective-permute-start.20) | collective-permute-done | bytes 262176 | tf_op jit(solution)/shard_map/ppermute | solution.py:84
  81.7 1.5 %shard_map.64 = (f32[2,256,256]{2,1,0:T(8,128)S(1)}, bf16[2,256,256]{2,1,0:T(8,128)(2,1)S(1)}) custom-call(s32[4]{0:T(128)S(1)} %copy-done.2, f32[2,512,512]{2,1,0:T(8,128)S(1)} %get-tuple-element.29.refs_1_, bf16[2,512,256]{2,1,0:T(8,128)(2,1)S(1)} %get-tuple-element.30.refs_2_, bf16[2,512,256]{2,1,0:T(8,128)(2,1)S(1)} %get-tuple-element.31.refs_3_, ...), custom_call_target="tpu_custom_call" | custom-call | flops 268435456 | bytes 6291472 | tf_op jit(solution)/shard_map/pallas_call | solution.py:38
  83.2 0.1 collective-permute-start.21
  83.3 5.2 %collective-permute-done.19.given0 = bf16[2,256,256]{2,1,0:T(8,128)(2,1)S(1)} collective-permute-done((bf16[2,256,256]{2,1,0:T(8,128)(2,1)S(1)}, bf16[2,256,256]{2,1,0:T(8,128)(2,1)S(1)}, u32[]{:S(2)}, u32[]{:S(2)}) %collective-permute-start.19) | collective-permute-done | bytes 262176 | tf_op jit(solution)/shard_map/ppermute | solution.py:28
  88.5 3.7 %collective-permute-done.21.given1 = bf16[2,256,256]{2,1,0:T(8,128)(2,1)S(1)} collective-permute-done((bf16[2,256,256]{2,1,0:T(8,128)(2,1)S(1)}, bf16[2,256,256]{2,1,0:T(8,128)(2,1)S(1)}, u32[]{:S(2)}, u32[]{:S(2)}) %collective-permute-start.21) | collective-permute-done | bytes 262176 | tf_op jit(solution)/shard_map/ppermute | solution.py:28
  92.2 1.1 %shard_map.65 = f32[2,256,512]{2,1,0:T(8,128)} custom-call(f32[2,256,256]{2,1,0:T(8,128)S(1)} %get-tuple-element.32.mine0, bf16[2,256,256]{2,1,0:T(8,128)(2,1)S(1)} %collective-permute-done.19.given0, f32[2,256,256]{2,1,0:T(8,128)S(1)} %get-tuple-element.34.mine1, bf16[2,256,256]{2,1,0:T(8,128)(2,1)S(1)} %collective-permute-done.21.given1), custom_call_target="tpu_custom_call" | custom-call | bytes 2621440 | tf_op jit(solution)/shard_map/pallas_call | solution.py:38
  (17 shorter events, 0.1 us)
Async XLA Ops:
  0.6 1.0 %copy-start.1 = (bf16[1,1,2,256,512]{4,3,2,1,0:T(8,128)(2,1)S(1)}, bf16[1,1,2,256,512]{4,3,2,1,0:T(8,128)(2,1)}, u32[]{:S(2)}) copy-start(bf16[1,1,2,256,512]{4,3,2,1,0:T(8,128)(2,1)} %param.4) | copy-start | bytes 1572868
  1.7 0.7 copy-start.3
  3.1 2.7 %collective-permute-start.2 = (bf16[2,256,256]{2,1,0:T(8,128)(2,1)S(1)}, bf16[2,256,256]{2,1,0:T(8,128)(2,1)S(1)}, u32[]{:S(2)}, u32[]{:S(2)}) collective-permute-start(bf16[2,256,256]{2,1,0:T(8,128)(2,1)S(1)} %get-tuple-element.21), channel_id=1, source_target_pairs={{24,28},{25,29}} | collective-permute-start | bytes 786440 | tf_op jit(solution)/shard_map/ppermute | solution.py:84
  3.8 3.4 %collective-permute-start.4 = (bf16[2,256,256]{2,1,0:T(8,128)(2,1)S(1)}, bf16[2,256,256]{2,1,0:T(8,128)(2,1)S(1)}, u32[]{:S(2)}, u32[]{:S(2)}) collective-permute-start(bf16[2,256,256]{2,1,0:T(8,128)(2,1)S(1)} %get-tuple-element.22), channel_id=1, source_target_pairs={{24,29},{25,28}} | collective-permute-start | bytes 786440 | tf_op jit(solution)/shard_map/ppermute | solution.py:84
  4.5 5.3 %collective-permute-start = (bf16[2,256,256]{2,1,0:T(8,128)(2,1)S(1)}, bf16[2,256,256]{2,1,0:T(8,128)(2,1)S(1)}, u32[]{:S(2)}, u32[]{:S(2)}) collective-permute-start(bf16[2,256,256]{2,1,0:T(8,128)(2,1)S(1)} %get-tuple-element.21), channel_id=1, source_target_pairs={{8,2},{9,3},{16,4},{17,5},{18,12},{19,13},{26,14},{27,15},{28,22},... | collective-permute-start | bytes 786440 | tf_op jit(solution)/shard_map/ppermute | solution.py:84
  5.2 4.6 %collective-permute-start.1 = (bf16[2,256,256]{2,1,0:T(8,128)(2,1)S(1)}, bf16[2,256,256]{2,1,0:T(8,128)(2,1)S(1)}, u32[]{:S(2)}, u32[]{:S(2)}) collective-permute-start(bf16[2,256,256]{2,1,0:T(8,128)(2,1)S(1)} %get-tuple-element.22), channel_id=1, source_target_pairs={{8,3},{9,2},{16,5},{17,4},{18,13},{19,12},{26,15},{27,14},{28,23},... | collective-permute-start | bytes 786440 | tf_op jit(solution)/shard_map/ppermute | solution.py:84
  5.9 15.0 %collective-permute-start.3 = (bf16[2,256,256]{2,1,0:T(8,128)(2,1)S(1)}, bf16[2,256,256]{2,1,0:T(8,128)(2,1)S(1)}, u32[]{:S(2)}, u32[]{:S(2)}) collective-permute-start(bf16[2,256,256]{2,1,0:T(8,128)(2,1)S(1)} %collective-permute-done.2), channel_id=1, source_target_pairs={{28,6},{29,7}} | collective-permute-start | bytes 786440 | tf_op jit(solution)/shard_map/ppermute | solution.py:84
  7.2 17.5 %collective-permute-start.5 = (bf16[2,256,256]{2,1,0:T(8,128)(2,1)S(1)}, bf16[2,256,256]{2,1,0:T(8,128)(2,1)S(1)}, u32[]{:S(2)}, u32[]{:S(2)}) collective-permute-start(bf16[2,256,256]{2,1,0:T(8,128)(2,1)S(1)} %collective-permute-done.4), channel_id=1, source_target_pairs={{28,6},{29,7}} | collective-permute-start | bytes 786440 | tf_op jit(solution)/shard_map/ppermute | solution.py:84
  8.5 1.2 %copy-start = (bf16[2,512,512]{2,1,0:T(8,128)(2,1)S(1)}, bf16[2,512,512]{2,1,0:T(8,128)(2,1)}, u32[]{:S(2)}) copy-start(bf16[2,512,512]{2,1,0:T(8,128)(2,1)} %value.1) | copy-start | bytes 3145732
  9.8 51.8 %copy-start.2 = (s32[4]{0:T(128)S(1)}, s32[4]{0:T(128)}, u32[]{:S(2)}) copy-start(s32[4]{0:T(128)} %refs_0_.3) | copy-start | bytes 52
  26.0 24.5 %copy-start.4 = (bf16[2,256,512]{2,1,0:T(8,128)(2,1)S(1)}, bf16[2,256,512]{2,1,0:T(8,128)(2,1)}, u32[]{:S(2)}) copy-start(bf16[2,256,512]{2,1,0:T(8,128)(2,1)} %get-tuple-element.24) | copy-start | bytes 1572868
  26.0 5.2 %collective-permute-start.8 = (bf16[2,256,256]{2,1,0:T(8,128)(2,1)S(1)}, bf16[2,256,256]{2,1,0:T(8,128)(2,1)S(1)}, u32[]{:S(2)}, u32[]{:S(2)}) collective-permute-start(bf16[2,256,256]{2,1,0:T(8,128)(2,1)S(1)} %get-tuple-element.25), channel_id=1, source_target_pairs={{0,4},{2,6},{4,0},{6,2},{1,5},{3,7},{5,1},{7,3},{8,12},{10,14},{12... | collective-permute-start | bytes 786440 | tf_op jit(solution)/shard_map/ppermute | solution.py:28
  26.0 20.0 %collective-permute-start.11 = (bf16[2,256,512]{2,1,0:T(8,128)(2,1)S(1)}, bf16[2,256,512]{2,1,0:T(8,128)(2,1)S(1)}, u32[]{:S(2)}, u32[]{:S(2)}) collective-permute-start(bf16[2,256,512]{2,1,0:T(8,128)(2,1)S(1)} %get-tuple-element.20.own), channel_id=1, source_target_pairs={{8,16},{9,17},{10,18},{11,19},{20,12},{21,13},{28,4},{29,5},{30,6}... | collective-permute-start | bytes 1572872 | tf_op jit(solution)/shard_map/ppermute | solution.py:84
  27.4 9.2 %collective-permute-start.6 = (bf16[2,256,256]{2,1,0:T(8,128)(2,1)S(1)}, bf16[2,256,256]{2,1,0:T(8,128)(2,1)S(1)}, u32[]{:S(2)}, u32[]{:S(2)}) collective-permute-start(bf16[2,256,256]{2,1,0:T(8,128)(2,1)S(1)} %get-tuple-element.26), channel_id=1, source_target_pairs={{0,1},{1,0},{2,3},{3,2},{4,5},{5,4},{6,7},{7,6},{8,9},{9,8},{10,11... | collective-permute-start | bytes 786440 | tf_op jit(solution)/shard_map/ppermute | solution.py:28
  27.8 22.1 %collective-permute-start.14 = (bf16[2,256,512]{2,1,0:T(8,128)(2,1)S(1)}, bf16[2,256,512]{2,1,0:T(8,128)(2,1)S(1)}, u32[]{:S(2)}, u32[]{:S(2)}) collective-permute-start(bf16[2,256,512]{2,1,0:T(8,128)(2,1)S(1)} %get-tuple-element.20.own), channel_id=1, source_target_pairs={{0,8},{1,9},{8,0},{9,1},{10,2},{11,3},{16,24},{17,25},{18,26},{19,... | collective-permute-start | bytes 1572872 | tf_op jit(solution)/shard_map/ppermute | solution.py:84
  28.5 10.1 %collective-permute-start.9 = (bf16[2,256,256]{2,1,0:T(8,128)(2,1)S(1)}, bf16[2,256,256]{2,1,0:T(8,128)(2,1)S(1)}, u32[]{:S(2)}, u32[]{:S(2)}) collective-permute-start(bf16[2,256,256]{2,1,0:T(8,128)(2,1)S(1)} %get-tuple-element.26), channel_id=1, source_target_pairs={{0,5},{1,4},{2,7},{3,6},{4,1},{5,0},{6,3},{7,2},{8,13},{9,12},{10,... | collective-permute-start | bytes 786440 | tf_op jit(solution)/shard_map/ppermute | solution.py:133
  31.2 19.3 %collective-permute-start.12 = (bf16[2,256,256]{2,1,0:T(8,128)(2,1)S(1)}, bf16[2,256,256]{2,1,0:T(8,128)(2,1)S(1)}, u32[]{:S(2)}, u32[]{:S(2)}) collective-permute-start(bf16[2,256,256]{2,1,0:T(8,128)(2,1)S(1)} %get-tuple-element.27.home0), channel_id=1, source_target_pairs={{0,24},{1,25},{2,26},{3,27},{4,28},{5,29},{6,30},{7,31},{12,20},{1... | collective-permute-start | bytes 786440 | tf_op jit(solution)/shard_map/ppermute | solution.py:84
  36.7 21.5 %collective-permute-start.13 = (bf16[2,256,256]{2,1,0:T(8,128)(2,1)S(1)}, bf16[2,256,256]{2,1,0:T(8,128)(2,1)S(1)}, u32[]{:S(2)}, u32[]{:S(2)}) collective-permute-start(bf16[2,256,256]{2,1,0:T(8,128)(2,1)S(1)} %get-tuple-element.28.home1), channel_id=1, source_target_pairs={{0,24},{1,25},{2,26},{3,27},{4,28},{5,29},{6,30},{7,31},{12,20},{1... | collective-permute-start | bytes 786440 | tf_op jit(solution)/shard_map/ppermute | solution.py:84
  38.6 20.3 %collective-permute-start.7 = (bf16[2,512,256]{2,1,0:T(8,128)(2,1)S(1)}, bf16[2,512,256]{2,1,0:T(8,128)(2,1)S(1)}, u32[]{:S(2)}, u32[]{:S(2)}) collective-permute-start(bf16[2,512,256]{2,1,0:T(8,128)(2,1)S(1)} %constant_dynamic-update-slice_fusion.left0), channel_id=1, source_target_pairs={{0,2},{2,0},{4,6},{6,4},{1,3},{3,1},{5,7},{7,5},{8,10},{10,8},{12,... | collective-permute-start | bytes 1572872 | tf_op jit(solution)/shard_map/ppermute | solution.py:28
  46.0 14.2 %collective-permute-start.10 = (bf16[2,512,256]{2,1,0:T(8,128)(2,1)S(1)}, bf16[2,512,256]{2,1,0:T(8,128)(2,1)S(1)}, u32[]{:S(2)}, u32[]{:S(2)}) collective-permute-start(bf16[2,512,256]{2,1,0:T(8,128)(2,1)S(1)} %constant_dynamic-update-slice_fusion.2.left2), channel_id=1, source_target_pairs={{0,2},{2,0},{4,6},{6,4},{1,3},{3,1},{5,7},{7,5},{8,10},{10,8},{12,... | collective-permute-start | bytes 1572872 | tf_op jit(solution)/shard_map/ppermute | solution.py:28
  49.8 14.1 %collective-permute-start.16 = (bf16[2,256,512]{2,1,0:T(8,128)(2,1)S(1)}, bf16[2,256,512]{2,1,0:T(8,128)(2,1)S(1)}, u32[]{:S(2)}, u32[]{:S(2)}) collective-permute-start(bf16[2,256,512]{2,1,0:T(8,128)(2,1)S(1)} %get-tuple-element.20.own), channel_id=1, source_target_pairs={{8,24},{9,25},{10,26},{11,27},{20,4},{21,5}} | collective-permute-start | bytes 1572872 | tf_op jit(solution)/shard_map/ppermute | solution.py:84
  50.5 25.5 %collective-permute-start.15 = (bf16[2,256,512]{2,1,0:T(8,128)(2,1)S(1)}, bf16[2,256,512]{2,1,0:T(8,128)(2,1)S(1)}, u32[]{:S(2)}, u32[]{:S(2)}) collective-permute-start(bf16[2,256,512]{2,1,0:T(8,128)(2,1)S(1)} %copy-done.4), channel_id=1, source_target_pairs={{2,10},{3,11},{4,12},{5,13},{6,14},{7,15},{12,4},{13,5},{14,6},{15... | collective-permute-start | bytes 1572872 | tf_op jit(solution)/shard_map/ppermute | solution.py:84
  58.2 17.9 %collective-permute-start.17 = (bf16[2,256,512]{2,1,0:T(8,128)(2,1)S(1)}, bf16[2,256,512]{2,1,0:T(8,128)(2,1)S(1)}, u32[]{:S(2)}, u32[]{:S(2)}) collective-permute-start(bf16[2,256,512]{2,1,0:T(8,128)(2,1)S(1)} %collective-permute-done.14.refs_4_), channel_id=1, source_target_pairs={{20,12},{21,13},{22,14},{23,15}} | collective-permute-start | bytes 1572872 | tf_op jit(solution)/shard_map/ppermute | solution.py:84
  58.9 19.7 %collective-permute-start.18 = (bf16[2,256,256]{2,1,0:T(8,128)(2,1)S(1)}, bf16[2,256,256]{2,1,0:T(8,128)(2,1)S(1)}, u32[]{:S(2)}, u32[]{:S(2)}) collective-permute-start(bf16[2,256,256]{2,1,0:T(8,128)(2,1)S(1)} %collective-permute-done.12.far0), channel_id=1, source_target_pairs={{0,8},{1,9},{2,10},{3,11},{8,0},{9,1},{10,2},{11,3},{14,6},{15,7},... | collective-permute-start | bytes 786440 | tf_op jit(solution)/shard_map/ppermute | solution.py:84
  60.2 21.5 %collective-permute-start.20 = (bf16[2,256,256]{2,1,0:T(8,128)(2,1)S(1)}, bf16[2,256,256]{2,1,0:T(8,128)(2,1)S(1)}, u32[]{:S(2)}, u32[]{:S(2)}) collective-permute-start(bf16[2,256,256]{2,1,0:T(8,128)(2,1)S(1)} %collective-permute-done.13.far1), channel_id=1, source_target_pairs={{0,8},{1,9},{2,10},{3,11},{8,0},{9,1},{10,2},{11,3},{14,6},{15,7},... | collective-permute-start | bytes 786440 | tf_op jit(solution)/shard_map/ppermute | solution.py:84
  80.1 8.4 %collective-permute-start.19 = (bf16[2,256,256]{2,1,0:T(8,128)(2,1)S(1)}, bf16[2,256,256]{2,1,0:T(8,128)(2,1)S(1)}, u32[]{:S(2)}, u32[]{:S(2)}) collective-permute-start(bf16[2,256,256]{2,1,0:T(8,128)(2,1)S(1)} %get-tuple-element.33), channel_id=1, source_target_pairs={{0,1},{1,0},{2,3},{3,2},{4,5},{5,4},{6,7},{7,6},{8,9},{9,8},{10,11... | collective-permute-start | bytes 786440 | tf_op jit(solution)/shard_map/ppermute | solution.py:28
  83.2 9.0 %collective-permute-start.21 = (bf16[2,256,256]{2,1,0:T(8,128)(2,1)S(1)}, bf16[2,256,256]{2,1,0:T(8,128)(2,1)S(1)}, u32[]{:S(2)}, u32[]{:S(2)}) collective-permute-start(bf16[2,256,256]{2,1,0:T(8,128)(2,1)S(1)} %get-tuple-element.35), channel_id=1, source_target_pairs={{0,1},{1,0},{2,3},{3,2},{4,5},{5,4},{6,7},{7,6},{8,9},{9,8},{10,11... | collective-permute-start | bytes 786440 | tf_op jit(solution)/shard_map/ppermute | solution.py:28

commit v4 on v3

--- a/solution.py
+++ b/solution.py
@@ -258,10 +258,26 @@
         give[index] = total[rows:].astype(jnp.bfloat16)
 
 
-def finish_kernel(mine0, given0, mine1, given1, out):
-    rows = mine0.shape[1]
-    out[:, :, :rows] = mine0[...] + given0[...].astype(jnp.float32)
-    out[:, :, rows:] = mine1[...] + given1[...].astype(jnp.float32)
+def finish_kernel(part, mine, given, *refs):
+    out, total, sem = refs[-3:]
+    rows = mine.shape[1]
+    total[...] = mine[...] + given[...].astype(jnp.float32)
+    copy = pltpu.make_async_copy(total, out.at[:, :, part * rows : (part + 1) * rows], sem)
+    copy.start()
+    copy.wait()
+
+
+def finish(part, mine, given, width, *whole):
+    anywhere = pl.BlockSpec(memory_space=pltpu.HBM)
+    return pl.pallas_call(
+        lambda *refs: finish_kernel(part, *refs),
+        out_shape=jax.ShapeDtypeStruct((*mine.shape[:2], width), jnp.float32),
+        in_specs=[VMEM, VMEM] + [anywhere] * len(whole),
+        out_specs=anywhere,
+        scratch_shapes=[pltpu.VMEM(mine.shape, jnp.float32), pltpu.SemaphoreType.DMA],
+        input_output_aliases={2: 0} if whole else {},
+        compiler_params=pltpu.CompilerParams(vmem_limit_bytes=16 * 2**20),
+    )(mine, given, *whole)
 
 
 def along_z(mask, chosen):
@@ -325,7 +341,8 @@
             flops=16 * rows * rows * rows,
         )
         ends += [mine, swap(given, "sub", 1)]
-    total = local_call(finish_kernel, jax.ShapeDtypeStruct(own.shape, jnp.float32), tuple(ends))
+    total = finish(0, *ends[:2], width)
+    total = finish(1, *ends[2:], width, total)
     return full_half, total
 
 

time: 93.7 us -> 93.5 us (level)
    pallas_call x0 -> x2, Pallas kernels: none -> 1.71 us  [finish(): pl.pallas_call(lambda *refs: finish_kernel(part, *refs), out_shape=jax.Sh...]
    pallas_call x7 -> x6, Pallas kernels: 8.7 us -> 7.62 us  [local_call(): pl.pallas_call(kernel, out_shape=out_shape, in_specs=[SMEM] * tables + [V...]
  transfers between devices with their start and end apart: 22 -> 22, of which waited for: 8 -> 8; matrix products, arithmetic and copies ran while one was open for 0% -> 0% of each run, Pallas kernels for 6% -> 7%
where the time goes in v4:
time: 93.5 us; the launch traced here: 93.1 us
  starting transfers between devices  40.4 us (43%)
  waiting for transfers between devices  39.4 us (42%)
  Pallas kernels  9.33 us (10%)
  local copies, waits for them, and re-layouts  2.99 us (3%)
  between operations  0.97 us (1%)
    ppermute x15, waiting for transfers between devices, send(): return lax.ppermute(value, AXES, pairs)  30.9 us
    ppermute x15, starting transfers between devices, send(): return lax.ppermute(value, AXES, pairs)  26.3 us
    ppermute x6, starting transfers between devices, swap(): return lax.ppermute(value, axis, [(i, i ^ mask) for i in range(size)])  11.8 us
    ppermute x6, waiting for transfers between devices, swap(): return lax.ppermute(value, axis, [(i, i ^ mask) for i in range(size)])  8.48 us
    pallas_call x6, Pallas kernels, local_call(): pl.pallas_call(kernel, out_shape=out_shape, in_specs=[SMEM] * tables + [V...  7.62 us
    unnamed x12, local copies, waits for them, and re-layouts  2.96 us
    ppermute x1, starting transfers between devices, left_panel(): give_x = lax.ppermute(give, ('snk', 'sub'), across)  2.3 us
  transfers between devices with their start and end apart: 22, of which 8 were waited for; matrix products, arithmetic and copies ran while one was open for 0% of the time, Pallas kernels for 7%

profile of v4, /device:TPU:3, one launch (start us, length us, event | category | flops | bytes accessed | tf_op | source)
XLA Modules:
  0.0 93.1 jit_solution(14694386048970515461)
XLA Ops:
  0.6 1.0 %copy-done.1 = bf16[1,1,2,256,512]{4,3,2,1,0:T(8,128)(2,1)S(1)} copy-done((bf16[1,1,2,256,512]{4,3,2,1,0:T(8,128)(2,1)S(1)}, bf16[1,1,2,256,512]{4,3,2,1,0:T(8,128)(2,1)}, u32[]{:S(2)}) %copy-start.1) | copy-done | bytes 524312
  1.7 0.7 copy-done.3
  2.3 0.8 shard_map.59
  3.1 0.7 collective-permute-start.2
  3.8 0.7 collective-permute-start.4
  4.5 0.7 collective-permute-start
  5.2 0.7 collective-permute-start.1
  5.9 1.3 %collective-permute-start.3 = (bf16[2,256,256]{2,1,0:T(8,128)(2,1)S(1)}, bf16[2,256,256]{2,1,0:T(8,128)(2,1)S(1)}, u32[]{:S(2)}, u32[]{:S(2)}) collective-permute-start(bf16[2,256,256]{2,1,0:T(8,128)(2,1)S(1)} %collective-permute-done.2), channel_id=1, source_target_pairs={{28,6},{29,7}} | collective-permute-start | bytes 786440 | tf_op jit(solution)/shard_map/ppermute | solution.py:84
  7.2 1.3 %collective-permute-start.5 = (bf16[2,256,256]{2,1,0:T(8,128)(2,1)S(1)}, bf16[2,256,256]{2,1,0:T(8,128)(2,1)S(1)}, u32[]{:S(2)}, u32[]{:S(2)}) collective-permute-start(bf16[2,256,256]{2,1,0:T(8,128)(2,1)S(1)} %collective-permute-done.4), channel_id=1, source_target_pairs={{28,6},{29,7}} | collective-permute-start | bytes 786440 | tf_op jit(solution)/shard_map/ppermute | solution.py:84
  8.5 0.0 copy-start
  8.5 1.2 %copy-done = bf16[2,512,512]{2,1,0:T(8,128)(2,1)S(1)} copy-done((bf16[2,512,512]{2,1,0:T(8,128)(2,1)S(1)}, bf16[2,512,512]{2,1,0:T(8,128)(2,1)}, u32[]{:S(2)}) %copy-start) | copy-done | bytes 1048600
  9.7 0.1 shard_map.60.elem
  9.8 0.0 copy-start.2
  9.8 0.0 collective-permute-done.direct0
  9.8 11.1 %collective-permute-done.3.hand0 = bf16[2,256,256]{2,1,0:T(8,128)(2,1)S(1)} collective-permute-done((bf16[2,256,256]{2,1,0:T(8,128)(2,1)S(1)}, bf16[2,256,256]{2,1,0:T(8,128)(2,1)S(1)}, u32[]{:S(2)}, u32[]{:S(2)}) %collective-permute-start.3) | collective-permute-done | bytes 262176 | tf_op jit(solution)/shard_map/ppermute | solution.py:84
  20.9 3.8 %collective-permute-done.5.hand1 = bf16[2,256,256]{2,1,0:T(8,128)(2,1)S(1)} collective-permute-done((bf16[2,256,256]{2,1,0:T(8,128)(2,1)S(1)}, bf16[2,256,256]{2,1,0:T(8,128)(2,1)S(1)}, u32[]{:S(2)}, u32[]{:S(2)}) %collective-permute-start.5) | collective-permute-done | bytes 262176 | tf_op jit(solution)/shard_map/ppermute | solution.py:84
  24.6 1.4 %shard_map.61 = (bf16[2,256,512]{2,1,0:T(8,128)(2,1)}, bf16[2,256,256]{2,1,0:T(8,128)(2,1)S(1)}, bf16[2,256,256]{2,1,0:T(8,128)(2,1)S(1)}, bf16[2,256,256]{2,1,0:T(8,128)(2,1)S(1)}, bf16[2,256,256]{2,1,0:T(8,128)(2,1)S(1)}) custom-call(bf16[2,256,512]{2,1,0:T(8,128)(2,1)S(1)} %get-tuple-element.20.own, ...), custom_call_target="tpu_custom_call" | custom-call | flops 536870912 | bytes 4194304 | tf_op jit(solution)/shard_map/pallas_call | solution.py:38
  26.0 0.0 collective-permute-start.8
  26.0 1.4 %collective-permute-start.11 = (bf16[2,256,512]{2,1,0:T(8,128)(2,1)S(1)}, bf16[2,256,512]{2,1,0:T(8,128)(2,1)S(1)}, u32[]{:S(2)}, u32[]{:S(2)}) collective-permute-start(bf16[2,256,512]{2,1,0:T(8,128)(2,1)S(1)} %get-tuple-element.20.own), channel_id=1, source_target_pairs={{8,16},{9,17},{10,18},{11,19},{20,12},{21,13},{28,4},{29,5},{30,6}... | collective-permute-start | bytes 1572872 | tf_op jit(solution)/shard_map/ppermute | solution.py:84
  27.4 0.3 collective-permute-start.6
  27.8 0.7 collective-permute-start.14
  28.5 2.3 %collective-permute-start.9 = (bf16[2,256,256]{2,1,0:T(8,128)(2,1)S(1)}, bf16[2,256,256]{2,1,0:T(8,128)(2,1)S(1)}, u32[]{:S(2)}, u32[]{:S(2)}) collective-permute-start(bf16[2,256,256]{2,1,0:T(8,128)(2,1)S(1)} %get-tuple-element.26), channel_id=1, source_target_pairs={{0,5},{1,4},{2,7},{3,6},{4,1},{5,0},{6,3},{7,2},{8,13},{9,12},{10,... | collective-permute-start | bytes 786440 | tf_op jit(solution)/shard_map/ppermute | solution.py:133
  30.8 0.4 collective-permute-done.8
  31.2 5.4 %collective-permute-start.12 = (bf16[2,256,256]{2,1,0:T(8,128)(2,1)S(1)}, bf16[2,256,256]{2,1,0:T(8,128)(2,1)S(1)}, u32[]{:S(2)}, u32[]{:S(2)}) collective-permute-start(bf16[2,256,256]{2,1,0:T(8,128)(2,1)S(1)} %get-tuple-element.27.home0), channel_id=1, source_target_pairs={{0,24},{1,25},{2,26},{3,27},{4,28},{5,29},{6,30},{7,31},{12,20},{1... | collective-permute-start | bytes 786440 | tf_op jit(solution)/shard_map/ppermute | solution.py:84
  36.7 1.8 %collective-permute-start.13 = (bf16[2,256,256]{2,1,0:T(8,128)(2,1)S(1)}, bf16[2,256,256]{2,1,0:T(8,128)(2,1)S(1)}, u32[]{:S(2)}, u32[]{:S(2)}) collective-permute-start(bf16[2,256,256]{2,1,0:T(8,128)(2,1)S(1)} %get-tuple-element.28.home1), channel_id=1, source_target_pairs={{0,24},{1,25},{2,26},{3,27},{4,28},{5,29},{6,30},{7,31},{12,20},{1... | collective-permute-start | bytes 786440 | tf_op jit(solution)/shard_map/ppermute | solution.py:84
  38.6 0.0 collective-permute-done.9
  38.6 7.4 %collective-permute-start.7 = (bf16[2,512,256]{2,1,0:T(8,128)(2,1)S(1)}, bf16[2,512,256]{2,1,0:T(8,128)(2,1)S(1)}, u32[]{:S(2)}, u32[]{:S(2)}) collective-permute-start(bf16[2,512,256]{2,1,0:T(8,128)(2,1)S(1)} %constant_dynamic-update-slice_fusion.left0), channel_id=1, source_target_pairs={{0,2},{2,0},{4,6},{6,4},{1,3},{3,1},{5,7},{7,5},{8,10},{10,8},{12,... | collective-permute-start | bytes 1572872 | tf_op jit(solution)/shard_map/ppermute | solution.py:28
  46.0 0.0 collective-permute-done.11.far_early
  46.0 3.8 %collective-permute-start.10 = (bf16[2,512,256]{2,1,0:T(8,128)(2,1)S(1)}, bf16[2,512,256]{2,1,0:T(8,128)(2,1)S(1)}, u32[]{:S(2)}, u32[]{:S(2)}) collective-permute-start(bf16[2,512,256]{2,1,0:T(8,128)(2,1)S(1)} %constant_dynamic-update-slice_fusion.2.left2), channel_id=1, source_target_pairs={{0,2},{2,0},{4,6},{6,4},{1,3},{3,1},{5,7},{7,5},{8,10},{10,8},{12,... | collective-permute-start | bytes 1572872 | tf_op jit(solution)/shard_map/ppermute | solution.py:28
  49.8 0.0 collective-permute-done.14.refs_4_
  49.8 0.7 collective-permute-start.16
  50.5 7.7 %collective-permute-start.15 = (bf16[2,256,512]{2,1,0:T(8,128)(2,1)S(1)}, bf16[2,256,512]{2,1,0:T(8,128)(2,1)S(1)}, u32[]{:S(2)}, u32[]{:S(2)}) collective-permute-start(bf16[2,256,512]{2,1,0:T(8,128)(2,1)S(1)} %copy-done.4), channel_id=1, source_target_pairs={{2,10},{3,11},{4,12},{5,13},{6,14},{7,15},{12,4},{13,5},{14,6},{15... | collective-permute-start | bytes 1572872 | tf_op jit(solution)/shard_map/ppermute | solution.py:84
  58.2 0.7 collective-permute-start.17
  58.9 0.0 collective-permute-done.7.left1
  58.9 1.3 %collective-permute-start.20 = (bf16[2,256,256]{2,1,0:T(8,128)(2,1)S(1)}, bf16[2,256,256]{2,1,0:T(8,128)(2,1)S(1)}, u32[]{:S(2)}, u32[]{:S(2)}) collective-permute-start(bf16[2,256,256]{2,1,0:T(8,128)(2,1)S(1)} %collective-permute-done.12.far0), channel_id=1, source_target_pairs={{0,8},{1,9},{2,10},{3,11},{8,0},{9,1},{10,2},{11,3},{14,6},{15,7},... | collective-permute-start | bytes 786440 | tf_op jit(solution)/shard_map/ppermute | solution.py:84
  60.2 1.3 %collective-permute-start.18 = (bf16[2,256,256]{2,1,0:T(8,128)(2,1)S(1)}, bf16[2,256,256]{2,1,0:T(8,128)(2,1)S(1)}, u32[]{:S(2)}, u32[]{:S(2)}) collective-permute-start(bf16[2,256,256]{2,1,0:T(8,128)(2,1)S(1)} %collective-permute-done.13.far1), channel_id=1, source_target_pairs={{0,8},{1,9},{2,10},{3,11},{8,0},{9,1},{10,2},{11,3},{14,6},{15,7},... | collective-permute-start | bytes 786440 | tf_op jit(solution)/shard_map/ppermute | solution.py:84
  61.5 2.4 %shard_map.62 = (f32[2,512,512]{2,1,0:T(8,128)S(1)}, bf16[2,512,256]{2,1,0:T(8,128)(2,1)S(1)}, bf16[2,512,256]{2,1,0:T(8,128)(2,1)S(1)}) custom-call(s32[4]{0:T(128)S(1)} %copy-done.2, bf16[2,512,256]{2,1,0:T(8,128)(2,1)S(1)} %constant_dynamic-update-slice_fusion.left0, bf16[2,512,256]{2,1,0:T(8,128)(2,1)S(1)} %collective-permute-done.7.left1, ...), custom_call_target="tpu_custom_call" | custom-call | flops 1073741824 | bytes 6815760 | tf_op jit(solution)/shard_map/pallas_call | solution.py:38
  64.0 12.1 %collective-permute-done.15.refs_5_ = bf16[2,256,512]{2,1,0:T(8,128)(2,1)S(1)} collective-permute-done((bf16[2,256,512]{2,1,0:T(8,128)(2,1)S(1)}, bf16[2,256,512]{2,1,0:T(8,128)(2,1)S(1)}, u32[]{:S(2)}, u32[]{:S(2)}) %collective-permute-start.15) | collective-permute-done | bytes 524320 | tf_op jit(solution)/shard_map/ppermute | solution.py:84
  76.1 2.5 %collective-permute-done.20.refs_8_ = bf16[2,256,256]{2,1,0:T(8,128)(2,1)S(1)} collective-permute-done((bf16[2,256,256]{2,1,0:T(8,128)(2,1)S(1)}, bf16[2,256,256]{2,1,0:T(8,128)(2,1)S(1)}, u32[]{:S(2)}, u32[]{:S(2)}) %collective-permute-start.20) | collective-permute-done | bytes 262176 | tf_op jit(solution)/shard_map/ppermute | solution.py:84
  78.6 1.5 %shard_map.64 = (f32[2,256,256]{2,1,0:T(8,128)S(1)}, bf16[2,256,256]{2,1,0:T(8,128)(2,1)S(1)}) custom-call(s32[4]{0:T(128)S(1)} %copy-done.2, f32[2,512,512]{2,1,0:T(8,128)S(1)} %get-tuple-element.29.refs_1_, bf16[2,512,256]{2,1,0:T(8,128)(2,1)S(1)} %get-tuple-element.30.refs_2_, bf16[2,512,256]{2,1,0:T(8,128)(2,1)S(1)} %get-tuple-element.31.refs_3_, ...), custom_call_target="tpu_custom_call" | custom-call | flops 268435456 | bytes 6291472 | tf_op jit(solution)/shard_map/pallas_call | solution.py:38
  80.1 0.2 collective-permute-start.21
  80.3 1.4 %collective-permute-done.18.refs_8_ = bf16[2,256,256]{2,1,0:T(8,128)(2,1)S(1)} collective-permute-done((bf16[2,256,256]{2,1,0:T(8,128)(2,1)S(1)}, bf16[2,256,256]{2,1,0:T(8,128)(2,1)S(1)}, u32[]{:S(2)}, u32[]{:S(2)}) %collective-permute-start.18) | collective-permute-done | bytes 262176 | tf_op jit(solution)/shard_map/ppermute | solution.py:84
  81.7 1.5 %shard_map.63 = (f32[2,256,256]{2,1,0:T(8,128)S(1)}, bf16[2,256,256]{2,1,0:T(8,128)(2,1)S(1)}) custom-call(s32[4]{0:T(128)S(1)} %copy-done.2, f32[2,512,512]{2,1,0:T(8,128)S(1)} %get-tuple-element.29.refs_1_, bf16[2,512,256]{2,1,0:T(8,128)(2,1)S(1)} %get-tuple-element.30.refs_2_, bf16[2,512,256]{2,1,0:T(8,128)(2,1)S(1)} %get-tuple-element.31.refs_3_, ...), custom_call_target="tpu_custom_call" | custom-call | flops 268435456 | bytes 6291472 | tf_op jit(solution)/shard_map/pallas_call | solution.py:38
  83.2 0.1 collective-permute-start.19
  83.3 5.2 %collective-permute-done.21.refs_1_ = bf16[2,256,256]{2,1,0:T(8,128)(2,1)S(1)} collective-permute-done((bf16[2,256,256]{2,1,0:T(8,128)(2,1)S(1)}, bf16[2,256,256]{2,1,0:T(8,128)(2,1)S(1)}, u32[]{:S(2)}, u32[]{:S(2)}) %collective-permute-start.21) | collective-permute-done | bytes 262176 | tf_op jit(solution)/shard_map/ppermute | solution.py:28
  88.5 0.8 shard_map.65.refs_2_
  89.4 2.8 %collective-permute-done.19.refs_1_ = bf16[2,256,256]{2,1,0:T(8,128)(2,1)S(1)} collective-permute-done((bf16[2,256,256]{2,1,0:T(8,128)(2,1)S(1)}, bf16[2,256,256]{2,1,0:T(8,128)(2,1)S(1)}, u32[]{:S(2)}, u32[]{:S(2)}) %collective-permute-start.19) | collective-permute-done | bytes 262176 | tf_op jit(solution)/shard_map/ppermute | solution.py:28
  92.2 0.9 shard_map.66
  (18 shorter events, 0.1 us)
Async XLA Ops:
  0.6 1.0 %copy-start.1 = (bf16[1,1,2,256,512]{4,3,2,1,0:T(8,128)(2,1)S(1)}, bf16[1,1,2,256,512]{4,3,2,1,0:T(8,128)(2,1)}, u32[]{:S(2)}) copy-start(bf16[1,1,2,256,512]{4,3,2,1,0:T(8,128)(2,1)} %param.4) | copy-start | bytes 1572868
  1.7 0.7 copy-start.3
  3.1 2.7 %collective-permute-start.2 = (bf16[2,256,256]{2,1,0:T(8,128)(2,1)S(1)}, bf16[2,256,256]{2,1,0:T(8,128)(2,1)S(1)}, u32[]{:S(2)}, u32[]{:S(2)}) collective-permute-start(bf16[2,256,256]{2,1,0:T(8,128)(2,1)S(1)} %get-tuple-element.21), channel_id=1, source_target_pairs={{24,28},{25,29}} | collective-permute-start | bytes 786440 | tf_op jit(solution)/shard_map/ppermute | solution.py:84
  3.8 3.4 %collective-permute-start.4 = (bf16[2,256,256]{2,1,0:T(8,128)(2,1)S(1)}, bf16[2,256,256]{2,1,0:T(8,128)(2,1)S(1)}, u32[]{:S(2)}, u32[]{:S(2)}) collective-permute-start(bf16[2,256,256]{2,1,0:T(8,128)(2,1)S(1)} %get-tuple-element.22), channel_id=1, source_target_pairs={{24,29},{25,28}} | collective-permute-start | bytes 786440 | tf_op jit(solution)/shard_map/ppermute | solution.py:84
  4.5 5.3 %collective-permute-start = (bf16[2,256,256]{2,1,0:T(8,128)(2,1)S(1)}, bf16[2,256,256]{2,1,0:T(8,128)(2,1)S(1)}, u32[]{:S(2)}, u32[]{:S(2)}) collective-permute-start(bf16[2,256,256]{2,1,0:T(8,128)(2,1)S(1)} %get-tuple-element.21), channel_id=1, source_target_pairs={{8,2},{9,3},{16,4},{17,5},{18,12},{19,13},{26,14},{27,15},{28,22},... | collective-permute-start | bytes 786440 | tf_op jit(solution)/shard_map/ppermute | solution.py:84
  5.2 4.6 %collective-permute-start.1 = (bf16[2,256,256]{2,1,0:T(8,128)(2,1)S(1)}, bf16[2,256,256]{2,1,0:T(8,128)(2,1)S(1)}, u32[]{:S(2)}, u32[]{:S(2)}) collective-permute-start(bf16[2,256,256]{2,1,0:T(8,128)(2,1)S(1)} %get-tuple-element.22), channel_id=1, source_target_pairs={{8,3},{9,2},{16,5},{17,4},{18,13},{19,12},{26,15},{27,14},{28,23},... | collective-permute-start | bytes 786440 | tf_op jit(solution)/shard_map/ppermute | solution.py:84
  5.9 15.0 %collective-permute-start.3 = (bf16[2,256,256]{2,1,0:T(8,128)(2,1)S(1)}, bf16[2,256,256]{2,1,0:T(8,128)(2,1)S(1)}, u32[]{:S(2)}, u32[]{:S(2)}) collective-permute-start(bf16[2,256,256]{2,1,0:T(8,128)(2,1)S(1)} %collective-permute-done.2), channel_id=1, source_target_pairs={{28,6},{29,7}} | collective-permute-start | bytes 786440 | tf_op jit(solution)/shard_map/ppermute | solution.py:84
  7.2 17.5 %collective-permute-start.5 = (bf16[2,256,256]{2,1,0:T(8,128)(2,1)S(1)}, bf16[2,256,256]{2,1,0:T(8,128)(2,1)S(1)}, u32[]{:S(2)}, u32[]{:S(2)}) collective-permute-start(bf16[2,256,256]{2,1,0:T(8,128)(2,1)S(1)} %collective-permute-done.4), channel_id=1, source_target_pairs={{28,6},{29,7}} | collective-permute-start | bytes 786440 | tf_op jit(solution)/shard_map/ppermute | solution.py:84
  8.5 1.2 %copy-start = (bf16[2,512,512]{2,1,0:T(8,128)(2,1)S(1)}, bf16[2,512,512]{2,1,0:T(8,128)(2,1)}, u32[]{:S(2)}) copy-start(bf16[2,512,512]{2,1,0:T(8,128)(2,1)} %value.1) | copy-start | bytes 3145732
  9.8 51.8 %copy-start.2 = (s32[4]{0:T(128)S(1)}, s32[4]{0:T(128)}, u32[]{:S(2)}) copy-start(s32[4]{0:T(128)} %refs_0_.3) | copy-start | bytes 52
  26.0 24.5 %copy-start.4 = (bf16[2,256,512]{2,1,0:T(8,128)(2,1)S(1)}, bf16[2,256,512]{2,1,0:T(8,128)(2,1)}, u32[]{:S(2)}) copy-start(bf16[2,256,512]{2,1,0:T(8,128)(2,1)} %get-tuple-element.24) | copy-start | bytes 1572868
  26.0 5.2 %collective-permute-start.8 = (bf16[2,256,256]{2,1,0:T(8,128)(2,1)S(1)}, bf16[2,256,256]{2,1,0:T(8,128)(2,1)S(1)}, u32[]{:S(2)}, u32[]{:S(2)}) collective-permute-start(bf16[2,256,256]{2,1,0:T(8,128)(2,1)S(1)} %get-tuple-element.25), channel_id=1, source_target_pairs={{0,4},{2,6},{4,0},{6,2},{1,5},{3,7},{5,1},{7,3},{8,12},{10,14},{12... | collective-permute-start | bytes 786440 | tf_op jit(solution)/shard_map/ppermute | solution.py:28
  26.0 20.0 %collective-permute-start.11 = (bf16[2,256,512]{2,1,0:T(8,128)(2,1)S(1)}, bf16[2,256,512]{2,1,0:T(8,128)(2,1)S(1)}, u32[]{:S(2)}, u32[]{:S(2)}) collective-permute-start(bf16[2,256,512]{2,1,0:T(8,128)(2,1)S(1)} %get-tuple-element.20.own), channel_id=1, source_target_pairs={{8,16},{9,17},{10,18},{11,19},{20,12},{21,13},{28,4},{29,5},{30,6}... | collective-permute-start | bytes 1572872 | tf_op jit(solution)/shard_map/ppermute | solution.py:84
  27.4 9.2 %collective-permute-start.6 = (bf16[2,256,256]{2,1,0:T(8,128)(2,1)S(1)}, bf16[2,256,256]{2,1,0:T(8,128)(2,1)S(1)}, u32[]{:S(2)}, u32[]{:S(2)}) collective-permute-start(bf16[2,256,256]{2,1,0:T(8,128)(2,1)S(1)} %get-tuple-element.26), channel_id=1, source_target_pairs={{0,1},{1,0},{2,3},{3,2},{4,5},{5,4},{6,7},{7,6},{8,9},{9,8},{10,11... | collective-permute-start | bytes 786440 | tf_op jit(solution)/shard_map/ppermute | solution.py:28
  27.8 22.1 %collective-permute-start.14 = (bf16[2,256,512]{2,1,0:T(8,128)(2,1)S(1)}, bf16[2,256,512]{2,1,0:T(8,128)(2,1)S(1)}, u32[]{:S(2)}, u32[]{:S(2)}) collective-permute-start(bf16[2,256,512]{2,1,0:T(8,128)(2,1)S(1)} %get-tuple-element.20.own), channel_id=1, source_target_pairs={{0,8},{1,9},{8,0},{9,1},{10,2},{11,3},{16,24},{17,25},{18,26},{19,... | collective-permute-start | bytes 1572872 | tf_op jit(solution)/shard_map/ppermute | solution.py:84
  28.5 10.1 %collective-permute-start.9 = (bf16[2,256,256]{2,1,0:T(8,128)(2,1)S(1)}, bf16[2,256,256]{2,1,0:T(8,128)(2,1)S(1)}, u32[]{:S(2)}, u32[]{:S(2)}) collective-permute-start(bf16[2,256,256]{2,1,0:T(8,128)(2,1)S(1)} %get-tuple-element.26), channel_id=1, source_target_pairs={{0,5},{1,4},{2,7},{3,6},{4,1},{5,0},{6,3},{7,2},{8,13},{9,12},{10,... | collective-permute-start | bytes 786440 | tf_op jit(solution)/shard_map/ppermute | solution.py:133
  31.2 19.3 %collective-permute-start.12 = (bf16[2,256,256]{2,1,0:T(8,128)(2,1)S(1)}, bf16[2,256,256]{2,1,0:T(8,128)(2,1)S(1)}, u32[]{:S(2)}, u32[]{:S(2)}) collective-permute-start(bf16[2,256,256]{2,1,0:T(8,128)(2,1)S(1)} %get-tuple-element.27.home0), channel_id=1, source_target_pairs={{0,24},{1,25},{2,26},{3,27},{4,28},{5,29},{6,30},{7,31},{12,20},{1... | collective-permute-start | bytes 786440 | tf_op jit(solution)/shard_map/ppermute | solution.py:84
  36.7 21.5 %collective-permute-start.13 = (bf16[2,256,256]{2,1,0:T(8,128)(2,1)S(1)}, bf16[2,256,256]{2,1,0:T(8,128)(2,1)S(1)}, u32[]{:S(2)}, u32[]{:S(2)}) collective-permute-start(bf16[2,256,256]{2,1,0:T(8,128)(2,1)S(1)} %get-tuple-element.28.home1), channel_id=1, source_target_pairs={{0,24},{1,25},{2,26},{3,27},{4,28},{5,29},{6,30},{7,31},{12,20},{1... | collective-permute-start | bytes 786440 | tf_op jit(solution)/shard_map/ppermute | solution.py:84
  38.6 20.3 %collective-permute-start.7 = (bf16[2,512,256]{2,1,0:T(8,128)(2,1)S(1)}, bf16[2,512,256]{2,1,0:T(8,128)(2,1)S(1)}, u32[]{:S(2)}, u32[]{:S(2)}) collective-permute-start(bf16[2,512,256]{2,1,0:T(8,128)(2,1)S(1)} %constant_dynamic-update-slice_fusion.left0), channel_id=1, source_target_pairs={{0,2},{2,0},{4,6},{6,4},{1,3},{3,1},{5,7},{7,5},{8,10},{10,8},{12,... | collective-permute-start | bytes 1572872 | tf_op jit(solution)/shard_map/ppermute | solution.py:28
  46.0 14.2 %collective-permute-start.10 = (bf16[2,512,256]{2,1,0:T(8,128)(2,1)S(1)}, bf16[2,512,256]{2,1,0:T(8,128)(2,1)S(1)}, u32[]{:S(2)}, u32[]{:S(2)}) collective-permute-start(bf16[2,512,256]{2,1,0:T(8,128)(2,1)S(1)} %constant_dynamic-update-slice_fusion.2.left2), channel_id=1, source_target_pairs={{0,2},{2,0},{4,6},{6,4},{1,3},{3,1},{5,7},{7,5},{8,10},{10,8},{12,... | collective-permute-start | bytes 1572872 | tf_op jit(solution)/shard_map/ppermute | solution.py:28
  49.8 14.1 %collective-permute-start.16 = (bf16[2,256,512]{2,1,0:T(8,128)(2,1)S(1)}, bf16[2,256,512]{2,1,0:T(8,128)(2,1)S(1)}, u32[]{:S(2)}, u32[]{:S(2)}) collective-permute-start(bf16[2,256,512]{2,1,0:T(8,128)(2,1)S(1)} %get-tuple-element.20.own), channel_id=1, source_target_pairs={{8,24},{9,25},{10,26},{11,27},{20,4},{21,5}} | collective-permute-start | bytes 1572872 | tf_op jit(solution)/shard_map/ppermute | solution.py:84
  50.5 25.5 %collective-permute-start.15 = (bf16[2,256,512]{2,1,0:T(8,128)(2,1)S(1)}, bf16[2,256,512]{2,1,0:T(8,128)(2,1)S(1)}, u32[]{:S(2)}, u32[]{:S(2)}) collective-permute-start(bf16[2,256,512]{2,1,0:T(8,128)(2,1)S(1)} %copy-done.4), channel_id=1, source_target_pairs={{2,10},{3,11},{4,12},{5,13},{6,14},{7,15},{12,4},{13,5},{14,6},{15... | collective-permute-start | bytes 1572872 | tf_op jit(solution)/shard_map/ppermute | solution.py:84
  58.2 17.9 %collective-permute-start.17 = (bf16[2,256,512]{2,1,0:T(8,128)(2,1)S(1)}, bf16[2,256,512]{2,1,0:T(8,128)(2,1)S(1)}, u32[]{:S(2)}, u32[]{:S(2)}) collective-permute-start(bf16[2,256,512]{2,1,0:T(8,128)(2,1)S(1)} %collective-permute-done.14.refs_4_), channel_id=1, source_target_pairs={{20,12},{21,13},{22,14},{23,15}} | collective-permute-start | bytes 1572872 | tf_op jit(solution)/shard_map/ppermute | solution.py:84
  58.9 19.7 %collective-permute-start.20 = (bf16[2,256,256]{2,1,0:T(8,128)(2,1)S(1)}, bf16[2,256,256]{2,1,0:T(8,128)(2,1)S(1)}, u32[]{:S(2)}, u32[]{:S(2)}) collective-permute-start(bf16[2,256,256]{2,1,0:T(8,128)(2,1)S(1)} %collective-permute-done.12.far0), channel_id=1, source_target_pairs={{0,8},{1,9},{2,10},{3,11},{8,0},{9,1},{10,2},{11,3},{14,6},{15,7},... | collective-permute-start | bytes 786440 | tf_op jit(solution)/shard_map/ppermute | solution.py:84
  60.2 21.5 %collective-permute-start.18 = (bf16[2,256,256]{2,1,0:T(8,128)(2,1)S(1)}, bf16[2,256,256]{2,1,0:T(8,128)(2,1)S(1)}, u32[]{:S(2)}, u32[]{:S(2)}) collective-permute-start(bf16[2,256,256]{2,1,0:T(8,128)(2,1)S(1)} %collective-permute-done.13.far1), channel_id=1, source_target_pairs={{0,8},{1,9},{2,10},{3,11},{8,0},{9,1},{10,2},{11,3},{14,6},{15,7},... | collective-permute-start | bytes 786440 | tf_op jit(solution)/shard_map/ppermute | solution.py:84
  80.1 8.4 %collective-permute-start.21 = (bf16[2,256,256]{2,1,0:T(8,128)(2,1)S(1)}, bf16[2,256,256]{2,1,0:T(8,128)(2,1)S(1)}, u32[]{:S(2)}, u32[]{:S(2)}) collective-permute-start(bf16[2,256,256]{2,1,0:T(8,128)(2,1)S(1)} %get-tuple-element.35), channel_id=1, source_target_pairs={{0,1},{1,0},{2,3},{3,2},{4,5},{5,4},{6,7},{7,6},{8,9},{9,8},{10,11... | collective-permute-start | bytes 786440 | tf_op jit(solution)/shard_map/ppermute | solution.py:28
  83.2 9.0 %collective-permute-start.19 = (bf16[2,256,256]{2,1,0:T(8,128)(2,1)S(1)}, bf16[2,256,256]{2,1,0:T(8,128)(2,1)S(1)}, u32[]{:S(2)}, u32[]{:S(2)}) collective-permute-start(bf16[2,256,256]{2,1,0:T(8,128)(2,1)S(1)} %get-tuple-element.33), channel_id=1, source_target_pairs={{0,1},{1,0},{2,3},{3,2},{4,5},{5,4},{6,7},{7,6},{8,9},{9,8},{10,11... | collective-permute-start | bytes 786440 | tf_op jit(solution)/shard_map/ppermute | solution.py:28
